TPU v7x, 32 devices: a whole 2x2x4 slice. The times are simulated.
32 devices in a mesh: groups: 2 (over y), space: 4 (over z), clus: 4 (over x, core).
Axes of the slice: x: 2, y: 2, z: 4, core: 2. Of those that a mesh axis runs over, the one named last changes fastest.
Arguments:
- snapshots: bfloat16 [256, 5, 49152], P('groups', None, ('space', 'clus')), parts along dimension 0
- labels: int32 [256], P('groups'), parts along dimension 0, may hold values from 0 to 3, as said below
- start: float32 [256, 16], P('groups'), parts along dimension 0, may hold values from -6 to 6
- successor: int32 [8], P('groups'), parts along dimension 0, may hold values from 0 to 3, as said below
Outputs:
- modes: bfloat16 [8, 16, 5, 49152], P(('groups', 'clus'), None, None, 'space'), parts along dimension 0
- coefficients: float32 [256, 16], P(('groups', 'clus')), parts along dimension 0
- correlations: float32 [8, 16, 16], P(('groups', 'clus')), parts along dimension 0
There are 2 independent parts, one for each index of `groups`. A program takes and returns all parts, laid end to end along the dimension named above; each array names one. Nothing has to cross between parts.
Inputs may be any that keep to these rules, and one draw needn't show every extreme that they name: `labels`: of the 32 snapshots of each aligned block (those of one index of clus), every cluster holds at least 6 and at most 8; in every block some cluster holds exactly 8. Following successor from any cluster visits all 4 clusters once before returning.
All inputs are finite; a program needn't handle non-finite values.
Results may differ from a plain program's by a relative error of at most 0.0045.
Values may be sent and summed in bfloat16 or wider, within the bound.
No kernel may reach another device: no remote copies, remote signals or barrier semaphores. Data moves between devices by JAX's collectives and lax.ppermute only.
A program may use at most 64 MiB of HBM per device.

v0:
```python
import jax
import jax.numpy as jnp
from jax import lax
from jax.sharding import PartitionSpec as P

ITERS = 2


def subspace(gram, member, start):
    basis = member[:, :, None] * start[None, :, :]
    for step in range(ITERS):
        image = (
            member[:, :, None]
            * jnp.einsum("st,ktm->ksm", gram, basis, precision=lax.Precision.HIGHEST)
            + basis
        )
        inner = jnp.einsum("ksm,ksn->kmn", image, image, precision=lax.Precision.HIGHEST)
        lower = jnp.linalg.cholesky(inner)
        basis = lax.linalg.triangular_solve(
            lower, image, left_side=False, lower=True, transpose_a=True
        )
    return basis


def local(snapshots, labels, start, successor):
    count, variables, cells = snapshots.shape
    clusters = lax.axis_size("clus")
    owner = lax.axis_index("clus")
    total_rows = variables * cells * lax.axis_size("space") * clusters
    flat = snapshots.reshape(count, variables * cells)
    partial_value = lax.dot_general(
        flat, flat, (((1,), (1,)), ((), ())), preferred_element_type=jnp.float32
    )
    gram = lax.psum(partial_value, ("space", "clus")) / total_rows
    cluster_ids = jnp.arange(clusters, dtype=jnp.int32)
    member = (labels[None, :] == cluster_ids[:, None]).astype(jnp.float32)
    basis = subspace(gram, member, start)
    picked = jnp.einsum("ks,ksm->sm", member, basis, precision=lax.Precision.HIGHEST)
    snap_dev = count // clusters
    coefficients = lax.dynamic_slice_in_dim(picked, owner * snap_dev, snap_dev, 0)
    rounded = basis.astype(jnp.bfloat16)
    mode_count = rounded.shape[2]
    modes_full = None
    left = jnp.transpose(rounded, (0, 2, 1)).reshape(clusters * mode_count, count)
    modes_full = jnp.dot(left, flat, preferred_element_type=jnp.float32)
    packed = modes_full.astype(jnp.bfloat16).reshape(clusters, mode_count, variables, cells)
    modes_out = lax.all_to_all(packed, "clus", split_axis=0, concat_axis=3, tiled=True)
    select = (successor[:, None] == cluster_ids[None, :]).astype(jnp.float32)
    wide = rounded.astype(jnp.float32)
    partner = jnp.einsum("ab,bsn->asn", select, wide, precision=lax.Precision.HIGHEST)
    image = jnp.einsum("st,atn->asn", gram, partner, precision=lax.Precision.HIGHEST)
    correlations = jnp.einsum("asm,asn->amn", wide, image, precision=lax.Precision.HIGHEST)
    own_correlation = lax.dynamic_slice_in_dim(correlations, owner, 1, 0)
    return (modes_out, coefficients, own_correlation)


def solution(mesh):
    in_specs = (P("groups", None, ("space", "clus")), P("groups"), P("groups", None), P("groups"))
    out_specs = (
        P(("groups", "clus"), None, None, "space"),
        P(("groups", "clus"), None),
        P(("groups", "clus"), None, None),
    )
    return jax.shard_map(local, mesh=mesh, in_specs=in_specs, out_specs=out_specs, check_vma=False)
```

profile of v0, /device:TPU:1, one launch (start us, length us, event | category | flops | bytes accessed | tf_op | source)
XLA Modules:
  0.0 172.4 jit_solution(173776694287602055)
XLA Ops:
  7.2 0.0 copy-start.2
  7.2 0.0 all-reduce.2.cloned.1.call-start
  7.2 5.1 %convolution_bitcast_fusion = f32[128,128]{1,0:T(8,128)} fusion(bf16[128,5,3072]{2,0,1:T(8,128)(2,1)} %param.7), kind=kOutput, calls=%fused_computation.1 | convolution fusion | flops 503316480 | bytes 3997696 | tf_op jit(solution)/shard_map/dot_general | solution.py:31
  12.3 0.0 all-reduce.2.cloned.1.call-update
  12.4 0.0 copy-done.2
  12.4 0.0 copy-start.1
  12.4 6.3 %copy.38 = bf16[128,5,3072]{0,2,1:T(8,128)(2,1)} copy(bf16[128,5,3072]{2,0,1:T(8,128)(2,1)} %param.7) | data formatting | bytes 7864320 | tf_op args[0]
  18.7 80.9 %all-reduce.2.cloned.1.call-done = f32[128,128]{1,0:T(8,128)} async-done(((f32[128,128]{1,0:T(8,128)}), f32[128,128]{1,0:T(8,128)}) %all-reduce.2.cloned.1.call-update) | async-done | bytes 65552 | tf_op jit(solution)/shard_map/psum | solution.py:34
  99.6 0.0 copy-done.1
  99.6 1.1 fusion.3
  100.7 0.2 fusion.35
  100.8 0.1 copy.34
  100.9 5.9 %custom-call.8 = f32[4,16,16]{2,1,0:T(8,128)S(1)} custom-call(f32[4,16,16]{2,1,0:T(8,128)S(1)} %fusion.16), custom_call_target="Cholesky" | custom-call | tf_op jit(solution)/shard_map/jit(cholesky)/cholesky | solution.py:18
  106.8 0.1 compare_reduce_fusion.1
  106.9 0.1 select_bitcast_fusion.1
  107.0 4.9 %custom-call.9 = f32[4,1,16,16]{2,3,1,0:T(8,128)S(1)} custom-call(f32[4,1,16,16]{3,2,1,0:T(8,128)S(1)} %select_bitcast_fusion.1), custom_call_target="InvertDiagBlocksLowerTriangular" | custom-call | tf_op jit(solution)/shard_map/triangular_solve/custom-call.0 | solution.py:19
  111.9 0.3 convolution_bitcast_fusion.1
  112.2 1.1 fusion.1
  113.3 0.2 fusion.36
  113.5 0.1 copy.36
  113.6 5.9 %custom-call.10 = f32[4,16,16]{2,1,0:T(8,128)S(1)} custom-call(f32[4,16,16]{2,1,0:T(8,128)S(1)} %fusion.14), custom_call_target="Cholesky" | custom-call | tf_op jit(solution)/shard_map/jit(cholesky)/cholesky | solution.py:18
  119.5 0.1 compare_reduce_fusion
  119.6 0.1 select_bitcast_fusion
  119.7 4.9 %custom-call.11 = f32[4,1,16,16]{2,3,1,0:T(8,128)S(1)} custom-call(f32[4,1,16,16]{3,2,1,0:T(8,128)S(1)} %select_bitcast_fusion), custom_call_target="InvertDiagBlocksLowerTriangular" | custom-call | tf_op jit(solution)/shard_map/triangular_solve/custom-call.0 | solution.py:19
  124.6 0.3 bitcast_convert_fusion
  124.9 4.9 %convolution_convert_fusion = bf16[64,15360]{1,0:T(8,128)(2,1)} fusion(bf16[64,128]{1,0:T(8,128)(2,1)S(1)} %bitcast.78, bf16[128,15360]{0,1:T(8,128)(2,1)} %bitcast.75), kind=kOutput, calls=%fused_computation | convolution fusion | flops 252641280 | bytes 5914624 | tf_op jit(solution)/shard_map/dot_general | solution.py:45
  129.8 4.6 %reshape.50 = bf16[4,16,5,3072]{3,2,1,0:T(8,128)(2,1)S(1)} reshape(bf16[64,15360]{1,0:T(8,128)(2,1)} %convolution_convert_fusion) | data formatting | bytes 3932160 | tf_op jit(solution)/shard_map/reshape | solution.py:46
  134.3 0.0 copy-start.3
  134.3 0.0 copy-start
  134.3 2.6 %copy.39 = bf16[4,16,5,3072]{3,1,2,0:T(8,128)(2,1)} copy(bf16[4,16,5,3072]{3,2,1,0:T(8,128)(2,1)S(1)} %reshape.50) | data formatting | bytes 3932160 | tf_op jit(solution)/shard_map/reshape | solution.py:46
  136.9 3.8 %all-to-all-start = ((bf16[4,16,5,3072]{3,1,2,0:T(8,128)(2,1)}), bf16[4,16,5,3072]{3,1,2,0:T(8,128)(2,1)S(1)}, u32[]{:S(2)}, u32[]{:S(2)}) async-start(bf16[4,16,5,3072]{3,1,2,0:T(8,128)(2,1)} %copy.39), calls=%async_computation | async-start | bytes 3932160 | tf_op jit(solution)/shard_map/all_to_all | solution.py:47
  140.7 0.7 constant_dynamic-slice_fusion.1
  141.4 0.0 copy-done.3
  141.4 0.2 fusion.22
  141.6 0.0 copy-done
  141.6 0.2 fusion.4
  141.8 0.1 fusion.37
  142.0 0.6 constant_dynamic-slice_fusion
  142.6 21.5 %all-to-all-done = bf16[4,16,5,3072]{3,1,2,0:T(8,128)(2,1)S(1)} async-done(((bf16[4,16,5,3072]{3,1,2,0:T(8,128)(2,1)}), bf16[4,16,5,3072]{3,1,2,0:T(8,128)(2,1)S(1)}, u32[]{:S(2)}, u32[]{:S(2)}) %all-to-all-start) | async-done | bytes 1966112 | tf_op jit(solution)/shard_map/all_to_all | solution.py:47
  164.1 1.4 copy.52
  (8 shorter events, 0.1 us)
Async XLA Ops:
  7.2 5.2 %copy-start.2 = (s32[128]{0:T(128)S(1)}, s32[128]{0:T(128)}, u32[]{:S(2)}) copy-start(s32[128]{0:T(128)} %param.8) | copy-start | bytes 1540
  7.2 92.4 %all-reduce.2.cloned.1.call-start = ((), (), s32[]{:S(2)}) async-start(), calls=%async_computation.1 | async-start | bytes 131072 | tf_op jit(solution)/shard_map/psum | solution.py:34
  12.4 87.1 %copy-start.1 = (f32[128,16]{0,1:T(8,128)S(1)}, f32[128,16]{0,1:T(8,128)}, u32[]{:S(2)}) copy-start(f32[128,16]{0,1:T(8,128)} %param.9) | copy-start | bytes 24580
  134.3 7.0 %copy-start.3 = (s32[4]{0:T(128)S(1)}, s32[4]{0:T(128)}, u32[]{:S(2)}) copy-start(s32[4]{0:T(128)} %param.10) | copy-start | bytes 52
  134.3 7.2 %copy-start = (f32[128,128]{1,0:T(8,128)S(1)}, f32[128,128]{1,0:T(8,128)}, u32[]{:S(2)}) copy-start(f32[128,128]{1,0:T(8,128)} %all-reduce.2.cloned.1.call-done) | copy-start | bytes 196612
  136.9 27.2 %all-to-all-start = ((bf16[4,16,5,3072]{3,1,2,0:T(8,128)(2,1)}), bf16[4,16,5,3072]{3,1,2,0:T(8,128)(2,1)S(1)}, u32[]{:S(2)}, u32[]{:S(2)}) async-start(bf16[4,16,5,3072]{3,1,2,0:T(8,128)(2,1)} %copy.39), calls=%async_computation | async-start | bytes 3932160 | tf_op jit(solution)/shard_map/all_to_all | solution.py:47
Sparse Core Ops, SparseCore 0:
  12.5 87.0 all-reduce.1
where the time goes:
time: 175 us; the launch traced here: 172 us
  waiting for transfers between devices  102 us (58%)
  other arithmetic  22.1 us (13%)
  local copies, waits for them, and re-layouts  16.3 us (9%)
  between operations  14.2 us (8%)
  matrix products  13.6 us (8%)
  starting transfers between devices  3.8 us (2%)
    psum x1, waiting for transfers between devices, local(): gram = lax.psum(partial_value, ('space', 'clus')) / total_rows  80.9 us
    all_to_all x1, waiting for transfers between devices, local(): lax.all_to_all(packed, 'clus', split_axis=0, concat_axis=3, tiled=True)  21.5 us
    another operation x7, other arithmetic, subspace(): lower = jnp.linalg.cholesky(inner)  12 us
    another operation x5, other arithmetic, subspace(): lax.linalg.triangular_solve(lower, image, left_side=False, lower=True, tr...  9.99 us
    reshape x2, local copies, waits for them, and re-layouts, local(): modes_full.astype(jnp.bfloat16)  7.12 us
    unnamed x9, local copies, waits for them, and re-layouts  6.29 us
    dot_general x1, matrix products, local(): lax.dot_general(flat, flat, (((1,), (1,)), ((), ())), preferred_element_t...  5.13 us
    dot_general x1, matrix products, local(): modes_full = jnp.dot(left, flat, preferred_element_type=jnp.float32)  4.86 us
  transfers between devices with their start and end apart: 2, of which 2 were waited for; matrix products, arithmetic and copies ran while one was open for 5% of the time, Pallas kernels for 0%

commit v1 on v0

v1 whole, which is shorter than its diff:
```python
import functools

import jax
import jax.numpy as jnp
from jax import lax
from jax.experimental import pallas as pl
from jax.experimental.pallas import tpu as pltpu
from jax.sharding import PartitionSpec as P

ITERS = 2
HIGH = lax.Precision.HIGHEST
VMEM_LIMIT = 48 * 1024 * 1024


def gram_body(x_ref, gram_ref):
    @pl.when(pl.program_id(0) == 0)
    def _():
        gram_ref[...] = jnp.zeros_like(gram_ref)

    x = x_ref[0]
    gram_ref[...] += lax.dot_general(
        x, x, (((1,), (1,)), ((), ())), preferred_element_type=jnp.float32
    )


def partial_gram(x):
    variables, count, cells = x.shape
    return pl.pallas_call(
        gram_body,
        grid=(variables,),
        in_specs=[pl.BlockSpec((1, count, cells), lambda v: (v, 0, 0))],
        out_specs=pl.BlockSpec((count, count), lambda v: (0, 0)),
        out_shape=jax.ShapeDtypeStruct((count, count), jnp.float32),
        cost_estimate=pl.CostEstimate(
            flops=2 * variables * count * count * cells,
            bytes_accessed=2 * variables * count * cells,
            transcendentals=0,
        ),
        name="gram",
    )(x)


def orthonormal(image, same):
    modes = image.shape[0]
    products = jnp.concatenate([image * image[c : c + 1, :] for c in range(modes)], axis=0)
    inner = jnp.dot(products, same, precision=HIGH, preferred_element_type=jnp.float32)
    columns = [inner[c * modes : (c + 1) * modes] for c in range(modes)]
    row = lax.broadcasted_iota(jnp.int32, image.shape, 0)
    scale = jnp.zeros_like(image)
    for j in range(modes):
        pivot = columns[j][j : j + 1, :]
        scale = jnp.where(row == j, lax.rsqrt(pivot), scale)
        if j + 1 < modes:
            factor = jnp.where(row > j, columns[j] * (1.0 / pivot), 0.0)
            for c in range(j + 1, modes):
                columns[c] = columns[c] - factor * columns[c][j : j + 1, :]
            image = image - factor * image[j : j + 1, :]
    return image * scale


def subspace_body(me_ref, gram_ref, row_ref, column_ref, start_ref, basis_ref, left_ref, *, total_rows, clusters):
    row_labels = row_ref[...]
    same = (column_ref[...] == row_labels).astype(jnp.float32)
    gram = gram_ref[...] * same * (1.0 / total_rows)
    rows = lax.broadcasted_iota(jnp.int32, gram.shape, 0)
    lanes = lax.broadcasted_iota(jnp.int32, gram.shape, 1)
    shifted = gram + (rows == lanes).astype(jnp.float32)
    basis = start_ref[...]
    for step in range(ITERS):
        image = jnp.dot(basis, shifted, precision=HIGH, preferred_element_type=jnp.float32)
        basis = orthonormal(image, same)
    basis_ref[...] = basis
    rounded = basis.astype(jnp.bfloat16).astype(jnp.float32)
    for k in range(clusters):
        left_ref[k] = jnp.where(row_labels == (me_ref[0] ^ k), rounded, 0.0).astype(jnp.bfloat16)


def subspace(me, gram, labels, start, total_rows, clusters):
    modes, count = start.shape
    vmem = pl.BlockSpec(memory_space=pltpu.VMEM)
    return pl.pallas_call(
        functools.partial(subspace_body, total_rows=total_rows, clusters=clusters),
        in_specs=[pl.BlockSpec(memory_space=pltpu.SMEM), vmem, vmem, vmem, vmem],
        out_specs=(vmem, vmem),
        out_shape=(
            jax.ShapeDtypeStruct((modes, count), jnp.float32),
            jax.ShapeDtypeStruct((clusters, modes, count), jnp.bfloat16),
        ),
        name="subspace",
    )(me, gram, labels[None, :], labels[:, None], start)


def small_body(me_ref, successor_ref, gram_ref, row_ref, basis_ref, coefficients_ref, correlations_ref, *, total_rows):
    me = me_ref[0]
    row_labels = row_ref[...]
    basis = basis_ref[...]
    rounded = basis.astype(jnp.bfloat16).astype(jnp.float32)
    mine = jnp.where(row_labels == me, rounded, 0.0)
    other = jnp.where(row_labels == successor_ref[me], rounded, 0.0)
    image = jnp.dot(mine, gram_ref[...], precision=HIGH, preferred_element_type=jnp.float32)
    correlations_ref[0] = lax.dot_general(
        image, other, (((1,), (1,)), ((), ())), precision=HIGH, preferred_element_type=jnp.float32
    ) * (1.0 / total_rows)
    count = basis.shape[1]
    own = coefficients_ref.shape[1]
    coefficients_ref[...] = pltpu.roll(basis, (count - me * own) % count, 1)[:, :own]


def small_outputs(me, successor, gram, labels, basis, total_rows, clusters):
    modes, count = basis.shape
    vmem = pl.BlockSpec(memory_space=pltpu.VMEM)
    smem = pl.BlockSpec(memory_space=pltpu.SMEM)
    return pl.pallas_call(
        functools.partial(small_body, total_rows=total_rows),
        in_specs=[smem, smem, vmem, vmem, vmem],
        out_specs=(vmem, vmem),
        out_shape=(
            jax.ShapeDtypeStruct((modes, count // clusters), jnp.float32),
            jax.ShapeDtypeStruct((1, modes, modes), jnp.float32),
        ),
        name="small",
    )(me, successor, gram, labels[None, :], basis)


def modes_body(left_ref, x_ref, *out_refs, order):
    x = x_ref[0]
    for k, out_ref in zip(order, out_refs):
        out_ref[0] = jnp.dot(left_ref[k], x, preferred_element_type=jnp.float32).astype(jnp.bfloat16)


def local_modes(left, x, order):
    variables, count, cells = x.shape
    clusters, modes, _ = left.shape
    out = jax.ShapeDtypeStruct((variables, modes, cells), jnp.bfloat16)
    return pl.pallas_call(
        functools.partial(modes_body, order=order),
        grid=(variables,),
        in_specs=[
            pl.BlockSpec((clusters, modes, count), lambda v: (0, 0, 0)),
            pl.BlockSpec((1, count, cells), lambda v: (v, 0, 0)),
        ],
        out_specs=[pl.BlockSpec((1, modes, cells), lambda v: (v, 0, 0)) for _ in order],
        out_shape=[out for _ in order],
        cost_estimate=pl.CostEstimate(
            flops=2 * variables * count * cells * modes * len(order),
            bytes_accessed=2 * variables * cells * (count + modes * len(order)),
            transcendentals=0,
        ),
        name="modes",
    )(left, x)


def place_body(me_ref, *refs, order, aliased):
    pieces = refs[aliased : aliased + len(order)]
    out_ref = refs[aliased + len(order)]
    sems = refs[aliased + len(order) + 1]
    cells = pieces[0].shape[2]
    copies = []
    for i, k in enumerate(order):
        at = pl.multiple_of((me_ref[0] ^ k) * cells, 128)
        copy = pltpu.make_async_copy(pieces[i], out_ref.at[:, :, pl.ds(at, cells)], sems.at[i])
        copy.start()
        copies.append(copy)
    for copy in copies:
        copy.wait()


def place(me, out, pieces, order, clusters):
    variables, modes, cells = pieces[0].shape
    anywhere = pl.BlockSpec(memory_space=pl.ANY)
    aliased = 0 if out is None else 1
    operands = ([] if out is None else [out]) + list(pieces)
    return pl.pallas_call(
        functools.partial(place_body, order=order, aliased=aliased),
        in_specs=[pl.BlockSpec(memory_space=pltpu.SMEM)] + [anywhere] * len(operands),
        out_specs=anywhere,
        out_shape=jax.ShapeDtypeStruct((variables, modes, clusters * cells), jnp.bfloat16),
        scratch_shapes=[pltpu.SemaphoreType.DMA((len(order),))],
        input_output_aliases={1: 0} if aliased else {},
        name="place",
    )(me, *operands)


def swap(x, axis, offset):
    size = lax.axis_size(axis)
    return lax.ppermute(x, axis, [(i, i ^ offset) for i in range(size)])


def powers(size):
    return [1 << b for b in range(size.bit_length() - 1)]


def local(snapshots, labels, start, successor):
    count, variables, cells = snapshots.shape
    clusters = lax.axis_size("clus")
    space = lax.axis_size("space")
    me = lax.axis_index("clus").astype(jnp.int32).reshape(1)
    total_rows = variables * cells * space * clusters
    x = jnp.transpose(snapshots, (1, 0, 2))
    gram = partial_gram(x)
    for axis, size in (("clus", clusters), ("space", space)):
        for offset in powers(size):
            gram = gram + swap(gram, axis, offset)
    basis, left = subspace(me, gram, labels, start.T, total_rows, clusters)
    far = list(range(2, clusters))
    sent = local_modes(left, x, far)
    got = [swap(piece, "clus", k) for piece, k in zip(sent, far)]
    own, sibling = local_modes(left, x, [0, 1])
    sibling = swap(sibling, "clus", 1)
    coefficients, correlations = small_outputs(me, successor, gram, labels, basis, total_rows, clusters)
    out = place(me, None, [own, sibling], [0, 1], clusters)
    for piece, k in zip(got, far):
        out = place(me, out, [piece], [k], clusters)
    modes_out = jnp.transpose(out, (1, 0, 2))[None]
    return modes_out, coefficients.T, correlations


def solution(mesh):
    in_specs = (P("groups", None, ("space", "clus")), P("groups"), P("groups", None), P("groups"))
    out_specs = (
        P(("groups", "clus"), None, None, "space"),
        P(("groups", "clus"), None),
        P(("groups", "clus"), None, None),
    )
    return jax.shard_map(local, mesh=mesh, in_specs=in_specs, out_specs=out_specs, check_vma=False)
```

time: 175 us -> 107 us (0.61)
  waiting for transfers between devices: 102 us -> 6.92 us
  Pallas kernels: 0 us -> 83.1 us
  other arithmetic: 22.1 us -> 1.5 us
  matrix products: 13.6 us -> 0 us
  between operations: 14.2 us -> 0.71 us
  local copies, waits for them, and re-layouts: 16.3 us -> 3.08 us
  starting transfers between devices: 3.8 us -> 10.5 us
    pallas_call x0 -> x8, Pallas kernels: none -> 83.1 us  [the longest x3 62.9 us: place(): pl.pallas_call(functools.partial(place_body, order=order, aliased=aliased...]
    psum x1 -> x0, waiting for transfers between devices: 80.9 us -> none  [local(): gram = lax.psum(partial_value, ('space', 'clus')) / total_rows]
    another operation x12 -> x0, other arithmetic: 22 us -> none  [the longest x7 12 us: subspace(): lower = jnp.linalg.cholesky(inner)]
    all_to_all x1 -> x0, waiting for transfers between devices: 21.5 us -> none  [local(): lax.all_to_all(packed, 'clus', split_axis=0, concat_axis=3, tiled=True)]
    dot_general x9 -> x0, matrix products: 13 us -> none  [the longest x1 5.13 us: local(): lax.dot_general(flat, flat, (((1,), (1,)), ((), ())), preferred_element_t...]
    ppermute x0 -> x7, starting transfers between devices: none -> 10.5 us  [swap(): return lax.ppermute(x, axis, [(i, i ^ offset) for i in range(size)])]
    reshape x2 -> x0, local copies, waits for them, and re-layouts: 7.12 us -> none  [local(): modes_full.astype(jnp.bfloat16)]
    ppermute x0 -> x7, waiting for transfers between devices: none -> 6.92 us  [swap(): return lax.ppermute(x, axis, [(i, i ^ offset) for i in range(size)])]
  transfers between devices with their start and end apart: 2 -> 7, of which waited for: 2 -> 4; matrix products, arithmetic and copies ran while one was open for 5% -> 1% of each run, Pallas kernels for 0% -> 51%
where the time goes in v1:
time: 107 us; the launch traced here: 106 us
  Pallas kernels  83.1 us (78%)
  starting transfers between devices  10.5 us (10%)
  waiting for transfers between devices  6.92 us (6%)
  local copies, waits for them, and re-layouts  3.08 us (3%)
  other arithmetic  1.5 us (1%)
    pallas_call x3, Pallas kernels, place(): pl.pallas_call(functools.partial(place_body, order=order, aliased=aliased...  62.9 us
    ppermute x7, starting transfers between devices, swap(): return lax.ppermute(x, axis, [(i, i ^ offset) for i in range(size)])  10.5 us
    pallas_call x2, Pallas kernels, local_modes(): pl.pallas_call(functools.partial(modes_body, order=order), grid=(variable...  10.3 us
    ppermute x7, waiting for transfers between devices, swap(): return lax.ppermute(x, axis, [(i, i ^ offset) for i in range(size)])  6.92 us
    pallas_call x1, Pallas kernels, partial_gram(): pl.pallas_call(gram_body, grid=(variables,), in_specs=[pl.BlockSpec((1, c...  5.18 us
    pallas_call x1, Pallas kernels, subspace(): pl.pallas_call(functools.partial(subspace_body, total_rows=total_rows, cl...  2.86 us
    unnamed x8, local copies, waits for them, and re-layouts  2.34 us
  transfers between devices with their start and end apart: 7, of which 4 were waited for; matrix products, arithmetic and copies ran while one was open for 1% of the time, Pallas kernels for 51%

profile of v1, /device:TPU:1, one launch (start us, length us, event | category | flops | bytes accessed | tf_op | source)
XLA Modules:
  0.0 105.8 jit_solution(1950614584631382484)
XLA Ops:
  0.6 0.0 copy-start.3
  0.6 5.2 %gram.1 = f32[128,128]{1,0:T(8,128)} custom-call(bf16[5,128,3072]{2,1,0:T(8,128)(2,1)} %bitcast.9), custom_call_target="tpu_custom_call" | custom-call | flops 503316480 | bytes 3932160 | tf_op jit(solution)/shard_map/gram/pallas_call | solution.py:28
  5.8 0.1 collective-permute-start
  5.9 1.4 %collective-permute-done = f32[128,128]{1,0:T(8,128)S(1)} collective-permute-done((f32[128,128]{1,0:T(8,128)}, f32[128,128]{1,0:T(8,128)S(1)}, u32[]{:S(2)}, u32[]{:S(2)}) %collective-permute-start) | collective-permute-done | bytes 65568 | tf_op jit(solution)/shard_map/ppermute | solution.py:186
  7.3 0.9 add.12
  8.1 2.4 %collective-permute-start.1 = (f32[128,128]{1,0:T(8,128)S(1)}, f32[128,128]{1,0:T(8,128)S(1)}, u32[]{:S(2)}, u32[]{:S(2)}) collective-permute-start(f32[128,128]{1,0:T(8,128)S(1)} %add.12), channel_id=1, source_target_pairs={{0,2},{1,3},{2,0},{3,1},{4,6},{5,7},{6,4},{7,5},{8,10},{9,11},{10,... | collective-permute-start | bytes 196616 | tf_op jit(solution)/shard_map/ppermute | solution.py:186
  10.6 2.2 %collective-permute-done.1 = f32[128,128]{1,0:T(8,128)S(1)} collective-permute-done((f32[128,128]{1,0:T(8,128)S(1)}, f32[128,128]{1,0:T(8,128)S(1)}, u32[]{:S(2)}, u32[]{:S(2)}) %collective-permute-start.1) | collective-permute-done | bytes 65568 | tf_op jit(solution)/shard_map/ppermute | solution.py:186
  12.8 1.1 %collective-permute-start.2 = (f32[128,128]{1,0:T(8,128)S(1)}, f32[128,128]{1,0:T(8,128)S(1)}, u32[]{:S(2)}, u32[]{:S(2)}) collective-permute-start(f32[128,128]{1,0:T(8,128)S(1)} %add.13), channel_id=1, source_target_pairs={{0,4},{4,0},{8,12},{12,8},{1,5},{5,1},{9,13},{13,9},{2,6},{6,2},{1... | collective-permute-start | bytes 196616 | tf_op jit(solution)/shard_map/ppermute | solution.py:186
  13.8 2.1 %collective-permute-done.2 = f32[128,128]{1,0:T(8,128)S(1)} collective-permute-done((f32[128,128]{1,0:T(8,128)S(1)}, f32[128,128]{1,0:T(8,128)S(1)}, u32[]{:S(2)}, u32[]{:S(2)}) %collective-permute-start.2) | collective-permute-done | bytes 65568 | tf_op jit(solution)/shard_map/ppermute | solution.py:186
  15.9 2.1 %collective-permute-start.3 = (f32[128,128]{1,0:T(8,128)S(1)}, f32[128,128]{1,0:T(8,128)S(1)}, u32[]{:S(2)}, u32[]{:S(2)}) collective-permute-start(f32[128,128]{1,0:T(8,128)S(1)} %add.14), channel_id=1, source_target_pairs={{0,8},{4,12},{8,0},{12,4},{1,9},{5,13},{9,1},{13,5},{2,10},{6,14},... | collective-permute-start | bytes 196616 | tf_op jit(solution)/shard_map/ppermute | solution.py:186
  18.0 0.0 copy-done.3
  18.1 0.7 copy.9.column_ref
  18.8 1.2 %collective-permute-done.3 = f32[128,128]{1,0:T(8,128)S(1)} collective-permute-done((f32[128,128]{1,0:T(8,128)S(1)}, f32[128,128]{1,0:T(8,128)S(1)}, u32[]{:S(2)}, u32[]{:S(2)}) %collective-permute-start.3) | collective-permute-done | bytes 65568 | tf_op jit(solution)/shard_map/ppermute | solution.py:186
  20.0 0.6 add.15.gram_ref
  20.7 2.9 %subspace.1 = (f32[16,128]{1,0:T(8,128)}, bf16[4,16,128]{2,1,0:T(8,128)(2,1)}) custom-call(s32[1]{0:T(128)} %bitcast.me_ref, f32[128,128]{1,0:T(8,128)} %add.15.gram_ref, s32[1,128]{1,0:T(1,128)} %bitcast.14, s32[128,1]{1,0:T(8,128)} %copy.9.column_ref, f32[16,128]{1,0:T(8,128)} %bitcast.13), custom_call_target="tpu_custom_call" | custom-call | tf_op jit(solution)/shard_map/subspace/pallas_call | solution.py:81
  23.5 5.2 %modes.2 = (bf16[5,16,3072]{2,1,0:T(8,128)(2,1)}, bf16[5,16,3072]{2,1,0:T(8,128)(2,1)}) custom-call(bf16[4,16,128]{2,1,0:T(8,128)(2,1)} %get-tuple-element.11.left_ref, bf16[5,128,3072]{2,1,0:T(8,128)(2,1)} %bitcast.10), custom_call_target="tpu_custom_call" | custom-call | flops 125829120 | bytes 4915200 | tf_op jit(solution)/shard_map/modes/pallas_call | solution.py:135
  28.7 3.2 %collective-permute-start.4 = (bf16[5,16,3072]{2,1,0:T(8,128)(2,1)}, bf16[5,16,3072]{2,1,0:T(8,128)(2,1)S(1)}, u32[]{:S(2)}, u32[]{:S(2)}) collective-permute-start(bf16[5,16,3072]{2,1,0:T(8,128)(2,1)} %get-tuple-element.13), channel_id=1, source_target_pairs={{0,1},{1,0},{2,3},{3,2},{4,5},{5,4},{6,7},{7,6},{8,9},{9,8},{10,11... | collective-permute-start | bytes 1474568 | tf_op jit(solution)/shard_map/ppermute | solution.py:186
  31.9 5.2 %modes.3 = (bf16[5,16,3072]{2,1,0:T(8,128)(2,1)}, bf16[5,16,3072]{2,1,0:T(8,128)(2,1)}) custom-call(bf16[4,16,128]{2,1,0:T(8,128)(2,1)} %get-tuple-element.11.left_ref, bf16[5,128,3072]{2,1,0:T(8,128)(2,1)} %bitcast.11), custom_call_target="tpu_custom_call" | custom-call | flops 125829120 | bytes 4915200 | tf_op jit(solution)/shard_map/modes/pallas_call | solution.py:135
  37.1 1.5 %collective-permute-start.5 = (bf16[5,16,3072]{2,1,0:T(8,128)(2,1)}, bf16[5,16,3072]{2,1,0:T(8,128)(2,1)S(1)}, u32[]{:S(2)}, u32[]{:S(2)}) collective-permute-start(bf16[5,16,3072]{2,1,0:T(8,128)(2,1)} %get-tuple-element.14), channel_id=1, source_target_pairs={{0,2},{1,3},{2,0},{3,1},{4,6},{5,7},{6,4},{7,5},{8,10},{9,11},{10,... | collective-permute-start | bytes 1474568 | tf_op jit(solution)/shard_map/ppermute | solution.py:186
  38.6 0.1 collective-permute-start.6
  38.7 1.8 %small.1 = (f32[16,32]{1,0:T(8,128)}, f32[1,16,16]{2,1,0:T(8,128)}) custom-call(s32[1]{0:T(128)} %bitcast.me_ref, s32[4]{0:T(128)} %successor_ref.1, f32[128,128]{1,0:T(8,128)} %add.15.gram_ref, s32[1,128]{1,0:T(1,128)} %bitcast.15, f32[16,128]{1,0:T(8,128)} %get-tuple-element.16.basis_ref), custom_call_target="tpu_custom_call" | custom-call | tf_op jit(solution)/shard_map/small/pallas_call | solution.py:113
  40.5 0.0 collective-permute-done.4.refs_1_
  40.5 0.0 copy-start
  40.5 0.8 copy-done
  41.3 30.9 %place.3.refs_0_ = bf16[5,16,12288]{2,1,0:T(8,128)(2,1)} custom-call(s32[1]{0:T(128)} %bitcast.me_ref, bf16[5,16,3072]{2,1,0:T(8,128)(2,1)} %get-tuple-element.12.refs_0_, bf16[5,16,3072]{2,1,0:T(8,128)(2,1)} %copy-done), custom_call_target="tpu_custom_call" | custom-call | tf_op jit(solution)/shard_map/place/pallas_call | solution.py:173
  72.2 0.0 collective-permute-done.5.refs_1_
  72.2 0.0 copy-start.2
  72.2 0.8 copy-done.2
  73.0 16.0 %place.4.refs_0_ = bf16[5,16,12288]{2,1,0:T(8,128)(2,1)} custom-call(s32[1]{0:T(128)} %bitcast.me_ref, bf16[5,16,12288]{2,1,0:T(8,128)(2,1)} %place.3.refs_0_, bf16[5,16,3072]{2,1,0:T(8,128)(2,1)} %copy-done.2), custom_call_target="tpu_custom_call", output_to_operand_aliasing={{}: (1, {})} | custom-call | tf_op jit(solution)/shard_map/place/pallas_call | solution.py:173
  89.0 0.0 collective-permute-done.6.refs_1_
  89.0 0.0 copy-start.1
  89.0 0.8 copy-done.1
  89.8 16.0 %place.5 = bf16[5,16,12288]{2,1,0:T(8,128)(2,1)} custom-call(s32[1]{0:T(128)} %bitcast.me_ref, bf16[5,16,12288]{2,1,0:T(8,128)(2,1)} %place.4.refs_0_, bf16[5,16,3072]{2,1,0:T(8,128)(2,1)} %copy-done.1), custom_call_target="tpu_custom_call", output_to_operand_aliasing={{}: (1, {})} | custom-call | tf_op jit(solution)/shard_map/place/pallas_call | solution.py:173
  (2 shorter events, 0.0 us)
Async XLA Ops:
  0.6 17.4 %copy-start.3 = (s32[128]{0:T(128)S(1)}, s32[128]{0:T(128)}, u32[]{:S(2)}) copy-start(s32[128]{0:T(128)} %param.5) | copy-start | bytes 1540
  5.8 1.5 %collective-permute-start = (f32[128,128]{1,0:T(8,128)}, f32[128,128]{1,0:T(8,128)S(1)}, u32[]{:S(2)}, u32[]{:S(2)}) collective-permute-start(f32[128,128]{1,0:T(8,128)} %gram.1), channel_id=1, source_target_pairs={{0,1},{1,0},{2,3},{3,2},{4,5},{5,4},{6,7},{7,6},{8,9},{9,8},{10,11... | collective-permute-start | bytes 196616 | tf_op jit(solution)/shard_map/ppermute | solution.py:186
  8.1 4.6 %collective-permute-start.1 = (f32[128,128]{1,0:T(8,128)S(1)}, f32[128,128]{1,0:T(8,128)S(1)}, u32[]{:S(2)}, u32[]{:S(2)}) collective-permute-start(f32[128,128]{1,0:T(8,128)S(1)} %add.12), channel_id=1, source_target_pairs={{0,2},{1,3},{2,0},{3,1},{4,6},{5,7},{6,4},{7,5},{8,10},{9,11},{10,... | collective-permute-start | bytes 196616 | tf_op jit(solution)/shard_map/ppermute | solution.py:186
  12.8 3.2 %collective-permute-start.2 = (f32[128,128]{1,0:T(8,128)S(1)}, f32[128,128]{1,0:T(8,128)S(1)}, u32[]{:S(2)}, u32[]{:S(2)}) collective-permute-start(f32[128,128]{1,0:T(8,128)S(1)} %add.13), channel_id=1, source_target_pairs={{0,4},{4,0},{8,12},{12,8},{1,5},{5,1},{9,13},{13,9},{2,6},{6,2},{1... | collective-permute-start | bytes 196616 | tf_op jit(solution)/shard_map/ppermute | solution.py:186
  15.9 4.1 %collective-permute-start.3 = (f32[128,128]{1,0:T(8,128)S(1)}, f32[128,128]{1,0:T(8,128)S(1)}, u32[]{:S(2)}, u32[]{:S(2)}) collective-permute-start(f32[128,128]{1,0:T(8,128)S(1)} %add.14), channel_id=1, source_target_pairs={{0,8},{4,12},{8,0},{12,4},{1,9},{5,13},{9,1},{13,5},{2,10},{6,14},... | collective-permute-start | bytes 196616 | tf_op jit(solution)/shard_map/ppermute | solution.py:186
  28.7 11.8 %collective-permute-start.4 = (bf16[5,16,3072]{2,1,0:T(8,128)(2,1)}, bf16[5,16,3072]{2,1,0:T(8,128)(2,1)S(1)}, u32[]{:S(2)}, u32[]{:S(2)}) collective-permute-start(bf16[5,16,3072]{2,1,0:T(8,128)(2,1)} %get-tuple-element.13), channel_id=1, source_target_pairs={{0,1},{1,0},{2,3},{3,2},{4,5},{5,4},{6,7},{7,6},{8,9},{9,8},{10,11... | collective-permute-start | bytes 1474568 | tf_op jit(solution)/shard_map/ppermute | solution.py:186
  37.1 35.1 %collective-permute-start.5 = (bf16[5,16,3072]{2,1,0:T(8,128)(2,1)}, bf16[5,16,3072]{2,1,0:T(8,128)(2,1)S(1)}, u32[]{:S(2)}, u32[]{:S(2)}) collective-permute-start(bf16[5,16,3072]{2,1,0:T(8,128)(2,1)} %get-tuple-element.14), channel_id=1, source_target_pairs={{0,2},{1,3},{2,0},{3,1},{4,6},{5,7},{6,4},{7,5},{8,10},{9,11},{10,... | collective-permute-start | bytes 1474568 | tf_op jit(solution)/shard_map/ppermute | solution.py:186
  38.6 50.4 %collective-permute-start.6 = (bf16[5,16,3072]{2,1,0:T(8,128)(2,1)}, bf16[5,16,3072]{2,1,0:T(8,128)(2,1)S(1)}, u32[]{:S(2)}, u32[]{:S(2)}) collective-permute-start(bf16[5,16,3072]{2,1,0:T(8,128)(2,1)} %get-tuple-element.15), channel_id=1, source_target_pairs={{0,3},{1,2},{2,1},{3,0},{4,7},{5,6},{6,5},{7,4},{8,11},{9,10},{10,... | collective-permute-start | bytes 1474568 | tf_op jit(solution)/shard_map/ppermute | solution.py:186
  40.5 0.8 copy-start
  72.2 0.8 copy-start.2
  89.0 0.8 copy-start.1

commit v2 on v0

v2 whole, which is shorter than its diff:
```python
import functools

import jax
import jax.numpy as jnp
from jax import lax
from jax.experimental import pallas as pl
from jax.experimental.pallas import tpu as pltpu
from jax.sharding import PartitionSpec as P

ITERS = 2
CAP = 8
HIGH = lax.Precision.HIGHEST
IN_VMEM = pl.BlockSpec(memory_space=pltpu.VMEM)
IN_SMEM = pl.BlockSpec(memory_space=pltpu.SMEM)
ANYWHERE = pl.BlockSpec(memory_space=pl.ANY)
LIMIT = 20 * 1024 * 1024
LARGE = 46 * 1024 * 1024
EARLY = 1152


def call(body, name, in_specs, outs, *operands, flops=0, scratch=(), aliases=None, out_specs=None, limit=LIMIT):
    return pl.pallas_call(
        body,
        in_specs=in_specs,
        out_specs=out_specs or [IN_VMEM] * len(outs),
        out_shape=outs,
        scratch_shapes=list(scratch),
        input_output_aliases=aliases or {},
        compiler_params=pltpu.CompilerParams(vmem_limit_bytes=limit),
        cost_estimate=pl.CostEstimate(flops=0, bytes_accessed=0, transcendentals=0),
        name=name,
    )(*operands)


def same_cluster(row_labels):
    count = row_labels.shape[1]
    wide = jnp.broadcast_to(row_labels.astype(jnp.float32), (count, count))
    return wide.T == wide


def slot_choice(row_labels, same, cluster, slots):
    count = row_labels.shape[1]
    earlier = lax.broadcasted_iota(jnp.int32, (count, count), 0) < lax.broadcasted_iota(
        jnp.int32, (count, count), 1
    )
    rank = jnp.sum(jnp.where(same & earlier, 1.0, 0.0), axis=0, keepdims=True).astype(jnp.int32)
    wanted = lax.broadcasted_iota(jnp.int32, (slots, count), 0)
    return jnp.where((rank == wanted) & (row_labels == cluster), 1.0, 0.0).astype(jnp.bfloat16)


def gram_body(me_ref, row_ref, x_hbm, gram_ref, x_ref, *refs, far):
    pick_refs = refs[: len(far)]
    sems = refs[len(far)]
    variables = x_ref.shape[0]
    copies = [pltpu.make_async_copy(x_hbm.at[v], x_ref.at[v], sems.at[v]) for v in range(variables)]
    for copy in copies:
        copy.start()
    row_labels = row_ref[...]
    same = same_cluster(row_labels)
    slots, early = pick_refs[0].shape[1:]
    choice = jnp.concatenate(
        [slot_choice(row_labels, same, me_ref[0] ^ k, slots) for k in far], axis=0
    )
    total = None
    for v in range(variables):
        copies[v].wait()
        x = x_ref[v]
        part = lax.dot_general(x, x, (((1,), (1,)), ((), ())), preferred_element_type=jnp.float32)
        total = part if total is None else total + part
        rows = jnp.dot(choice, x[:, :early], preferred_element_type=jnp.float32)
        rows = rows.astype(jnp.bfloat16)
        for i, pick_ref in enumerate(pick_refs):
            pick_ref[v] = rows[i * slots : (i + 1) * slots]
    gram_ref[...] = total


def partial_gram(me, labels, x, far, slots, early):
    variables, count, cells = x.shape
    picked = pltpu.VMEM((variables, slots, early), jnp.bfloat16)
    return call(
        functools.partial(gram_body, far=far),
        "gram",
        [IN_SMEM, IN_VMEM, ANYWHERE],
        [pltpu.VMEM((count, count), jnp.float32), pltpu.VMEM(x.shape, x.dtype)] + [picked for _ in far],
        me,
        labels,
        x,
        scratch=[pltpu.SemaphoreType.DMA((variables,))],
        limit=LARGE,
    )


def orthonormal(image, same):
    modes = image.shape[0]
    products = jnp.concatenate([image * image[c : c + 1, :] for c in range(modes)], axis=0)
    inner = jnp.dot(products, same, precision=HIGH, preferred_element_type=jnp.float32)
    columns = [inner[c * modes : (c + 1) * modes] for c in range(modes)]
    row = lax.broadcasted_iota(jnp.int32, image.shape, 0)
    scale = jnp.zeros_like(image)
    for j in range(modes):
        pivot = columns[j][j : j + 1, :]
        scale = jnp.where(row == j, lax.rsqrt(pivot), scale)
        if j + 1 < modes:
            factor = jnp.where(row > j, columns[j] * (1.0 / pivot), 0.0)
            for c in range(j + 1, modes):
                columns[c] = columns[c] - factor * columns[c][j : j + 1, :]
            image = image - factor * image[j : j + 1, :]
    return image * scale


def subspace_body(
    me_ref, first_ref, second_ref, row_ref, start_ref, gram_ref, basis_ref, left_ref, own_ref, *, total_rows
):
    clusters = left_ref.shape[0]
    row_labels = row_ref[...]
    together = same_cluster(row_labels)
    gram = (first_ref[...] + second_ref[...]) * (1.0 / total_rows)
    gram_ref[...] = gram
    same = together.astype(jnp.float32)
    rows = lax.broadcasted_iota(jnp.int32, gram.shape, 0)
    lanes = lax.broadcasted_iota(jnp.int32, gram.shape, 1)
    shifted = gram * same + (rows == lanes).astype(jnp.float32)
    basis = start_ref[...]
    for step in range(ITERS):
        image = jnp.dot(basis, shifted, precision=HIGH, preferred_element_type=jnp.float32)
        basis = orthonormal(image, same)
    basis_ref[...] = basis
    rounded = basis.astype(jnp.bfloat16).astype(jnp.float32)
    me = me_ref[0]
    for k in range(clusters):
        left_ref[k] = jnp.where(row_labels == (me ^ k), rounded, 0.0).astype(jnp.bfloat16)
    choice = slot_choice(row_labels, together, me, own_ref.shape[1])
    own_ref[...] = lax.dot_general(
        rounded.astype(jnp.bfloat16), choice, (((1,), (1,)), ((), ())), preferred_element_type=jnp.float32
    ).astype(jnp.bfloat16)


def subspace(me, first, second, labels, start, total_rows, clusters, slots):
    modes, count = start.shape
    return call(
        functools.partial(subspace_body, total_rows=total_rows),
        "subspace",
        [IN_SMEM, IN_VMEM, IN_VMEM, IN_VMEM, IN_VMEM],
        [
            pltpu.VMEM((count, count), jnp.float32),
            pltpu.VMEM((modes, count), jnp.float32),
            pltpu.VMEM((clusters, modes, count), jnp.bfloat16),
            pltpu.VMEM((modes, slots), jnp.bfloat16),
        ],
        me,
        first,
        second,
        labels,
        start,
    )


def small_body(me_ref, successor_ref, gram_ref, row_ref, basis_ref, coefficients_ref, correlations_ref):
    me = me_ref[0]
    row_labels = row_ref[...]
    basis = basis_ref[...]
    rounded = basis.astype(jnp.bfloat16).astype(jnp.float32)
    mine = jnp.where(row_labels == me, rounded, 0.0)
    other = jnp.where(row_labels == successor_ref[me], rounded, 0.0)
    image = jnp.dot(mine, gram_ref[...], precision=HIGH, preferred_element_type=jnp.float32)
    correlations_ref[0] = lax.dot_general(
        image, other, (((1,), (1,)), ((), ())), precision=HIGH, preferred_element_type=jnp.float32
    )
    count = basis.shape[1]
    own = coefficients_ref.shape[1]
    coefficients_ref[...] = pltpu.roll(basis, (count - me * own) % count, 1)[:, :own]


def small_outputs(me, successor, gram, labels, basis, clusters):
    modes, count = basis.shape
    return call(
        small_body,
        "small",
        [IN_SMEM, IN_SMEM, IN_VMEM, IN_VMEM, IN_VMEM],
        [
            jax.ShapeDtypeStruct((modes, count // clusters), jnp.float32),
            jax.ShapeDtypeStruct((1, modes, modes), jnp.float32),
        ],
        me,
        successor,
        gram,
        labels,
        basis,
    )


def modes_body(left_ref, x_ref, *out_refs):
    clusters, modes, count = left_ref.shape
    near = left_ref[:2].reshape(2 * modes, count)
    left = left_ref[2:].reshape((clusters - 2) * modes, count)
    begin = x_ref.shape[2] - out_refs[2].shape[2]
    for v in range(x_ref.shape[0]):
        product = jnp.dot(left, x_ref[v, :, begin:], preferred_element_type=jnp.float32)
        product = product.astype(jnp.bfloat16)
        for i, out_ref in enumerate(out_refs[2:]):
            out_ref[v] = product[i * modes : (i + 1) * modes]
        product = jnp.dot(near, x_ref[v], preferred_element_type=jnp.float32)
        product = product.astype(jnp.bfloat16)
        for i, out_ref in enumerate(out_refs[:2]):
            out_ref[v] = product[i * modes : (i + 1) * modes]


def local_modes(left, x, begin):
    variables, count, cells = x.shape
    clusters, modes, _ = left.shape
    near = pltpu.VMEM((variables, modes, cells), jnp.bfloat16)
    late = pltpu.VMEM((variables, modes, cells - begin), jnp.bfloat16)
    return call(
        modes_body,
        "modes",
        [IN_VMEM, IN_VMEM],
        [near, near] + [late] * (clusters - 2),
        left,
        x,
    )


def owner_body(me_ref, own_ref, near_ref, near2_ref, *refs, far):
    rows_refs = refs[: len(far)]
    out_ref = refs[len(far)]
    early_refs = refs[len(far) + 1 : 2 * len(far) + 1]
    sems = refs[2 * len(far) + 1]
    me = me_ref[0]
    cells = near_ref.shape[2]
    copies = []

    def put(source, k):
        at = pl.multiple_of((me ^ k) * cells, 128)
        copy = pltpu.make_async_copy(
            source, out_ref.at[:, :, pl.ds(at, source.shape[2])], sems.at[len(copies)]
        )
        copy.start()
        copies.append(copy)

    put(near_ref, 0)
    put(near2_ref, 1)
    own = own_ref[...]
    for k, rows_ref, early_ref in zip(far, rows_refs, early_refs):
        for v in range(rows_ref.shape[0]):
            early_ref[v] = jnp.dot(own, rows_ref[v], preferred_element_type=jnp.float32).astype(
                jnp.bfloat16
            )
        put(early_ref, k)
    for copy in copies:
        copy.wait()


def owner_modes(me, own, near, rows, far, clusters):
    variables, modes, cells = near[0].shape
    early = rows[0].shape[2]
    scratch = [pltpu.VMEM((variables, modes, early), jnp.bfloat16) for _ in far]
    return call(
        functools.partial(owner_body, far=far),
        "owner",
        [IN_SMEM] + [IN_VMEM] * (3 + len(rows)),
        [jax.ShapeDtypeStruct((variables, modes, clusters * cells), jnp.bfloat16)],
        me,
        own,
        *near,
        *rows,
        scratch=scratch + [pltpu.SemaphoreType.DMA((2 + len(far),))],
        out_specs=[ANYWHERE],
    )[0]


def place_body(me_ref, out_in_ref, piece_ref, out_ref, sem, *, offset, cells):
    late = piece_ref.shape[2]
    at = pl.multiple_of((me_ref[0] ^ offset) * cells + (cells - late), 128)
    copy = pltpu.make_async_copy(piece_ref, out_ref.at[:, :, pl.ds(at, late)], sem)
    copy.start()
    copy.wait()


def place(me, out, piece, offset, clusters):
    return call(
        functools.partial(place_body, offset=offset, cells=out.shape[2] // clusters),
        "place",
        [IN_SMEM, ANYWHERE, IN_VMEM],
        [jax.ShapeDtypeStruct(out.shape, out.dtype)],
        me,
        out,
        piece,
        scratch=[pltpu.SemaphoreType.DMA],
        aliases={1: 0},
        out_specs=[ANYWHERE],
    )[0]


def swap(x, axis, offset):
    size = lax.axis_size(axis)
    return lax.ppermute(x, axis, [(i, i ^ offset) for i in range(size)])


def local(snapshots, labels, start, successor):
    count, variables, cells = snapshots.shape
    clusters = lax.axis_size("clus")
    space = lax.axis_size("space")
    me = lax.axis_index("clus").astype(jnp.int32).reshape(1)
    total_rows = variables * cells * space * clusters
    slots = CAP * clusters
    far = list(range(2, clusters))
    labels = labels[None, :]
    x = jnp.transpose(snapshots, (1, 0, 2))
    gram, x, *picked = partial_gram(me, labels, x, far, slots, EARLY)
    rounds = [("clus", 1 << b) for b in range(1, clusters.bit_length() - 1)]
    links = len(rounds)
    rounds += [("clus", 1)]
    rounds += [("space", 1 << b) for b in range(space.bit_length() - 1)]
    other = None
    for step, (axis, offset) in enumerate(rounds):
        if other is not None:
            gram = gram + other
        other = swap(gram, axis, offset)
        if step == links - 1:
            other, *picked = lax.optimization_barrier((other, *picked))
            rows = [swap(piece, "clus", k) for piece, k in zip(picked, far)]
    gram, basis, left, own = subspace(
        me, gram, other, labels, start.T, total_rows, clusters, slots
    )
    own_piece, sibling, *late = local_modes(left, x, EARLY)
    both = lax.optimization_barrier((*late, *rows, sibling))
    late, rows, sibling = both[: len(far)], both[len(far) : -1], both[-1]
    late = [swap(piece, "clus", k) for piece, k in zip(late, far)]
    near = [own_piece, swap(sibling, "clus", 1)]
    coefficients, correlations = small_outputs(me, successor, gram, labels, basis, clusters)
    out = owner_modes(me, own, near, rows, far, clusters)
    for piece, k in zip(late, far):
        out = place(me, out, piece, k, clusters)
    modes_out = jnp.transpose(out, (1, 0, 2))[None]
    return modes_out, coefficients.T, correlations


def solution(mesh):
    in_specs = (P("groups", None, ("space", "clus")), P("groups"), P("groups", None), P("groups"))
    out_specs = (
        P(("groups", "clus"), None, None, "space"),
        P(("groups", "clus"), None),
        P(("groups", "clus"), None, None),
    )
    return jax.shard_map(local, mesh=mesh, in_specs=in_specs, out_specs=out_specs, check_vma=False)
```

time: 175 us -> 43.7 us (0.25); the launches traced: 172 us -> 43.5 us
  waiting for transfers between devices: 102 us -> 19.5 us
  other arithmetic: 22.1 us -> 0.03 us
  local copies, waits for them, and re-layouts: 16.3 us -> 0.66 us
  matrix products: 13.6 us -> 0 us
  between operations: 14.2 us -> 0.7 us
  Pallas kernels: 0 us -> 10.5 us
  starting transfers between devices: 3.8 us -> 12.1 us
    psum x1 -> x0, waiting for transfers between devices: 80.9 us -> none  [local(): gram = lax.psum(partial_value, ('space', 'clus')) / total_rows]
    another operation x12 -> x0, other arithmetic: 22 us -> none  [the longest x7 12 us: subspace(): lower = jnp.linalg.cholesky(inner)]
    all_to_all x1 -> x0, waiting for transfers between devices: 21.5 us -> none  [local(): lax.all_to_all(packed, 'clus', split_axis=0, concat_axis=3, tiled=True)]
    ppermute x0 -> x9, waiting for transfers between devices: none -> 19.5 us  [swap(): return lax.ppermute(x, axis, [(i, i ^ offset) for i in range(size)])]
    dot_general x9 -> x0, matrix products: 13 us -> none  [the longest x1 5.13 us: local(): lax.dot_general(flat, flat, (((1,), (1,)), ((), ())), preferred_element_t...]
    ppermute x0 -> x9, starting transfers between devices: none -> 12.1 us  [swap(): return lax.ppermute(x, axis, [(i, i ^ offset) for i in range(size)])]
    pallas_call x0 -> x7, Pallas kernels: none -> 10.5 us  [call(): pl.pallas_call(body, in_specs=in_specs, out_specs=out_specs or [IN_VMEM]...]
    reshape x2 -> x0, local copies, waits for them, and re-layouts: 7.12 us -> none  [local(): modes_full.astype(jnp.bfloat16)]
  transfers between devices with their start and end apart: 2 -> 9, of which waited for: 2 -> 7; matrix products, arithmetic and copies ran while one was open for 5% -> 0% of each run, Pallas kernels for 0% -> 13%
where the time goes in v2:
time: 43.7 us; the launch traced here: 43.5 us
  waiting for transfers between devices  19.5 us (45%)
  starting transfers between devices  12.1 us (28%)
  Pallas kernels  10.5 us (24%)
  between operations  0.7 us (2%)
  local copies, waits for them, and re-layouts  0.66 us (2%)
    ppermute x9, waiting for transfers between devices, swap(): return lax.ppermute(x, axis, [(i, i ^ offset) for i in range(size)])  19.5 us
    ppermute x9, starting transfers between devices, swap(): return lax.ppermute(x, axis, [(i, i ^ offset) for i in range(size)])  12.1 us
    pallas_call x7, Pallas kernels, call(): pl.pallas_call(body, in_specs=in_specs, out_specs=out_specs or [IN_VMEM]...  10.5 us
  transfers between devices with their start and end apart: 9, of which 7 were waited for; matrix products, arithmetic and copies ran while one was open for 0% of the time, Pallas kernels for 13%

profile of v2, /device:TPU:1, one launch (start us, length us, event | category | flops | bytes accessed | tf_op | source)
XLA Modules:
  0.0 43.5 jit_solution(5431764517934019324)
XLA Ops:
  0.6 0.0 copy-start.1
  0.6 0.6 %copy-done.1 = s32[128]{0:T(128)S(1)} copy-done((s32[128]{0:T(128)S(1)}, s32[128]{0:T(128)}, u32[]{:S(2)}) %copy-start.1) | copy-done | bytes 536
  1.3 0.0 copy-start
  1.3 3.9 %gram.1 = (f32[128,128]{1,0:T(8,128)S(1)}, bf16[5,128,3072]{2,1,0:T(8,128)(2,1)S(1)}, bf16[5,32,1152]{2,1,0:T(8,128)(2,1)S(1)}, bf16[5,32,1152]{2,1,0:T(8,128)(2,1)S(1)}) custom-call(s32[1]{0:T(128)} %bitcast.me_ref, s32[1,128]{1,0:T(1,128)S(1)} %bitcast.9, bf16[5,128,3072]{2,1,0:T(8,128)(2,1)} %bitcast.13), custom_call_target="tpu_custom_call" | custom-call | tf_op jit(solution)/shard_map/gram/pallas_call | solution.py:22
  5.2 2.1 %collective-permute-start = (f32[128,128]{1,0:T(8,128)S(1)}, f32[128,128]{1,0:T(8,128)S(1)}, u32[]{:S(2)}, u32[]{:S(2)}) collective-permute-start(f32[128,128]{1,0:T(8,128)S(1)} %get-tuple-element.25), channel_id=1, source_target_pairs={{0,2},{1,3},{2,0},{3,1},{4,6},{5,7},{6,4},{7,5},{8,10},{9,11},{10,... | collective-permute-start | bytes 196616 | tf_op jit(solution)/shard_map/ppermute | solution.py:296
  7.3 1.7 %collective-permute-done = f32[128,128]{1,0:T(8,128)S(1)} collective-permute-done((f32[128,128]{1,0:T(8,128)S(1)}, f32[128,128]{1,0:T(8,128)S(1)}, u32[]{:S(2)}, u32[]{:S(2)}) %collective-permute-start) | collective-permute-done | bytes 65568 | tf_op jit(solution)/shard_map/ppermute | solution.py:296
  9.0 1.5 %collective-permute-start.4 = (bf16[5,32,1152]{2,1,0:T(8,128)(2,1)S(1)}, bf16[5,32,1152]{2,1,0:T(8,128)(2,1)S(1)}, u32[]{:S(2)}, u32[]{:S(2)}) collective-permute-start(bf16[5,32,1152]{2,1,0:T(8,128)(2,1)S(1)} %get-tuple-element.35), channel_id=1, source_target_pairs={{0,2},{1,3},{2,0},{3,1},{4,6},{5,7},{6,4},{7,5},{8,10},{9,11},{10,... | collective-permute-start | bytes 1105928 | tf_op jit(solution)/shard_map/ppermute | solution.py:296
  10.4 1.7 %collective-permute-start.5 = (bf16[5,32,1152]{2,1,0:T(8,128)(2,1)S(1)}, bf16[5,32,1152]{2,1,0:T(8,128)(2,1)S(1)}, u32[]{:S(2)}, u32[]{:S(2)}) collective-permute-start(bf16[5,32,1152]{2,1,0:T(8,128)(2,1)S(1)} %get-tuple-element.36), channel_id=1, source_target_pairs={{0,3},{1,2},{2,1},{3,0},{4,7},{5,6},{6,5},{7,4},{8,11},{9,10},{10,... | collective-permute-start | bytes 1105928 | tf_op jit(solution)/shard_map/ppermute | solution.py:296
  12.2 0.4 collective-permute-start.1
  12.6 0.9 %collective-permute-done.1 = f32[128,128]{1,0:T(8,128)S(1)} collective-permute-done((f32[128,128]{1,0:T(8,128)S(1)}, f32[128,128]{1,0:T(8,128)S(1)}, u32[]{:S(2)}, u32[]{:S(2)}) %collective-permute-start.1) | collective-permute-done | bytes 65568 | tf_op jit(solution)/shard_map/ppermute | solution.py:296
  13.5 1.8 %collective-permute-start.2 = (f32[128,128]{1,0:T(8,128)S(1)}, f32[128,128]{1,0:T(8,128)S(1)}, u32[]{:S(2)}, u32[]{:S(2)}) collective-permute-start(f32[128,128]{1,0:T(8,128)S(1)} %add.10), channel_id=1, source_target_pairs={{0,4},{4,0},{8,12},{12,8},{1,5},{5,1},{9,13},{13,9},{2,6},{6,2},{1... | collective-permute-start | bytes 196616 | tf_op jit(solution)/shard_map/ppermute | solution.py:296
  15.4 2.2 %collective-permute-done.2 = f32[128,128]{1,0:T(8,128)S(1)} collective-permute-done((f32[128,128]{1,0:T(8,128)S(1)}, f32[128,128]{1,0:T(8,128)S(1)}, u32[]{:S(2)}, u32[]{:S(2)}) %collective-permute-start.2) | collective-permute-done | bytes 65568 | tf_op jit(solution)/shard_map/ppermute | solution.py:296
  17.6 2.4 %collective-permute-start.3 = (f32[128,128]{1,0:T(8,128)S(1)}, f32[128,128]{1,0:T(8,128)S(1)}, u32[]{:S(2)}, u32[]{:S(2)}) collective-permute-start(f32[128,128]{1,0:T(8,128)S(1)} %add.11.first_ref), channel_id=1, source_target_pairs={{0,8},{4,12},{8,0},{12,4},{1,9},{5,13},{9,1},{13,5},{2,10},{6,14},... | collective-permute-start | bytes 196616 | tf_op jit(solution)/shard_map/ppermute | solution.py:296
  20.0 1.7 %collective-permute-done.3.second_ref = f32[128,128]{1,0:T(8,128)S(1)} collective-permute-done((f32[128,128]{1,0:T(8,128)S(1)}, f32[128,128]{1,0:T(8,128)S(1)}, u32[]{:S(2)}, u32[]{:S(2)}) %collective-permute-start.3) | collective-permute-done | bytes 65568 | tf_op jit(solution)/shard_map/ppermute | solution.py:296
  21.7 0.0 copy-done
  21.7 1.5 %subspace.1 = (f32[128,128]{1,0:T(8,128)S(1)}, f32[16,128]{1,0:T(8,128)S(1)}, bf16[4,16,128]{2,1,0:T(8,128)(2,1)S(1)}, bf16[16,32]{1,0:T(8,128)(2,1)S(1)}) custom-call(s32[1]{0:T(128)} %bitcast.me_ref, f32[128,128]{1,0:T(8,128)S(1)} %add.11.first_ref, f32[128,128]{1,0:T(8,128)S(1)} %collective-permute-done.3.second_ref, s32[1,128]{1,0:T(1,128)S(1)} %bitcast.10, ...), custom_call_target="tpu_custom_call" | custom-call | tf_op jit(solution)/shard_map/subspace/pallas_call | solution.py:22
  23.2 0.0 copy-start.2
  23.2 1.0 %modes.1 = (bf16[5,16,3072]{2,1,0:T(8,128)(2,1)S(1)}, bf16[5,16,3072]{2,1,0:T(8,128)(2,1)S(1)}, bf16[5,16,1920]{2,1,0:T(8,128)(2,1)S(1)}, bf16[5,16,1920]{2,1,0:T(8,128)(2,1)S(1)}) custom-call(bf16[4,16,128]{2,1,0:T(8,128)(2,1)S(1)} %get-tuple-element.30.left_ref, bf16[5,128,3072]{2,1,0:T(8,128)(2,1)S(1)} %get-tuple-element.31.x_ref), custom_call_target="tpu_custom_call" | custom-call | tf_op jit(solution)/shard_map/modes/pallas_call | solution.py:22
  24.2 0.0 collective-permute-done.4.refs_0_
  24.2 2.9 %collective-permute-done.5.refs_1_ = bf16[5,32,1152]{2,1,0:T(8,128)(2,1)S(1)} collective-permute-done((bf16[5,32,1152]{2,1,0:T(8,128)(2,1)S(1)}, bf16[5,32,1152]{2,1,0:T(8,128)(2,1)S(1)}, u32[]{:S(2)}, u32[]{:S(2)}) %collective-permute-start.5) | collective-permute-done | bytes 368672 | tf_op jit(solution)/shard_map/ppermute | solution.py:296
  27.2 0.0 collective-permute-start.6
  27.2 1.5 %collective-permute-start.7 = (bf16[5,16,1920]{2,1,0:T(8,128)(2,1)S(1)}, bf16[5,16,1920]{2,1,0:T(8,128)(2,1)S(1)}, u32[]{:S(2)}, u32[]{:S(2)}) collective-permute-start(bf16[5,16,1920]{2,1,0:T(8,128)(2,1)S(1)} %get-tuple-element.41), channel_id=1, source_target_pairs={{0,2},{1,3},{2,0},{3,1},{4,6},{5,7},{6,4},{7,5},{8,10},{9,11},{10,... | collective-permute-start | bytes 921608 | tf_op jit(solution)/shard_map/ppermute | solution.py:296
  28.6 0.7 %collective-permute-start.8 = (bf16[5,16,1920]{2,1,0:T(8,128)(2,1)S(1)}, bf16[5,16,1920]{2,1,0:T(8,128)(2,1)S(1)}, u32[]{:S(2)}, u32[]{:S(2)}) collective-permute-start(bf16[5,16,1920]{2,1,0:T(8,128)(2,1)S(1)} %get-tuple-element.42), channel_id=1, source_target_pairs={{0,3},{1,2},{2,1},{3,0},{4,7},{5,6},{6,5},{7,4},{8,11},{9,10},{10,... | collective-permute-start | bytes 921608 | tf_op jit(solution)/shard_map/ppermute | solution.py:296
  29.3 0.0 copy-done.2
  29.3 1.5 %small.1 = (f32[16,32]{1,0:T(8,128)}, f32[1,16,16]{2,1,0:T(8,128)}) custom-call(s32[1]{0:T(128)} %bitcast.me_ref, s32[4]{0:T(128)S(1)} %copy-done.2, f32[128,128]{1,0:T(8,128)S(1)} %get-tuple-element.43.gram_ref, s32[1,128]{1,0:T(1,128)S(1)} %bitcast.11, f32[16,128]{1,0:T(8,128)S(1)} %get-tuple-element.44.basis_ref), custom_call_target="tpu_custom_call" | custom-call | tf_op jit(solution)/shard_map/small/pallas_call | solution.py:22
  30.8 0.0 collective-permute-done.6.near2_ref
  30.8 1.1 %owner.1.out_in_ref = bf16[5,16,12288]{2,1,0:T(8,128)(2,1)} custom-call(s32[1]{0:T(128)} %bitcast.me_ref, bf16[16,32]{1,0:T(8,128)(2,1)S(1)} %get-tuple-element.29.own_ref, bf16[5,16,3072]{2,1,0:T(8,128)(2,1)S(1)} %get-tuple-element.32.near_ref, bf16[5,16,3072]{2,1,0:T(8,128)(2,1)S(1)} %collective-permute-done.6.near2_ref, ...), custom_call_target="tpu_custom_call" | custom-call | tf_op jit(solution)/shard_map/owner/pallas_call | solution.py:22
  31.9 3.6 %collective-permute-done.7.piece_ref = bf16[5,16,1920]{2,1,0:T(8,128)(2,1)S(1)} collective-permute-done((bf16[5,16,1920]{2,1,0:T(8,128)(2,1)S(1)}, bf16[5,16,1920]{2,1,0:T(8,128)(2,1)S(1)}, u32[]{:S(2)}, u32[]{:S(2)}) %collective-permute-start.7) | collective-permute-done | bytes 307232 | tf_op jit(solution)/shard_map/ppermute | solution.py:296
  35.5 0.7 %place.2.out_in_ref = bf16[5,16,12288]{2,1,0:T(8,128)(2,1)} custom-call(s32[1]{0:T(128)} %bitcast.me_ref, bf16[5,16,12288]{2,1,0:T(8,128)(2,1)} %owner.1.out_in_ref, bf16[5,16,1920]{2,1,0:T(8,128)(2,1)S(1)} %collective-permute-done.7.piece_ref), custom_call_target="tpu_custom_call", output_to_operand_aliasing={{}: (1, {})} | custom-call | tf_op jit(solution)/shard_map/place/pallas_call | solution.py:22
  36.2 6.5 %collective-permute-done.8.piece_ref = bf16[5,16,1920]{2,1,0:T(8,128)(2,1)S(1)} collective-permute-done((bf16[5,16,1920]{2,1,0:T(8,128)(2,1)S(1)}, bf16[5,16,1920]{2,1,0:T(8,128)(2,1)S(1)}, u32[]{:S(2)}, u32[]{:S(2)}) %collective-permute-start.8) | collective-permute-done | bytes 307232 | tf_op jit(solution)/shard_map/ppermute | solution.py:296
  42.8 0.7 %place.3 = bf16[5,16,12288]{2,1,0:T(8,128)(2,1)} custom-call(s32[1]{0:T(128)} %bitcast.me_ref, bf16[5,16,12288]{2,1,0:T(8,128)(2,1)} %place.2.out_in_ref, bf16[5,16,1920]{2,1,0:T(8,128)(2,1)S(1)} %collective-permute-done.8.piece_ref), custom_call_target="tpu_custom_call", output_to_operand_aliasing={{}: (1, {})} | custom-call | tf_op jit(solution)/shard_map/place/pallas_call | solution.py:22
  (3 shorter events, 0.0 us)
Async XLA Ops:
  0.6 0.7 %copy-start.1 = (s32[128]{0:T(128)S(1)}, s32[128]{0:T(128)}, u32[]{:S(2)}) copy-start(s32[128]{0:T(128)} %param.5) | copy-start | bytes 1540
  1.3 20.4 %copy-start = (f32[128,16]{0,1:T(8,128)S(1)}, f32[128,16]{0,1:T(8,128)}, u32[]{:S(2)}) copy-start(f32[128,16]{0,1:T(8,128)} %param.6) | copy-start | bytes 24580
  5.2 3.8 %collective-permute-start = (f32[128,128]{1,0:T(8,128)S(1)}, f32[128,128]{1,0:T(8,128)S(1)}, u32[]{:S(2)}, u32[]{:S(2)}) collective-permute-start(f32[128,128]{1,0:T(8,128)S(1)} %get-tuple-element.25), channel_id=1, source_target_pairs={{0,2},{1,3},{2,0},{3,1},{4,6},{5,7},{6,4},{7,5},{8,10},{9,11},{10,... | collective-permute-start | bytes 196616 | tf_op jit(solution)/shard_map/ppermute | solution.py:296
  9.0 15.3 %collective-permute-start.4 = (bf16[5,32,1152]{2,1,0:T(8,128)(2,1)S(1)}, bf16[5,32,1152]{2,1,0:T(8,128)(2,1)S(1)}, u32[]{:S(2)}, u32[]{:S(2)}) collective-permute-start(bf16[5,32,1152]{2,1,0:T(8,128)(2,1)S(1)} %get-tuple-element.35), channel_id=1, source_target_pairs={{0,2},{1,3},{2,0},{3,1},{4,6},{5,7},{6,4},{7,5},{8,10},{9,11},{10,... | collective-permute-start | bytes 1105928 | tf_op jit(solution)/shard_map/ppermute | solution.py:296
  10.4 16.8 %collective-permute-start.5 = (bf16[5,32,1152]{2,1,0:T(8,128)(2,1)S(1)}, bf16[5,32,1152]{2,1,0:T(8,128)(2,1)S(1)}, u32[]{:S(2)}, u32[]{:S(2)}) collective-permute-start(bf16[5,32,1152]{2,1,0:T(8,128)(2,1)S(1)} %get-tuple-element.36), channel_id=1, source_target_pairs={{0,3},{1,2},{2,1},{3,0},{4,7},{5,6},{6,5},{7,4},{8,11},{9,10},{10,... | collective-permute-start | bytes 1105928 | tf_op jit(solution)/shard_map/ppermute | solution.py:296
  12.2 1.3 %collective-permute-start.1 = (f32[128,128]{1,0:T(8,128)S(1)}, f32[128,128]{1,0:T(8,128)S(1)}, u32[]{:S(2)}, u32[]{:S(2)}) collective-permute-start(f32[128,128]{1,0:T(8,128)S(1)} %add.9), channel_id=1, source_target_pairs={{0,1},{1,0},{2,3},{3,2},{4,5},{5,4},{6,7},{7,6},{8,9},{9,8},{10,11... | collective-permute-start | bytes 196616 | tf_op jit(solution)/shard_map/ppermute | solution.py:296
  13.5 4.1 %collective-permute-start.2 = (f32[128,128]{1,0:T(8,128)S(1)}, f32[128,128]{1,0:T(8,128)S(1)}, u32[]{:S(2)}, u32[]{:S(2)}) collective-permute-start(f32[128,128]{1,0:T(8,128)S(1)} %add.10), channel_id=1, source_target_pairs={{0,4},{4,0},{8,12},{12,8},{1,5},{5,1},{9,13},{13,9},{2,6},{6,2},{1... | collective-permute-start | bytes 196616 | tf_op jit(solution)/shard_map/ppermute | solution.py:296
  17.6 4.1 %collective-permute-start.3 = (f32[128,128]{1,0:T(8,128)S(1)}, f32[128,128]{1,0:T(8,128)S(1)}, u32[]{:S(2)}, u32[]{:S(2)}) collective-permute-start(f32[128,128]{1,0:T(8,128)S(1)} %add.11.first_ref), channel_id=1, source_target_pairs={{0,8},{4,12},{8,0},{12,4},{1,9},{5,13},{9,1},{13,5},{2,10},{6,14},... | collective-permute-start | bytes 196616 | tf_op jit(solution)/shard_map/ppermute | solution.py:296
  23.2 6.1 %copy-start.2 = (s32[4]{0:T(128)S(1)}, s32[4]{0:T(128)}, u32[]{:S(2)}) copy-start(s32[4]{0:T(128)} %successor_ref.1) | copy-start | bytes 52
  27.2 3.6 %collective-permute-start.6 = (bf16[5,16,3072]{2,1,0:T(8,128)(2,1)S(1)}, bf16[5,16,3072]{2,1,0:T(8,128)(2,1)S(1)}, u32[]{:S(2)}, u32[]{:S(2)}) collective-permute-start(bf16[5,16,3072]{2,1,0:T(8,128)(2,1)S(1)} %get-tuple-element.38), channel_id=1, source_target_pairs={{0,1},{1,0},{2,3},{3,2},{4,5},{5,4},{6,7},{7,6},{8,9},{9,8},{10,11... | collective-permute-start | bytes 1474568 | tf_op jit(solution)/shard_map/ppermute | solution.py:296
  27.2 8.3 %collective-permute-start.7 = (bf16[5,16,1920]{2,1,0:T(8,128)(2,1)S(1)}, bf16[5,16,1920]{2,1,0:T(8,128)(2,1)S(1)}, u32[]{:S(2)}, u32[]{:S(2)}) collective-permute-start(bf16[5,16,1920]{2,1,0:T(8,128)(2,1)S(1)} %get-tuple-element.41), channel_id=1, source_target_pairs={{0,2},{1,3},{2,0},{3,1},{4,6},{5,7},{6,4},{7,5},{8,10},{9,11},{10,... | collective-permute-start | bytes 921608 | tf_op jit(solution)/shard_map/ppermute | solution.py:296
  28.6 14.1 %collective-permute-start.8 = (bf16[5,16,1920]{2,1,0:T(8,128)(2,1)S(1)}, bf16[5,16,1920]{2,1,0:T(8,128)(2,1)S(1)}, u32[]{:S(2)}, u32[]{:S(2)}) collective-permute-start(bf16[5,16,1920]{2,1,0:T(8,128)(2,1)S(1)} %get-tuple-element.42), channel_id=1, source_target_pairs={{0,3},{1,2},{2,1},{3,0},{4,7},{5,6},{6,5},{7,4},{8,11},{9,10},{10,... | collective-permute-start | bytes 921608 | tf_op jit(solution)/shard_map/ppermute | solution.py:296

commit v3 on v2

--- a/solution.py
+++ b/solution.py
@@ -15,10 +15,10 @@
 ANYWHERE = pl.BlockSpec(memory_space=pl.ANY)
 LIMIT = 20 * 1024 * 1024
 LARGE = 46 * 1024 * 1024
-EARLY = 1152
-
-
-def call(body, name, in_specs, outs, *operands, flops=0, scratch=(), aliases=None, out_specs=None, limit=LIMIT):
+EARLY = 1024
+
+
+def call(body, name, in_specs, outs, *operands, scratch=(), aliases=None, out_specs=None, limit=LIMIT):
     return pl.pallas_call(
         body,
         in_specs=in_specs,
@@ -32,6 +32,25 @@
     )(*operands)
 
 
+def load_body(after_ref, x_hbm, x_ref, sem):
+    copy = pltpu.make_async_copy(x_hbm, x_ref, sem)
+    copy.start()
+    copy.wait()
+
+
+def load(after, x):
+    return call(
+        load_body,
+        "load",
+        [ANYWHERE, ANYWHERE],
+        [pltpu.VMEM(x.shape, x.dtype)],
+        after,
+        x,
+        scratch=[pltpu.SemaphoreType.DMA],
+        out_specs=[ANYWHERE],
+    )[0]
+
+
 def same_cluster(row_labels):
     count = row_labels.shape[1]
     wide = jnp.broadcast_to(row_labels.astype(jnp.float32), (count, count))
@@ -48,44 +67,50 @@
     return jnp.where((rank == wanted) & (row_labels == cluster), 1.0, 0.0).astype(jnp.bfloat16)
 
 
-def gram_body(me_ref, row_ref, x_hbm, gram_ref, x_ref, *refs, far):
+def gram_body(row_hbm, x_hbm, gram_ref, *refs, far):
     pick_refs = refs[: len(far)]
-    sems = refs[len(far)]
-    variables = x_ref.shape[0]
-    copies = [pltpu.make_async_copy(x_hbm.at[v], x_ref.at[v], sems.at[v]) for v in range(variables)]
-    for copy in copies:
-        copy.start()
+    x_ref, row_ref, sems = refs[len(far) :]
+    row_copy = pltpu.make_async_copy(row_hbm, row_ref, sems.at[0])
+    x_copy = pltpu.make_async_copy(x_hbm, x_ref, sems.at[1])
+    row_copy.start()
+    x_copy.start()
+    row_copy.wait()
+    me = lax.axis_index("clus")
     row_labels = row_ref[...]
     same = same_cluster(row_labels)
     slots, early = pick_refs[0].shape[1:]
     choice = jnp.concatenate(
-        [slot_choice(row_labels, same, me_ref[0] ^ k, slots) for k in far], axis=0
-    )
+        [slot_choice(row_labels, same, me ^ k, slots) for k in far], axis=0
+    )
+    x_copy.wait()
     total = None
-    for v in range(variables):
-        copies[v].wait()
+    for v in range(x_ref.shape[0]):
         x = x_ref[v]
         part = lax.dot_general(x, x, (((1,), (1,)), ((), ())), preferred_element_type=jnp.float32)
         total = part if total is None else total + part
-        rows = jnp.dot(choice, x[:, :early], preferred_element_type=jnp.float32)
+    gram_ref[...] = total
+    for v in range(x_ref.shape[0]):
+        rows = jnp.dot(choice, x_ref[v, :, :early], preferred_element_type=jnp.float32)
         rows = rows.astype(jnp.bfloat16)
         for i, pick_ref in enumerate(pick_refs):
             pick_ref[v] = rows[i * slots : (i + 1) * slots]
-    gram_ref[...] = total
-
-
-def partial_gram(me, labels, x, far, slots, early):
+
+
+def partial_gram(labels, x, far, slots, early):
     variables, count, cells = x.shape
     picked = pltpu.VMEM((variables, slots, early), jnp.bfloat16)
     return call(
         functools.partial(gram_body, far=far),
         "gram",
-        [IN_SMEM, IN_VMEM, ANYWHERE],
-        [pltpu.VMEM((count, count), jnp.float32), pltpu.VMEM(x.shape, x.dtype)] + [picked for _ in far],
-        me,
+        [ANYWHERE, ANYWHERE],
+        [pltpu.VMEM((count, count), jnp.float32)] + [picked for _ in far],
         labels,
         x,
-        scratch=[pltpu.SemaphoreType.DMA((variables,))],
+        scratch=[
+            pltpu.VMEM(x.shape, x.dtype),
+            pltpu.VMEM(labels.shape, labels.dtype),
+            pltpu.SemaphoreType.DMA((2,)),
+        ],
         limit=LARGE,
     )
 
@@ -109,9 +134,8 @@
 
 
 def subspace_body(
-    me_ref, first_ref, second_ref, row_ref, start_ref, gram_ref, basis_ref, left_ref, own_ref, *, total_rows
+    first_ref, second_ref, row_ref, start_ref, gram_ref, basis_ref, near_ref, left_ref, own_ref, *, total_rows
 ):
-    clusters = left_ref.shape[0]
     row_labels = row_ref[...]
     together = same_cluster(row_labels)
     gram = (first_ref[...] + second_ref[...]) * (1.0 / total_rows)
@@ -126,28 +150,30 @@
         basis = orthonormal(image, same)
     basis_ref[...] = basis
     rounded = basis.astype(jnp.bfloat16).astype(jnp.float32)
-    me = me_ref[0]
-    for k in range(clusters):
-        left_ref[k] = jnp.where(row_labels == (me ^ k), rounded, 0.0).astype(jnp.bfloat16)
+    me = lax.axis_index("clus")
+    for k in range(2):
+        near_ref[k] = jnp.where(row_labels == (me ^ k), rounded, 0.0).astype(jnp.bfloat16)
+    for k in range(left_ref.shape[0]):
+        left_ref[k] = jnp.where(row_labels == (me ^ (k + 2)), rounded, 0.0).astype(jnp.bfloat16)
     choice = slot_choice(row_labels, together, me, own_ref.shape[1])
     own_ref[...] = lax.dot_general(
         rounded.astype(jnp.bfloat16), choice, (((1,), (1,)), ((), ())), preferred_element_type=jnp.float32
     ).astype(jnp.bfloat16)
 
 
-def subspace(me, first, second, labels, start, total_rows, clusters, slots):
+def subspace(first, second, labels, start, total_rows, clusters, slots):
     modes, count = start.shape
     return call(
         functools.partial(subspace_body, total_rows=total_rows),
         "subspace",
-        [IN_SMEM, IN_VMEM, IN_VMEM, IN_VMEM, IN_VMEM],
+        [IN_VMEM, IN_VMEM, IN_VMEM, IN_VMEM],
         [
             pltpu.VMEM((count, count), jnp.float32),
             pltpu.VMEM((modes, count), jnp.float32),
-            pltpu.VMEM((clusters, modes, count), jnp.bfloat16),
+            pltpu.VMEM((2, modes, count), jnp.bfloat16),
+            pltpu.VMEM((clusters - 2, modes, count), jnp.bfloat16),
             pltpu.VMEM((modes, slots), jnp.bfloat16),
         ],
-        me,
         first,
         second,
         labels,
@@ -189,34 +215,25 @@
     )
 
 
-def modes_body(left_ref, x_ref, *out_refs):
-    clusters, modes, count = left_ref.shape
-    near = left_ref[:2].reshape(2 * modes, count)
-    left = left_ref[2:].reshape((clusters - 2) * modes, count)
+def modes_body(near_ref, far_ref, x_ref, *out_refs):
+    modes, count = near_ref.shape[1:]
     begin = x_ref.shape[2] - out_refs[2].shape[2]
     for v in range(x_ref.shape[0]):
-        product = jnp.dot(left, x_ref[v, :, begin:], preferred_element_type=jnp.float32)
-        product = product.astype(jnp.bfloat16)
-        for i, out_ref in enumerate(out_refs[2:]):
-            out_ref[v] = product[i * modes : (i + 1) * modes]
-        product = jnp.dot(near, x_ref[v], preferred_element_type=jnp.float32)
-        product = product.astype(jnp.bfloat16)
-        for i, out_ref in enumerate(out_refs[:2]):
-            out_ref[v] = product[i * modes : (i + 1) * modes]
-
-
-def local_modes(left, x, begin):
+        for left_ref, refs, at in ((far_ref, out_refs[2:], begin), (near_ref, out_refs[:2], 0)):
+            left = left_ref[...].reshape(len(refs) * modes, count)
+            product = jnp.dot(left, x_ref[v, :, at:], preferred_element_type=jnp.float32)
+            product = product.astype(jnp.bfloat16)
+            for i, out_ref in enumerate(refs):
+                out_ref[v] = product[i * modes : (i + 1) * modes]
+
+
+def local_modes(near, left, x, begin):
     variables, count, cells = x.shape
-    clusters, modes, _ = left.shape
-    near = pltpu.VMEM((variables, modes, cells), jnp.bfloat16)
+    number, modes, _ = left.shape
+    whole = pltpu.VMEM((variables, modes, cells), jnp.bfloat16)
     late = pltpu.VMEM((variables, modes, cells - begin), jnp.bfloat16)
     return call(
-        modes_body,
-        "modes",
-        [IN_VMEM, IN_VMEM],
-        [near, near] + [late] * (clusters - 2),
-        left,
-        x,
+        modes_body, "modes", [IN_VMEM] * 3, [whole, whole] + [late] * number, near, left, x
     )
 
 
@@ -305,24 +322,25 @@
     slots = CAP * clusters
     far = list(range(2, clusters))
     labels = labels[None, :]
+    labels_hbm = pltpu.with_memory_space_constraint(labels, pltpu.HBM)
     x = jnp.transpose(snapshots, (1, 0, 2))
-    gram, x, *picked = partial_gram(me, labels, x, far, slots, EARLY)
-    rounds = [("clus", 1 << b) for b in range(1, clusters.bit_length() - 1)]
-    links = len(rounds)
-    rounds += [("clus", 1)]
-    rounds += [("space", 1 << b) for b in range(space.bit_length() - 1)]
-    other = None
-    for step, (axis, offset) in enumerate(rounds):
-        if other is not None:
+    x_hbm = pltpu.with_memory_space_constraint(x, pltpu.HBM)
+    gram, *picked = partial_gram(labels_hbm, x_hbm, far, slots, EARLY)
+    terms = [gram] + [swap(gram, "clus", k) for k in range(1, clusters)]
+    terms[1], *picked = lax.optimization_barrier((terms[1], *picked))
+    rows = [swap(piece, "clus", k) for piece, k in zip(picked, far)]
+    while len(terms) > 1:
+        terms = [a + b for a, b in zip(terms[::2], terms[1::2])]
+    gram = terms[0]
+    x = load(gram, x_hbm)
+    for b in range(space.bit_length() - 1):
+        if b > 0:
             gram = gram + other
-        other = swap(gram, axis, offset)
-        if step == links - 1:
-            other, *picked = lax.optimization_barrier((other, *picked))
-            rows = [swap(piece, "clus", k) for piece, k in zip(picked, far)]
-    gram, basis, left, own = subspace(
-        me, gram, other, labels, start.T, total_rows, clusters, slots
-    )
-    own_piece, sibling, *late = local_modes(left, x, EARLY)
+        other = swap(gram, "space", 1 << b)
+    gram, basis, near, left, own = subspace(
+        gram, other, labels, start.T, total_rows, clusters, slots
+    )
+    own_piece, sibling, *late = local_modes(near, left, x, EARLY)
     both = lax.optimization_barrier((*late, *rows, sibling))
     late, rows, sibling = both[: len(far)], both[len(far) : -1], both[-1]
     late = [swap(piece, "clus", k) for piece, k in zip(late, far)]

time: 43.7 us -> 42.2 us (0.966)
  Pallas kernels: 10.5 us -> 12.2 us
  waiting for transfers between devices: 19.5 us -> 18 us
  starting transfers between devices: 12.1 us -> 11.1 us
  local copies, waits for them, and re-layouts: 0.66 us -> 0.02 us
    pallas_call x7 -> x8, Pallas kernels: 10.5 us -> 12.2 us  [call(): pl.pallas_call(body, in_specs=in_specs, out_specs=out_specs or [IN_VMEM]...]
    ppermute x9 -> x10, waiting for transfers between devices: 19.5 us -> 18 us  [swap(): return lax.ppermute(x, axis, [(i, i ^ offset) for i in range(size)])]
    ppermute x9 -> x10, starting transfers between devices: 12.1 us -> 11.1 us  [swap(): return lax.ppermute(x, axis, [(i, i ^ offset) for i in range(size)])]
    unnamed x6, local copies, waits for them, and re-layouts: 0.66 us -> 0.02 us
  transfers between devices with their start and end apart: 9 -> 10, of which waited for: 7 -> 6; matrix products, arithmetic and copies ran while one was open for 0% -> 0% of each run, Pallas kernels for 13% -> 19%
where the time goes in v3:
time: 42.2 us; the launch traced here: 42 us
  waiting for transfers between devices  18 us (43%)
  Pallas kernels  12.2 us (29%)
  starting transfers between devices  11.1 us (26%)
  between operations  0.73 us (2%)
    ppermute x10, waiting for transfers between devices, swap(): return lax.ppermute(x, axis, [(i, i ^ offset) for i in range(size)])  18 us
    pallas_call x8, Pallas kernels, call(): pl.pallas_call(body, in_specs=in_specs, out_specs=out_specs or [IN_VMEM]...  12.2 us
    ppermute x10, starting transfers between devices, swap(): return lax.ppermute(x, axis, [(i, i ^ offset) for i in range(size)])  11.1 us
  transfers between devices with their start and end apart: 10, of which 6 were waited for; matrix products, arithmetic and copies ran while one was open for 0% of the time, Pallas kernels for 19%

profile of v3, /device:TPU:1, one launch (start us, length us, event | category | flops | bytes accessed | tf_op | source)
XLA Modules:
  0.0 42.0 jit_solution(9599979957562324980)
XLA Ops:
  0.6 3.5 %gram.1 = (f32[128,128]{1,0:T(8,128)S(1)}, bf16[5,32,1024]{2,1,0:T(8,128)(2,1)S(1)}, bf16[5,32,1024]{2,1,0:T(8,128)(2,1)S(1)}) custom-call(s32[1,128]{1,0:T(1,128)} %bitcast.9, bf16[5,128,3072]{2,1,0:T(8,128)(2,1)} %bitcast.13), custom_call_target="tpu_custom_call" | custom-call | tf_op jit(solution)/shard_map/gram/pallas_call | solution.py:22
  4.1 0.1 collective-permute-start
  4.3 2.6 %collective-permute-start.2 = (f32[128,128]{1,0:T(8,128)S(1)}, f32[128,128]{1,0:T(8,128)S(1)}, u32[]{:S(2)}, u32[]{:S(2)}) collective-permute-start(f32[128,128]{1,0:T(8,128)S(1)} %get-tuple-element.25), channel_id=1, source_target_pairs={{0,3},{1,2},{2,1},{3,0},{4,7},{5,6},{6,5},{7,4},{8,11},{9,10},{10,... | collective-permute-start | bytes 196616 | tf_op jit(solution)/shard_map/ppermute | solution.py:313
  6.9 0.1 collective-permute-start.1
  7.0 0.0 collective-permute-done
  7.0 1.4 %collective-permute-start.5 = (bf16[5,32,1024]{2,1,0:T(8,128)(2,1)S(1)}, bf16[5,32,1024]{2,1,0:T(8,128)(2,1)S(1)}, u32[]{:S(2)}, u32[]{:S(2)}) collective-permute-start(bf16[5,32,1024]{2,1,0:T(8,128)(2,1)S(1)} %get-tuple-element.35), channel_id=1, source_target_pairs={{0,2},{1,3},{2,0},{3,1},{4,6},{5,7},{6,4},{7,5},{8,10},{9,11},{10,... | collective-permute-start | bytes 983048 | tf_op jit(solution)/shard_map/ppermute | solution.py:313
  8.4 0.7 %collective-permute-start.6 = (bf16[5,32,1024]{2,1,0:T(8,128)(2,1)S(1)}, bf16[5,32,1024]{2,1,0:T(8,128)(2,1)S(1)}, u32[]{:S(2)}, u32[]{:S(2)}) collective-permute-start(bf16[5,32,1024]{2,1,0:T(8,128)(2,1)S(1)} %get-tuple-element.36), channel_id=1, source_target_pairs={{0,3},{1,2},{2,1},{3,0},{4,7},{5,6},{6,5},{7,4},{8,11},{9,10},{10,... | collective-permute-start | bytes 983048 | tf_op jit(solution)/shard_map/ppermute | solution.py:313
  9.0 0.3 collective-permute-done.2
  9.3 0.7 %collective-permute-done.1 = f32[128,128]{1,0:T(8,128)S(1)} collective-permute-done((f32[128,128]{1,0:T(8,128)S(1)}, f32[128,128]{1,0:T(8,128)S(1)}, u32[]{:S(2)}, u32[]{:S(2)}) %collective-permute-start.1) | collective-permute-done | bytes 65568 | tf_op jit(solution)/shard_map/ppermute | solution.py:313
  10.0 1.6 %collective-permute-start.3 = (f32[128,128]{1,0:T(8,128)S(1)}, f32[128,128]{1,0:T(8,128)S(1)}, u32[]{:S(2)}, u32[]{:S(2)}) collective-permute-start(f32[128,128]{1,0:T(8,128)S(1)} %add_add_fusion.after_ref), channel_id=1, source_target_pairs={{0,4},{4,0},{8,12},{12,8},{1,5},{5,1},{9,13},{13,9},{2,6},{6,2},{1... | collective-permute-start | bytes 196616 | tf_op jit(solution)/shard_map/ppermute | solution.py:313
  11.6 2.0 %collective-permute-done.3 = f32[128,128]{1,0:T(8,128)S(1)} collective-permute-done((f32[128,128]{1,0:T(8,128)S(1)}, f32[128,128]{1,0:T(8,128)S(1)}, u32[]{:S(2)}, u32[]{:S(2)}) %collective-permute-start.3) | collective-permute-done | bytes 65568 | tf_op jit(solution)/shard_map/ppermute | solution.py:313
  13.5 0.0 copy-start
  13.6 0.0 copy-start.1
  13.6 2.5 %collective-permute-start.4 = (f32[128,128]{1,0:T(8,128)S(1)}, f32[128,128]{1,0:T(8,128)S(1)}, u32[]{:S(2)}, u32[]{:S(2)}) collective-permute-start(f32[128,128]{1,0:T(8,128)S(1)} %add.15.first_ref), channel_id=1, source_target_pairs={{0,8},{4,12},{8,0},{12,4},{1,9},{5,13},{9,1},{13,5},{2,10},{6,14},... | collective-permute-start | bytes 196616 | tf_op jit(solution)/shard_map/ppermute | solution.py:313
  16.1 2.1 %load.1.x_ref = bf16[5,128,3072]{2,1,0:T(8,128)(2,1)S(1)} custom-call(f32[128,128]{1,0:T(8,128)S(1)} %add_add_fusion.after_ref, bf16[5,128,3072]{2,1,0:T(8,128)(2,1)} %bitcast.14), custom_call_target="tpu_custom_call" | custom-call | tf_op jit(solution)/shard_map/load/pallas_call | solution.py:22
  18.2 0.0 collective-permute-done.4.second_ref
  18.2 0.0 copy-done
  18.2 0.0 copy-done.1
  18.3 1.5 %subspace.1 = (f32[128,128]{1,0:T(8,128)S(1)}, f32[16,128]{1,0:T(8,128)S(1)}, bf16[2,16,128]{2,1,0:T(8,128)(2,1)S(1)}, bf16[2,16,128]{2,1,0:T(8,128)(2,1)S(1)}, bf16[16,32]{1,0:T(8,128)(2,1)S(1)}) custom-call(f32[128,128]{1,0:T(8,128)S(1)} %add.15.first_ref, f32[128,128]{1,0:T(8,128)S(1)} %collective-permute-done.4.second_ref, s32[1,128]{1,0:T(1,128)S(1)} %bitcast.10, ...), custom_call_target="tpu_custom_call" | custom-call | tf_op jit(solution)/shard_map/subspace/pallas_call | solution.py:22
  19.8 0.0 copy-start.2
  19.8 1.0 %modes.1 = (bf16[5,16,3072]{2,1,0:T(8,128)(2,1)S(1)}, bf16[5,16,3072]{2,1,0:T(8,128)(2,1)S(1)}, bf16[5,16,2048]{2,1,0:T(8,128)(2,1)S(1)}, bf16[5,16,2048]{2,1,0:T(8,128)(2,1)S(1)}) custom-call(bf16[2,16,128]{2,1,0:T(8,128)(2,1)S(1)} %get-tuple-element.30.near_ref, bf16[2,16,128]{2,1,0:T(8,128)(2,1)S(1)} %get-tuple-element.31.far_ref, ...), custom_call_target="tpu_custom_call" | custom-call | tf_op jit(solution)/shard_map/modes/pallas_call | solution.py:22
  20.8 0.0 collective-permute-done.5.refs_0_
  20.8 4.0 %collective-permute-done.6.refs_1_ = bf16[5,32,1024]{2,1,0:T(8,128)(2,1)S(1)} collective-permute-done((bf16[5,32,1024]{2,1,0:T(8,128)(2,1)S(1)}, bf16[5,32,1024]{2,1,0:T(8,128)(2,1)S(1)}, u32[]{:S(2)}, u32[]{:S(2)}) %collective-permute-start.6) | collective-permute-done | bytes 327712 | tf_op jit(solution)/shard_map/ppermute | solution.py:313
  24.7 0.0 collective-permute-start.7
  24.7 1.5 %collective-permute-start.8 = (bf16[5,16,2048]{2,1,0:T(8,128)(2,1)S(1)}, bf16[5,16,2048]{2,1,0:T(8,128)(2,1)S(1)}, u32[]{:S(2)}, u32[]{:S(2)}) collective-permute-start(bf16[5,16,2048]{2,1,0:T(8,128)(2,1)S(1)} %get-tuple-element.41), channel_id=1, source_target_pairs={{0,2},{1,3},{2,0},{3,1},{4,6},{5,7},{6,4},{7,5},{8,10},{9,11},{10,... | collective-permute-start | bytes 983048 | tf_op jit(solution)/shard_map/ppermute | solution.py:313
  26.3 0.6 %collective-permute-start.9 = (bf16[5,16,2048]{2,1,0:T(8,128)(2,1)S(1)}, bf16[5,16,2048]{2,1,0:T(8,128)(2,1)S(1)}, u32[]{:S(2)}, u32[]{:S(2)}) collective-permute-start(bf16[5,16,2048]{2,1,0:T(8,128)(2,1)S(1)} %get-tuple-element.42), channel_id=1, source_target_pairs={{0,3},{1,2},{2,1},{3,0},{4,7},{5,6},{6,5},{7,4},{8,11},{9,10},{10,... | collective-permute-start | bytes 983048 | tf_op jit(solution)/shard_map/ppermute | solution.py:313
  26.9 0.0 copy-done.2
  26.9 1.5 %small.1 = (f32[16,32]{1,0:T(8,128)}, f32[1,16,16]{2,1,0:T(8,128)}) custom-call(s32[1]{0:T(128)} %bitcast.me_ref, s32[4]{0:T(128)S(1)} %copy-done.2, f32[128,128]{1,0:T(8,128)S(1)} %get-tuple-element.43.gram_ref, s32[1,128]{1,0:T(1,128)S(1)} %bitcast.11, f32[16,128]{1,0:T(8,128)S(1)} %get-tuple-element.44.basis_ref), custom_call_target="tpu_custom_call" | custom-call | tf_op jit(solution)/shard_map/small/pallas_call | solution.py:22
  28.4 0.0 collective-permute-done.7.near2_ref
  28.4 1.1 %owner.1.out_in_ref = bf16[5,16,12288]{2,1,0:T(8,128)(2,1)} custom-call(s32[1]{0:T(128)} %bitcast.me_ref, bf16[16,32]{1,0:T(8,128)(2,1)S(1)} %get-tuple-element.29.own_ref, bf16[5,16,3072]{2,1,0:T(8,128)(2,1)S(1)} %get-tuple-element.32.near_ref, bf16[5,16,3072]{2,1,0:T(8,128)(2,1)S(1)} %collective-permute-done.7.near2_ref, ...), custom_call_target="tpu_custom_call" | custom-call | tf_op jit(solution)/shard_map/owner/pallas_call | solution.py:22
  29.5 4.2 %collective-permute-done.8.piece_ref = bf16[5,16,2048]{2,1,0:T(8,128)(2,1)S(1)} collective-permute-done((bf16[5,16,2048]{2,1,0:T(8,128)(2,1)S(1)}, bf16[5,16,2048]{2,1,0:T(8,128)(2,1)S(1)}, u32[]{:S(2)}, u32[]{:S(2)}) %collective-permute-start.8) | collective-permute-done | bytes 327712 | tf_op jit(solution)/shard_map/ppermute | solution.py:313
  33.6 0.7 %place.2.out_in_ref = bf16[5,16,12288]{2,1,0:T(8,128)(2,1)} custom-call(s32[1]{0:T(128)} %bitcast.me_ref, bf16[5,16,12288]{2,1,0:T(8,128)(2,1)} %owner.1.out_in_ref, bf16[5,16,2048]{2,1,0:T(8,128)(2,1)S(1)} %collective-permute-done.8.piece_ref), custom_call_target="tpu_custom_call", output_to_operand_aliasing={{}: (1, {})} | custom-call | tf_op jit(solution)/shard_map/place/pallas_call | solution.py:22
  34.4 6.9 %collective-permute-done.9.piece_ref = bf16[5,16,2048]{2,1,0:T(8,128)(2,1)S(1)} collective-permute-done((bf16[5,16,2048]{2,1,0:T(8,128)(2,1)S(1)}, bf16[5,16,2048]{2,1,0:T(8,128)(2,1)S(1)}, u32[]{:S(2)}, u32[]{:S(2)}) %collective-permute-start.9) | collective-permute-done | bytes 327712 | tf_op jit(solution)/shard_map/ppermute | solution.py:313
  41.3 0.7 %place.3 = bf16[5,16,12288]{2,1,0:T(8,128)(2,1)} custom-call(s32[1]{0:T(128)} %bitcast.me_ref, bf16[5,16,12288]{2,1,0:T(8,128)(2,1)} %place.2.out_in_ref, bf16[5,16,2048]{2,1,0:T(8,128)(2,1)S(1)} %collective-permute-done.9.piece_ref), custom_call_target="tpu_custom_call", output_to_operand_aliasing={{}: (1, {})} | custom-call | tf_op jit(solution)/shard_map/place/pallas_call | solution.py:22
  (2 shorter events, 0.0 us)
Async XLA Ops:
  4.1 2.8 %collective-permute-start = (f32[128,128]{1,0:T(8,128)S(1)}, f32[128,128]{1,0:T(8,128)S(1)}, u32[]{:S(2)}, u32[]{:S(2)}) collective-permute-start(f32[128,128]{1,0:T(8,128)S(1)} %get-tuple-element.25), channel_id=1, source_target_pairs={{0,1},{1,0},{2,3},{3,2},{4,5},{5,4},{6,7},{7,6},{8,9},{9,8},{10,11... | collective-permute-start | bytes 196616 | tf_op jit(solution)/shard_map/ppermute | solution.py:313
  4.3 5.0 %collective-permute-start.2 = (f32[128,128]{1,0:T(8,128)S(1)}, f32[128,128]{1,0:T(8,128)S(1)}, u32[]{:S(2)}, u32[]{:S(2)}) collective-permute-start(f32[128,128]{1,0:T(8,128)S(1)} %get-tuple-element.25), channel_id=1, source_target_pairs={{0,3},{1,2},{2,1},{3,0},{4,7},{5,6},{6,5},{7,4},{8,11},{9,10},{10,... | collective-permute-start | bytes 196616 | tf_op jit(solution)/shard_map/ppermute | solution.py:313
  6.9 3.1 %collective-permute-start.1 = (f32[128,128]{1,0:T(8,128)S(1)}, f32[128,128]{1,0:T(8,128)S(1)}, u32[]{:S(2)}, u32[]{:S(2)}) collective-permute-start(f32[128,128]{1,0:T(8,128)S(1)} %get-tuple-element.25), channel_id=1, source_target_pairs={{0,2},{1,3},{2,0},{3,1},{4,6},{5,7},{6,4},{7,5},{8,10},{9,11},{10,... | collective-permute-start | bytes 196616 | tf_op jit(solution)/shard_map/ppermute | solution.py:313
  7.0 13.8 %collective-permute-start.5 = (bf16[5,32,1024]{2,1,0:T(8,128)(2,1)S(1)}, bf16[5,32,1024]{2,1,0:T(8,128)(2,1)S(1)}, u32[]{:S(2)}, u32[]{:S(2)}) collective-permute-start(bf16[5,32,1024]{2,1,0:T(8,128)(2,1)S(1)} %get-tuple-element.35), channel_id=1, source_target_pairs={{0,2},{1,3},{2,0},{3,1},{4,6},{5,7},{6,4},{7,5},{8,10},{9,11},{10,... | collective-permute-start | bytes 983048 | tf_op jit(solution)/shard_map/ppermute | solution.py:313
  8.4 16.4 %collective-permute-start.6 = (bf16[5,32,1024]{2,1,0:T(8,128)(2,1)S(1)}, bf16[5,32,1024]{2,1,0:T(8,128)(2,1)S(1)}, u32[]{:S(2)}, u32[]{:S(2)}) collective-permute-start(bf16[5,32,1024]{2,1,0:T(8,128)(2,1)S(1)} %get-tuple-element.36), channel_id=1, source_target_pairs={{0,3},{1,2},{2,1},{3,0},{4,7},{5,6},{6,5},{7,4},{8,11},{9,10},{10,... | collective-permute-start | bytes 983048 | tf_op jit(solution)/shard_map/ppermute | solution.py:313
  10.0 3.5 %collective-permute-start.3 = (f32[128,128]{1,0:T(8,128)S(1)}, f32[128,128]{1,0:T(8,128)S(1)}, u32[]{:S(2)}, u32[]{:S(2)}) collective-permute-start(f32[128,128]{1,0:T(8,128)S(1)} %add_add_fusion.after_ref), channel_id=1, source_target_pairs={{0,4},{4,0},{8,12},{12,8},{1,5},{5,1},{9,13},{13,9},{2,6},{6,2},{1... | collective-permute-start | bytes 196616 | tf_op jit(solution)/shard_map/ppermute | solution.py:313
  13.5 4.7 %copy-start = (f32[128,16]{0,1:T(8,128)S(1)}, f32[128,16]{0,1:T(8,128)}, u32[]{:S(2)}) copy-start(f32[128,16]{0,1:T(8,128)} %param.6) | copy-start | bytes 24580
  13.6 4.7 %copy-start.1 = (s32[128]{0:T(128)S(1)}, s32[128]{0:T(128)}, u32[]{:S(2)}) copy-start(s32[128]{0:T(128)} %param.5) | copy-start | bytes 1540
  13.6 4.7 %collective-permute-start.4 = (f32[128,128]{1,0:T(8,128)S(1)}, f32[128,128]{1,0:T(8,128)S(1)}, u32[]{:S(2)}, u32[]{:S(2)}) collective-permute-start(f32[128,128]{1,0:T(8,128)S(1)} %add.15.first_ref), channel_id=1, source_target_pairs={{0,8},{4,12},{8,0},{12,4},{1,9},{5,13},{9,1},{13,5},{2,10},{6,14},... | collective-permute-start | bytes 196616 | tf_op jit(solution)/shard_map/ppermute | solution.py:313
  19.8 7.1 %copy-start.2 = (s32[4]{0:T(128)S(1)}, s32[4]{0:T(128)}, u32[]{:S(2)}) copy-start(s32[4]{0:T(128)} %successor_ref.1) | copy-start | bytes 52
  24.7 3.6 %collective-permute-start.7 = (bf16[5,16,3072]{2,1,0:T(8,128)(2,1)S(1)}, bf16[5,16,3072]{2,1,0:T(8,128)(2,1)S(1)}, u32[]{:S(2)}, u32[]{:S(2)}) collective-permute-start(bf16[5,16,3072]{2,1,0:T(8,128)(2,1)S(1)} %get-tuple-element.38), channel_id=1, source_target_pairs={{0,1},{1,0},{2,3},{3,2},{4,5},{5,4},{6,7},{7,6},{8,9},{9,8},{10,11... | collective-permute-start | bytes 1474568 | tf_op jit(solution)/shard_map/ppermute | solution.py:313
  24.7 8.9 %collective-permute-start.8 = (bf16[5,16,2048]{2,1,0:T(8,128)(2,1)S(1)}, bf16[5,16,2048]{2,1,0:T(8,128)(2,1)S(1)}, u32[]{:S(2)}, u32[]{:S(2)}) collective-permute-start(bf16[5,16,2048]{2,1,0:T(8,128)(2,1)S(1)} %get-tuple-element.41), channel_id=1, source_target_pairs={{0,2},{1,3},{2,0},{3,1},{4,6},{5,7},{6,4},{7,5},{8,10},{9,11},{10,... | collective-permute-start | bytes 983048 | tf_op jit(solution)/shard_map/ppermute | solution.py:313
  26.3 15.0 %collective-permute-start.9 = (bf16[5,16,2048]{2,1,0:T(8,128)(2,1)S(1)}, bf16[5,16,2048]{2,1,0:T(8,128)(2,1)S(1)}, u32[]{:S(2)}, u32[]{:S(2)}) collective-permute-start(bf16[5,16,2048]{2,1,0:T(8,128)(2,1)S(1)} %get-tuple-element.42), channel_id=1, source_target_pairs={{0,3},{1,2},{2,1},{3,0},{4,7},{5,6},{6,5},{7,4},{8,11},{9,10},{10,... | collective-permute-start | bytes 983048 | tf_op jit(solution)/shard_map/ppermute | solution.py:313

commit v4 on v3

--- a/solution.py
+++ b/solution.py
@@ -65,6 +65,29 @@
     rank = jnp.sum(jnp.where(same & earlier, 1.0, 0.0), axis=0, keepdims=True).astype(jnp.int32)
     wanted = lax.broadcasted_iota(jnp.int32, (slots, count), 0)
     return jnp.where((rank == wanted) & (row_labels == cluster), 1.0, 0.0).astype(jnp.bfloat16)
+
+
+def pack(gram):
+    count = gram.shape[0]
+    half = count // 2
+    top, bottom = gram[:half], gram[half:]
+    row = lax.broadcasted_iota(jnp.int32, top.shape, 0)
+    lane = lax.broadcasted_iota(jnp.int32, top.shape, 1)
+    top = jnp.where((lane < half) & (row < lane), pltpu.roll(bottom, half, 1), top)
+    diagonal = jnp.sum(jnp.where(lane == row + half, bottom, 0.0), axis=0, keepdims=True)
+    return jnp.concatenate([top, jnp.broadcast_to(diagonal, (8, count))], axis=0)
+
+
+def unpack(packed):
+    half = packed.shape[0] - 8
+    top = packed[:half]
+    row = lax.broadcasted_iota(jnp.int32, top.shape, 0)
+    lane = lax.broadcasted_iota(jnp.int32, top.shape, 1)
+    upper = pltpu.roll(jnp.where((lane < half) & (row < lane), top, 0.0), half, 1)
+    upper = jnp.where(lane == row + half, 0.5 * packed[half : half + 1], upper)
+    lower = jnp.where(row == lane, 0.5 * top, jnp.where((lane < half) & (row < lane), 0.0, top))
+    both = jnp.concatenate([lower, upper], axis=0)
+    return both + both.T
 
 
 def gram_body(row_hbm, x_hbm, gram_ref, *refs, far):
@@ -88,7 +111,7 @@
         x = x_ref[v]
         part = lax.dot_general(x, x, (((1,), (1,)), ((), ())), preferred_element_type=jnp.float32)
         total = part if total is None else total + part
-    gram_ref[...] = total
+    gram_ref[...] = pack(total)
     for v in range(x_ref.shape[0]):
         rows = jnp.dot(choice, x_ref[v, :, :early], preferred_element_type=jnp.float32)
         rows = rows.astype(jnp.bfloat16)
@@ -103,7 +126,7 @@
         functools.partial(gram_body, far=far),
         "gram",
         [ANYWHERE, ANYWHERE],
-        [pltpu.VMEM((count, count), jnp.float32)] + [picked for _ in far],
+        [pltpu.VMEM((count // 2 + 8, count), jnp.float32)] + [picked for _ in far],
         labels,
         x,
         scratch=[
@@ -138,7 +161,7 @@
 ):
     row_labels = row_ref[...]
     together = same_cluster(row_labels)
-    gram = (first_ref[...] + second_ref[...]) * (1.0 / total_rows)
+    gram = unpack(first_ref[...] + second_ref[...]) * (1.0 / total_rows)
     gram_ref[...] = gram
     same = together.astype(jnp.float32)
     rows = lax.broadcasted_iota(jnp.int32, gram.shape, 0)
@@ -215,29 +238,62 @@
     )
 
 
-def modes_body(near_ref, far_ref, x_ref, *out_refs):
+def modes_body(near_ref, far_ref, x_ref, *out_refs, late_parts, near_parts):
     modes, count = near_ref.shape[1:]
-    begin = x_ref.shape[2] - out_refs[2].shape[2]
+    number = far_ref.shape[0]
+    own_ref = out_refs[0]
+    sibling_refs = out_refs[1 : 1 + len(near_parts)]
+    late_refs = out_refs[1 + len(near_parts) :]
+    begin = x_ref.shape[2] - late_refs[0].shape[2]
+
+    def place_of(parts, v):
+        part = max(i for i, first in enumerate(parts) if first <= v)
+        return part, v - parts[part]
+
     for v in range(x_ref.shape[0]):
-        for left_ref, refs, at in ((far_ref, out_refs[2:], begin), (near_ref, out_refs[:2], 0)):
-            left = left_ref[...].reshape(len(refs) * modes, count)
-            product = jnp.dot(left, x_ref[v, :, at:], preferred_element_type=jnp.float32)
-            product = product.astype(jnp.bfloat16)
-            for i, out_ref in enumerate(refs):
-                out_ref[v] = product[i * modes : (i + 1) * modes]
-
-
-def local_modes(near, left, x, begin):
+        left = far_ref[...].reshape(number * modes, count)
+        product = jnp.dot(left, x_ref[v, :, begin:], preferred_element_type=jnp.float32)
+        product = product.astype(jnp.bfloat16)
+        part, at = place_of(late_parts, v)
+        for i in range(number):
+            late_refs[i * len(late_parts) + part][at] = product[i * modes : (i + 1) * modes]
+        left = near_ref[...].reshape(2 * modes, count)
+        product = jnp.dot(left, x_ref[v], preferred_element_type=jnp.float32)
+        product = product.astype(jnp.bfloat16)
+        own_ref[v] = product[:modes]
+        part, at = place_of(near_parts, v)
+        sibling_refs[part][at] = product[modes:]
+
+
+def lengths(parts, total):
+    return [b - a for a, b in zip(parts, list(parts[1:]) + [total])]
+
+
+def local_modes(near, left, x, begin, late_parts, near_parts):
     variables, count, cells = x.shape
     number, modes, _ = left.shape
-    whole = pltpu.VMEM((variables, modes, cells), jnp.bfloat16)
-    late = pltpu.VMEM((variables, modes, cells - begin), jnp.bfloat16)
-    return call(
-        modes_body, "modes", [IN_VMEM] * 3, [whole, whole] + [late] * number, near, left, x
-    )
-
-
-def owner_body(me_ref, own_ref, near_ref, near2_ref, *refs, far):
+
+    def out(length, width):
+        return pltpu.VMEM((length, modes, width), jnp.bfloat16)
+
+    sibling = [out(length, cells) for length in lengths(near_parts, variables)]
+    late = [out(length, cells - begin) for length in lengths(late_parts, variables)]
+    outs = call(
+        functools.partial(modes_body, late_parts=late_parts, near_parts=near_parts),
+        "modes",
+        [IN_VMEM] * 3,
+        [out(variables, cells)] + sibling + late * number,
+        near,
+        left,
+        x,
+    )
+    first = 1 + len(sibling)
+    return outs[0], outs[1:first], outs[first:]
+
+
+def owner_body(me_ref, own_ref, near_ref, *refs, far, near_parts):
+    sibling_refs = refs[: len(near_parts)]
+    refs = refs[len(near_parts) :]
     rows_refs = refs[: len(far)]
     out_ref = refs[len(far)]
     early_refs = refs[len(far) + 1 : 2 * len(far) + 1]
@@ -246,63 +302,70 @@
     cells = near_ref.shape[2]
     copies = []
 
-    def put(source, k):
+    def put(source, k, v):
         at = pl.multiple_of((me ^ k) * cells, 128)
-        copy = pltpu.make_async_copy(
-            source, out_ref.at[:, :, pl.ds(at, source.shape[2])], sems.at[len(copies)]
-        )
+        target = out_ref.at[pl.ds(v, source.shape[0]), :, pl.ds(at, source.shape[2])]
+        copy = pltpu.make_async_copy(source, target, sems.at[len(copies)])
         copy.start()
         copies.append(copy)
 
-    put(near_ref, 0)
-    put(near2_ref, 1)
+    put(near_ref, 0, 0)
+    for v, sibling_ref in zip(near_parts, sibling_refs):
+        put(sibling_ref, 1, v)
     own = own_ref[...]
     for k, rows_ref, early_ref in zip(far, rows_refs, early_refs):
         for v in range(rows_ref.shape[0]):
             early_ref[v] = jnp.dot(own, rows_ref[v], preferred_element_type=jnp.float32).astype(
                 jnp.bfloat16
             )
-        put(early_ref, k)
+        put(early_ref, k, 0)
     for copy in copies:
         copy.wait()
 
 
-def owner_modes(me, own, near, rows, far, clusters):
-    variables, modes, cells = near[0].shape
+def owner_modes(me, own, near, sibling, near_parts, rows, far, clusters):
+    variables, modes, cells = near.shape
     early = rows[0].shape[2]
     scratch = [pltpu.VMEM((variables, modes, early), jnp.bfloat16) for _ in far]
     return call(
-        functools.partial(owner_body, far=far),
+        functools.partial(owner_body, far=far, near_parts=near_parts),
         "owner",
-        [IN_SMEM] + [IN_VMEM] * (3 + len(rows)),
+        [IN_SMEM] + [IN_VMEM] * (2 + len(sibling) + len(rows)),
         [jax.ShapeDtypeStruct((variables, modes, clusters * cells), jnp.bfloat16)],
         me,
         own,
-        *near,
+        near,
+        *sibling,
         *rows,
-        scratch=scratch + [pltpu.SemaphoreType.DMA((2 + len(far),))],
+        scratch=scratch + [pltpu.SemaphoreType.DMA((1 + len(sibling) + len(far),))],
         out_specs=[ANYWHERE],
     )[0]
 
 
-def place_body(me_ref, out_in_ref, piece_ref, out_ref, sem, *, offset, cells):
-    late = piece_ref.shape[2]
-    at = pl.multiple_of((me_ref[0] ^ offset) * cells + (cells - late), 128)
-    copy = pltpu.make_async_copy(piece_ref, out_ref.at[:, :, pl.ds(at, late)], sem)
-    copy.start()
-    copy.wait()
-
-
-def place(me, out, piece, offset, clusters):
-    return call(
-        functools.partial(place_body, offset=offset, cells=out.shape[2] // clusters),
+def place_body(me_ref, out_in_ref, *refs, where, cells):
+    piece_refs = refs[: len(where)]
+    out_ref, sems = refs[len(where) :]
+    copies = []
+    for (k, v), piece_ref in zip(where, piece_refs):
+        length, _, late = piece_ref.shape
+        at = pl.multiple_of((me_ref[0] ^ k) * cells + (cells - late), 128)
+        target = out_ref.at[pl.ds(v, length), :, pl.ds(at, late)]
+        copies.append(pltpu.make_async_copy(piece_ref, target, sems.at[len(copies)]))
+        copies[-1].start()
+    for copy in copies:
+        copy.wait()
+
+
+def place(me, out, pieces, where, clusters):
+    return call(
+        functools.partial(place_body, where=where, cells=out.shape[2] // clusters),
         "place",
-        [IN_SMEM, ANYWHERE, IN_VMEM],
+        [IN_SMEM, ANYWHERE] + [IN_VMEM] * len(pieces),
         [jax.ShapeDtypeStruct(out.shape, out.dtype)],
         me,
         out,
-        piece,
-        scratch=[pltpu.SemaphoreType.DMA],
+        *pieces,
+        scratch=[pltpu.SemaphoreType.DMA((len(pieces),))],
         aliases={1: 0},
         out_specs=[ANYWHERE],
     )[0]
@@ -340,15 +403,18 @@
     gram, basis, near, left, own = subspace(
         gram, other, labels, start.T, total_rows, clusters, slots
     )
-    own_piece, sibling, *late = local_modes(near, left, x, EARLY)
-    both = lax.optimization_barrier((*late, *rows, sibling))
-    late, rows, sibling = both[: len(far)], both[len(far) : -1], both[-1]
-    late = [swap(piece, "clus", k) for piece, k in zip(late, far)]
-    near = [own_piece, swap(sibling, "clus", 1)]
+    late_parts, near_parts = (0,), tuple(range(0, variables, 2))
+    own_piece, sibling, late = local_modes(near, left, x, EARLY, late_parts, near_parts)
+    where = [(k, v) for k in far for v in late_parts]
+    late = list(late)
+    both = lax.optimization_barrier((late[-1], *rows))
+    late[-1], rows = both[0], both[1:]
+    late = [swap(piece, "clus", k) for piece, (k, v) in zip(late, where)]
+    sibling = [swap(piece, "clus", 1) for piece in sibling]
     coefficients, correlations = small_outputs(me, successor, gram, labels, basis, clusters)
-    out = owner_modes(me, own, near, rows, far, clusters)
-    for piece, k in zip(late, far):
-        out = place(me, out, piece, k, clusters)
+    out = owner_modes(me, own, own_piece, sibling, near_parts, rows, far, clusters)
+    for group in (slice(0, -1), slice(-1, None)):
+        out = place(me, out, late[group], where[group], clusters)
     modes_out = jnp.transpose(out, (1, 0, 2))[None]
     return modes_out, coefficients.T, correlations
 

time: 42.2 us -> 39.2 us (0.929)
  waiting for transfers between devices: 18 us -> 14.3 us
  starting transfers between devices: 11.1 us -> 11.6 us
    ppermute x10 -> x12, waiting for transfers between devices: 18 us -> 14.3 us  [swap(): return lax.ppermute(x, axis, [(i, i ^ offset) for i in range(size)])]
    ppermute x10 -> x12, starting transfers between devices: 11.1 us -> 11.6 us  [swap(): return lax.ppermute(x, axis, [(i, i ^ offset) for i in range(size)])]
  transfers between devices with their start and end apart: 10 -> 12, of which waited for: 6 -> 4; matrix products, arithmetic and copies ran while one was open for 0% -> 0% of each run, Pallas kernels for 19% -> 21%
where the time goes in v4:
time: 39.2 us; the launch traced here: 39 us
  waiting for transfers between devices  14.3 us (36%)
  Pallas kernels  12.3 us (31%)
  starting transfers between devices  11.6 us (30%)
  between operations  0.73 us (2%)
    ppermute x12, waiting for transfers between devices, swap(): return lax.ppermute(x, axis, [(i, i ^ offset) for i in range(size)])  14.3 us
    pallas_call x8, Pallas kernels, call(): pl.pallas_call(body, in_specs=in_specs, out_specs=out_specs or [IN_VMEM]...  12.3 us
    ppermute x12, starting transfers between devices, swap(): return lax.ppermute(x, axis, [(i, i ^ offset) for i in range(size)])  11.6 us
  transfers between devices with their start and end apart: 12, of which 4 were waited for; matrix products, arithmetic and copies ran while one was open for 0% of the time, Pallas kernels for 21%

profile of v4, /device:TPU:1, one launch (start us, length us, event | category | flops | bytes accessed | tf_op | source)
XLA Modules:
  0.0 39.0 jit_solution(10302543650441011653)
XLA Ops:
  0.6 3.6 %gram.1 = (f32[72,128]{1,0:T(8,128)S(1)}, bf16[5,32,1024]{2,1,0:T(8,128)(2,1)S(1)}, bf16[5,32,1024]{2,1,0:T(8,128)(2,1)S(1)}) custom-call(s32[1,128]{1,0:T(1,128)} %bitcast.9, bf16[5,128,3072]{2,1,0:T(8,128)(2,1)} %bitcast.13), custom_call_target="tpu_custom_call" | custom-call | tf_op jit(solution)/shard_map/gram/pallas_call | solution.py:22
  4.2 0.1 collective-permute-start
  4.3 2.6 %collective-permute-start.2 = (f32[72,128]{1,0:T(8,128)S(1)}, f32[72,128]{1,0:T(8,128)S(1)}, u32[]{:S(2)}, u32[]{:S(2)}) collective-permute-start(f32[72,128]{1,0:T(8,128)S(1)} %get-tuple-element.25), channel_id=1, source_target_pairs={{0,3},{1,2},{2,1},{3,0},{4,7},{5,6},{6,5},{7,4},{8,11},{9,10},{10,... | collective-permute-start | bytes 110600 | tf_op jit(solution)/shard_map/ppermute | solution.py:376
  6.9 0.1 collective-permute-start.1
  7.0 0.0 collective-permute-done
  7.0 1.4 %collective-permute-start.8 = (bf16[5,32,1024]{2,1,0:T(8,128)(2,1)S(1)}, bf16[5,32,1024]{2,1,0:T(8,128)(2,1)S(1)}, u32[]{:S(2)}, u32[]{:S(2)}) collective-permute-start(bf16[5,32,1024]{2,1,0:T(8,128)(2,1)S(1)} %get-tuple-element.37), channel_id=1, source_target_pairs={{0,2},{1,3},{2,0},{3,1},{4,6},{5,7},{6,4},{7,5},{8,10},{9,11},{10,... | collective-permute-start | bytes 983048 | tf_op jit(solution)/shard_map/ppermute | solution.py:376
  8.4 0.7 %collective-permute-start.9 = (bf16[5,32,1024]{2,1,0:T(8,128)(2,1)S(1)}, bf16[5,32,1024]{2,1,0:T(8,128)(2,1)S(1)}, u32[]{:S(2)}, u32[]{:S(2)}) collective-permute-start(bf16[5,32,1024]{2,1,0:T(8,128)(2,1)S(1)} %get-tuple-element.38), channel_id=1, source_target_pairs={{0,3},{1,2},{2,1},{3,0},{4,7},{5,6},{6,5},{7,4},{8,11},{9,10},{10,... | collective-permute-start | bytes 983048 | tf_op jit(solution)/shard_map/ppermute | solution.py:376
  9.1 0.0 collective-permute-done.2
  9.1 0.7 %collective-permute-done.1 = f32[72,128]{1,0:T(8,128)S(1)} collective-permute-done((f32[72,128]{1,0:T(8,128)S(1)}, f32[72,128]{1,0:T(8,128)S(1)}, u32[]{:S(2)}, u32[]{:S(2)}) %collective-permute-start.1) | collective-permute-done | bytes 36896 | tf_op jit(solution)/shard_map/ppermute | solution.py:376
  9.8 1.4 %collective-permute-start.3 = (f32[72,128]{1,0:T(8,128)S(1)}, f32[72,128]{1,0:T(8,128)S(1)}, u32[]{:S(2)}, u32[]{:S(2)}) collective-permute-start(f32[72,128]{1,0:T(8,128)S(1)} %add_add_fusion.after_ref), channel_id=1, source_target_pairs={{0,4},{4,0},{8,12},{12,8},{1,5},{5,1},{9,13},{13,9},{2,6},{6,2},{1... | collective-permute-start | bytes 110600 | tf_op jit(solution)/shard_map/ppermute | solution.py:376
  11.1 1.8 %collective-permute-done.3 = f32[72,128]{1,0:T(8,128)S(1)} collective-permute-done((f32[72,128]{1,0:T(8,128)S(1)}, f32[72,128]{1,0:T(8,128)S(1)}, u32[]{:S(2)}, u32[]{:S(2)}) %collective-permute-start.3) | collective-permute-done | bytes 36896 | tf_op jit(solution)/shard_map/ppermute | solution.py:376
  12.9 0.0 copy-start
  13.0 0.0 copy-start.1
  13.0 2.4 %collective-permute-start.4 = (f32[72,128]{1,0:T(8,128)S(1)}, f32[72,128]{1,0:T(8,128)S(1)}, u32[]{:S(2)}, u32[]{:S(2)}) collective-permute-start(f32[72,128]{1,0:T(8,128)S(1)} %add.15.first_ref), channel_id=1, source_target_pairs={{0,8},{4,12},{8,0},{12,4},{1,9},{5,13},{9,1},{13,5},{2,10},{6,14},... | collective-permute-start | bytes 110600 | tf_op jit(solution)/shard_map/ppermute | solution.py:376
  15.3 2.1 %load.1.x_ref = bf16[5,128,3072]{2,1,0:T(8,128)(2,1)S(1)} custom-call(f32[72,128]{1,0:T(8,128)S(1)} %add_add_fusion.after_ref, bf16[5,128,3072]{2,1,0:T(8,128)(2,1)} %bitcast.14), custom_call_target="tpu_custom_call" | custom-call | tf_op jit(solution)/shard_map/load/pallas_call | solution.py:22
  17.5 0.0 collective-permute-done.4.second_ref
  17.5 0.0 copy-done
  17.5 0.0 copy-done.1
  17.5 1.6 %subspace.1 = (f32[128,128]{1,0:T(8,128)S(1)}, f32[16,128]{1,0:T(8,128)S(1)}, bf16[2,16,128]{2,1,0:T(8,128)(2,1)S(1)}, bf16[2,16,128]{2,1,0:T(8,128)(2,1)S(1)}, bf16[16,32]{1,0:T(8,128)(2,1)S(1)}) custom-call(f32[72,128]{1,0:T(8,128)S(1)} %add.15.first_ref, f32[72,128]{1,0:T(8,128)S(1)} %collective-permute-done.4.second_ref, s32[1,128]{1,0:T(1,128)S(1)} %bitcast.10, ...), custom_call_target="tpu_custom_call" | custom-call | tf_op jit(solution)/shard_map/subspace/pallas_call | solution.py:22
  19.1 0.0 copy-start.2
  19.1 1.0 %modes.1 = (bf16[5,16,3072]{2,1,0:T(8,128)(2,1)S(1)}, bf16[2,16,3072]{2,1,0:T(8,128)(2,1)S(1)}, bf16[2,16,3072]{2,1,0:T(8,128)(2,1)S(1)}, bf16[1,16,3072]{2,1,0:...) custom-call(bf16[2,16,128]{2,1,0:T(8,128)(2,1)S(1)} %get-tuple-element.30.near_ref, ...), custom_call_target="tpu_custom_call" | custom-call | tf_op jit(solution)/shard_map/modes/pallas_call | solution.py:22
  20.1 1.1 %collective-permute-start.10 = (bf16[5,16,2048]{2,1,0:T(8,128)(2,1)S(1)}, bf16[5,16,2048]{2,1,0:T(8,128)(2,1)S(1)}, u32[]{:S(2)}, u32[]{:S(2)}) collective-permute-start(bf16[5,16,2048]{2,1,0:T(8,128)(2,1)S(1)} %get-tuple-element.41), channel_id=1, source_target_pairs={{0,2},{1,3},{2,0},{3,1},{4,6},{5,7},{6,4},{7,5},{8,10},{9,11},{10,... | collective-permute-start | bytes 983048 | tf_op jit(solution)/shard_map/ppermute | solution.py:376
  21.2 0.0 collective-permute-done.8.refs_3_
  21.2 3.9 %collective-permute-done.9.refs_4_ = bf16[5,32,1024]{2,1,0:T(8,128)(2,1)S(1)} collective-permute-done((bf16[5,32,1024]{2,1,0:T(8,128)(2,1)S(1)}, bf16[5,32,1024]{2,1,0:T(8,128)(2,1)S(1)}, u32[]{:S(2)}, u32[]{:S(2)}) %collective-permute-start.9) | collective-permute-done | bytes 327712 | tf_op jit(solution)/shard_map/ppermute | solution.py:376
  25.1 0.0 collective-permute-start.11
  25.1 1.4 %collective-permute-start.5 = (bf16[2,16,3072]{2,1,0:T(8,128)(2,1)S(1)}, bf16[2,16,3072]{2,1,0:T(8,128)(2,1)S(1)}, u32[]{:S(2)}, u32[]{:S(2)}) collective-permute-start(bf16[2,16,3072]{2,1,0:T(8,128)(2,1)S(1)} %get-tuple-element.33), channel_id=1, source_target_pairs={{0,1},{1,0},{2,3},{3,2},{4,5},{5,4},{6,7},{7,6},{8,9},{9,8},{10,11... | collective-permute-start | bytes 589832 | tf_op jit(solution)/shard_map/ppermute | solution.py:376
  26.5 0.0 collective-permute-start.6
  26.5 0.5 %collective-permute-start.7 = (bf16[1,16,3072]{2,1,0:T(8,128)(2,1)S(1)}, bf16[1,16,3072]{2,1,0:T(8,128)(2,1)S(1)}, u32[]{:S(2)}, u32[]{:S(2)}) collective-permute-start(bf16[1,16,3072]{2,1,0:T(8,128)(2,1)S(1)} %get-tuple-element.35), channel_id=1, source_target_pairs={{0,1},{1,0},{2,3},{3,2},{4,5},{5,4},{6,7},{7,6},{8,9},{9,8},{10,11... | collective-permute-start | bytes 294920 | tf_op jit(solution)/shard_map/ppermute | solution.py:376
  27.0 0.0 copy-done.2
  27.0 1.5 %small.1 = (f32[16,32]{1,0:T(8,128)}, f32[1,16,16]{2,1,0:T(8,128)}) custom-call(s32[1]{0:T(128)} %bitcast.me_ref, s32[4]{0:T(128)S(1)} %copy-done.2, f32[128,128]{1,0:T(8,128)S(1)} %get-tuple-element.43.gram_ref, s32[1,128]{1,0:T(1,128)S(1)} %bitcast.11, f32[16,128]{1,0:T(8,128)S(1)} %get-tuple-element.44.basis_ref), custom_call_target="tpu_custom_call" | custom-call | tf_op jit(solution)/shard_map/small/pallas_call | solution.py:22
  28.5 0.0 collective-permute-done.7.refs_2_
  28.5 0.0 collective-permute-done.5.refs_0_
  28.5 0.0 collective-permute-done.6.refs_1_
  28.5 1.1 %owner.1.out_in_ref = bf16[5,16,12288]{2,1,0:T(8,128)(2,1)} custom-call(s32[1]{0:T(128)} %bitcast.me_ref, bf16[16,32]{1,0:T(8,128)(2,1)S(1)} %get-tuple-element.29.own_ref, bf16[5,16,3072]{2,1,0:T(8,128)(2,1)S(1)} %get-tuple-element.32.near_ref, bf16[2,16,3072]{2,1,0:T(8,128)(2,1)S(1)} %collective-permute-done.5.refs_0_, ...), custom_call_target="tpu_custom_call" | custom-call | tf_op jit(solution)/shard_map/owner/pallas_call | solution.py:22
  29.6 0.0 collective-permute-done.10.refs_0_
  29.6 0.7 %place.2.out_in_ref = bf16[5,16,12288]{2,1,0:T(8,128)(2,1)} custom-call(s32[1]{0:T(128)} %bitcast.me_ref, bf16[5,16,12288]{2,1,0:T(8,128)(2,1)} %owner.1.out_in_ref, bf16[5,16,2048]{2,1,0:T(8,128)(2,1)S(1)} %collective-permute-done.10.refs_0_), custom_call_target="tpu_custom_call", output_to_operand_aliasing={{}: (1, {})} | custom-call | tf_op jit(solution)/shard_map/place/pallas_call | solution.py:22
  30.4 7.9 %collective-permute-done.11.refs_0_ = bf16[5,16,2048]{2,1,0:T(8,128)(2,1)S(1)} collective-permute-done((bf16[5,16,2048]{2,1,0:T(8,128)(2,1)S(1)}, bf16[5,16,2048]{2,1,0:T(8,128)(2,1)S(1)}, u32[]{:S(2)}, u32[]{:S(2)}) %collective-permute-start.11) | collective-permute-done | bytes 327712 | tf_op jit(solution)/shard_map/ppermute | solution.py:376
  38.2 0.7 %place.3 = bf16[5,16,12288]{2,1,0:T(8,128)(2,1)} custom-call(s32[1]{0:T(128)} %bitcast.me_ref, bf16[5,16,12288]{2,1,0:T(8,128)(2,1)} %place.2.out_in_ref, bf16[5,16,2048]{2,1,0:T(8,128)(2,1)S(1)} %collective-permute-done.11.refs_0_), custom_call_target="tpu_custom_call", output_to_operand_aliasing={{}: (1, {})} | custom-call | tf_op jit(solution)/shard_map/place/pallas_call | solution.py:22
  (2 shorter events, 0.0 us)
Async XLA Ops:
  4.2 2.8 %collective-permute-start = (f32[72,128]{1,0:T(8,128)S(1)}, f32[72,128]{1,0:T(8,128)S(1)}, u32[]{:S(2)}, u32[]{:S(2)}) collective-permute-start(f32[72,128]{1,0:T(8,128)S(1)} %get-tuple-element.25), channel_id=1, source_target_pairs={{0,1},{1,0},{2,3},{3,2},{4,5},{5,4},{6,7},{7,6},{8,9},{9,8},{10,11... | collective-permute-start | bytes 110600 | tf_op jit(solution)/shard_map/ppermute | solution.py:376
  4.3 4.7 %collective-permute-start.2 = (f32[72,128]{1,0:T(8,128)S(1)}, f32[72,128]{1,0:T(8,128)S(1)}, u32[]{:S(2)}, u32[]{:S(2)}) collective-permute-start(f32[72,128]{1,0:T(8,128)S(1)} %get-tuple-element.25), channel_id=1, source_target_pairs={{0,3},{1,2},{2,1},{3,0},{4,7},{5,6},{6,5},{7,4},{8,11},{9,10},{10,... | collective-permute-start | bytes 110600 | tf_op jit(solution)/shard_map/ppermute | solution.py:376
  6.9 2.8 %collective-permute-start.1 = (f32[72,128]{1,0:T(8,128)S(1)}, f32[72,128]{1,0:T(8,128)S(1)}, u32[]{:S(2)}, u32[]{:S(2)}) collective-permute-start(f32[72,128]{1,0:T(8,128)S(1)} %get-tuple-element.25), channel_id=1, source_target_pairs={{0,2},{1,3},{2,0},{3,1},{4,6},{5,7},{6,4},{7,5},{8,10},{9,11},{10,... | collective-permute-start | bytes 110600 | tf_op jit(solution)/shard_map/ppermute | solution.py:376
  7.0 14.1 %collective-permute-start.8 = (bf16[5,32,1024]{2,1,0:T(8,128)(2,1)S(1)}, bf16[5,32,1024]{2,1,0:T(8,128)(2,1)S(1)}, u32[]{:S(2)}, u32[]{:S(2)}) collective-permute-start(bf16[5,32,1024]{2,1,0:T(8,128)(2,1)S(1)} %get-tuple-element.37), channel_id=1, source_target_pairs={{0,2},{1,3},{2,0},{3,1},{4,6},{5,7},{6,4},{7,5},{8,10},{9,11},{10,... | collective-permute-start | bytes 983048 | tf_op jit(solution)/shard_map/ppermute | solution.py:376
  8.4 16.7 %collective-permute-start.9 = (bf16[5,32,1024]{2,1,0:T(8,128)(2,1)S(1)}, bf16[5,32,1024]{2,1,0:T(8,128)(2,1)S(1)}, u32[]{:S(2)}, u32[]{:S(2)}) collective-permute-start(bf16[5,32,1024]{2,1,0:T(8,128)(2,1)S(1)} %get-tuple-element.38), channel_id=1, source_target_pairs={{0,3},{1,2},{2,1},{3,0},{4,7},{5,6},{6,5},{7,4},{8,11},{9,10},{10,... | collective-permute-start | bytes 983048 | tf_op jit(solution)/shard_map/ppermute | solution.py:376
  9.8 3.2 %collective-permute-start.3 = (f32[72,128]{1,0:T(8,128)S(1)}, f32[72,128]{1,0:T(8,128)S(1)}, u32[]{:S(2)}, u32[]{:S(2)}) collective-permute-start(f32[72,128]{1,0:T(8,128)S(1)} %add_add_fusion.after_ref), channel_id=1, source_target_pairs={{0,4},{4,0},{8,12},{12,8},{1,5},{5,1},{9,13},{13,9},{2,6},{6,2},{1... | collective-permute-start | bytes 110600 | tf_op jit(solution)/shard_map/ppermute | solution.py:376
  12.9 4.5 %copy-start = (f32[128,16]{0,1:T(8,128)S(1)}, f32[128,16]{0,1:T(8,128)}, u32[]{:S(2)}) copy-start(f32[128,16]{0,1:T(8,128)} %param.6) | copy-start | bytes 24580
  13.0 4.5 %copy-start.1 = (s32[128]{0:T(128)S(1)}, s32[128]{0:T(128)}, u32[]{:S(2)}) copy-start(s32[128]{0:T(128)} %param.5) | copy-start | bytes 1540
  13.0 4.5 %collective-permute-start.4 = (f32[72,128]{1,0:T(8,128)S(1)}, f32[72,128]{1,0:T(8,128)S(1)}, u32[]{:S(2)}, u32[]{:S(2)}) collective-permute-start(f32[72,128]{1,0:T(8,128)S(1)} %add.15.first_ref), channel_id=1, source_target_pairs={{0,8},{4,12},{8,0},{12,4},{1,9},{5,13},{9,1},{13,5},{2,10},{6,14},... | collective-permute-start | bytes 110600 | tf_op jit(solution)/shard_map/ppermute | solution.py:376
  19.1 7.9 %copy-start.2 = (s32[4]{0:T(128)S(1)}, s32[4]{0:T(128)}, u32[]{:S(2)}) copy-start(s32[4]{0:T(128)} %successor_ref.1) | copy-start | bytes 52
  20.1 9.5 %collective-permute-start.10 = (bf16[5,16,2048]{2,1,0:T(8,128)(2,1)S(1)}, bf16[5,16,2048]{2,1,0:T(8,128)(2,1)S(1)}, u32[]{:S(2)}, u32[]{:S(2)}) collective-permute-start(bf16[5,16,2048]{2,1,0:T(8,128)(2,1)S(1)} %get-tuple-element.41), channel_id=1, source_target_pairs={{0,2},{1,3},{2,0},{3,1},{4,6},{5,7},{6,4},{7,5},{8,10},{9,11},{10,... | collective-permute-start | bytes 983048 | tf_op jit(solution)/shard_map/ppermute | solution.py:376
  25.1 13.2 %collective-permute-start.11 = (bf16[5,16,2048]{2,1,0:T(8,128)(2,1)S(1)}, bf16[5,16,2048]{2,1,0:T(8,128)(2,1)S(1)}, u32[]{:S(2)}, u32[]{:S(2)}) collective-permute-start(bf16[5,16,2048]{2,1,0:T(8,128)(2,1)S(1)} %get-tuple-element.42), channel_id=1, source_target_pairs={{0,3},{1,2},{2,1},{3,0},{4,7},{5,6},{6,5},{7,4},{8,11},{9,10},{10,... | collective-permute-start | bytes 983048 | tf_op jit(solution)/shard_map/ppermute | solution.py:376
  25.1 3.4 %collective-permute-start.5 = (bf16[2,16,3072]{2,1,0:T(8,128)(2,1)S(1)}, bf16[2,16,3072]{2,1,0:T(8,128)(2,1)S(1)}, u32[]{:S(2)}, u32[]{:S(2)}) collective-permute-start(bf16[2,16,3072]{2,1,0:T(8,128)(2,1)S(1)} %get-tuple-element.33), channel_id=1, source_target_pairs={{0,1},{1,0},{2,3},{3,2},{4,5},{5,4},{6,7},{7,6},{8,9},{9,8},{10,11... | collective-permute-start | bytes 589832 | tf_op jit(solution)/shard_map/ppermute | solution.py:376
  26.5 2.0 %collective-permute-start.6 = (bf16[2,16,3072]{2,1,0:T(8,128)(2,1)S(1)}, bf16[2,16,3072]{2,1,0:T(8,128)(2,1)S(1)}, u32[]{:S(2)}, u32[]{:S(2)}) collective-permute-start(bf16[2,16,3072]{2,1,0:T(8,128)(2,1)S(1)} %get-tuple-element.34), channel_id=1, source_target_pairs={{0,1},{1,0},{2,3},{3,2},{4,5},{5,4},{6,7},{7,6},{8,9},{9,8},{10,11... | collective-permute-start | bytes 589832 | tf_op jit(solution)/shard_map/ppermute | solution.py:376
  26.5 2.0 %collective-permute-start.7 = (bf16[1,16,3072]{2,1,0:T(8,128)(2,1)S(1)}, bf16[1,16,3072]{2,1,0:T(8,128)(2,1)S(1)}, u32[]{:S(2)}, u32[]{:S(2)}) collective-permute-start(bf16[1,16,3072]{2,1,0:T(8,128)(2,1)S(1)} %get-tuple-element.35), channel_id=1, source_target_pairs={{0,1},{1,0},{2,3},{3,2},{4,5},{5,4},{6,7},{7,6},{8,9},{9,8},{10,11... | collective-permute-start | bytes 294920 | tf_op jit(solution)/shard_map/ppermute | solution.py:376

commit v5 on v4

--- a/solution.py
+++ b/solution.py
@@ -15,7 +15,7 @@
 ANYWHERE = pl.BlockSpec(memory_space=pl.ANY)
 LIMIT = 20 * 1024 * 1024
 LARGE = 46 * 1024 * 1024
-EARLY = 1024
+EARLY = 896
 
 
 def call(body, name, in_specs, outs, *operands, scratch=(), aliases=None, out_specs=None, limit=LIMIT):
@@ -157,7 +157,7 @@
 
 
 def subspace_body(
-    first_ref, second_ref, row_ref, start_ref, gram_ref, basis_ref, near_ref, left_ref, own_ref, *, total_rows
+    first_ref, second_ref, row_ref, start_ref, x_ref, gram_ref, basis_ref, near_ref, own_ref, *late_refs, total_rows
 ):
     row_labels = row_ref[...]
     together = same_cluster(row_labels)
@@ -176,36 +176,48 @@
     me = lax.axis_index("clus")
     for k in range(2):
         near_ref[k] = jnp.where(row_labels == (me ^ k), rounded, 0.0).astype(jnp.bfloat16)
-    for k in range(left_ref.shape[0]):
-        left_ref[k] = jnp.where(row_labels == (me ^ (k + 2)), rounded, 0.0).astype(jnp.bfloat16)
+    left = jnp.concatenate(
+        [jnp.where(row_labels == (me ^ (k + 2)), rounded, 0.0) for k in range(len(late_refs))], axis=0
+    ).astype(jnp.bfloat16)
+    begin = x_ref.shape[2] - late_refs[0].shape[2]
+    modes = rounded.shape[0]
+    for v in range(x_ref.shape[0]):
+        product = jnp.dot(left, x_ref[v, :, begin:], preferred_element_type=jnp.float32)
+        product = product.astype(jnp.bfloat16)
+        for k, late_ref in enumerate(late_refs):
+            late_ref[v] = product[k * modes : (k + 1) * modes]
     choice = slot_choice(row_labels, together, me, own_ref.shape[1])
     own_ref[...] = lax.dot_general(
         rounded.astype(jnp.bfloat16), choice, (((1,), (1,)), ((), ())), preferred_element_type=jnp.float32
     ).astype(jnp.bfloat16)
 
 
-def subspace(first, second, labels, start, total_rows, clusters, slots):
+def subspace(first, second, labels, start, x, total_rows, clusters, slots, early):
     modes, count = start.shape
-    return call(
+    variables, _, cells = x.shape
+    late = pltpu.VMEM((variables, modes, cells - early), jnp.bfloat16)
+    gram, basis, near, own, *late = call(
         functools.partial(subspace_body, total_rows=total_rows),
         "subspace",
-        [IN_VMEM, IN_VMEM, IN_VMEM, IN_VMEM],
+        [IN_VMEM] * 5,
         [
             pltpu.VMEM((count, count), jnp.float32),
             pltpu.VMEM((modes, count), jnp.float32),
             pltpu.VMEM((2, modes, count), jnp.bfloat16),
-            pltpu.VMEM((clusters - 2, modes, count), jnp.bfloat16),
             pltpu.VMEM((modes, slots), jnp.bfloat16),
-        ],
+        ]
+        + [late] * (clusters - 2),
         first,
         second,
         labels,
         start,
-    )
-
-
-def small_body(me_ref, successor_ref, gram_ref, row_ref, basis_ref, coefficients_ref, correlations_ref):
-    me = me_ref[0]
+        x,
+    )
+    return gram, basis, near, own, late
+
+
+def small_body(successor_ref, gram_ref, row_ref, basis_ref, coefficients_ref, correlations_ref):
+    me = lax.axis_index("clus")
     row_labels = row_ref[...]
     basis = basis_ref[...]
     rounded = basis.astype(jnp.bfloat16).astype(jnp.float32)
@@ -220,17 +232,16 @@
     coefficients_ref[...] = pltpu.roll(basis, (count - me * own) % count, 1)[:, :own]
 
 
-def small_outputs(me, successor, gram, labels, basis, clusters):
+def small_outputs(successor, gram, labels, basis, clusters):
     modes, count = basis.shape
     return call(
         small_body,
         "small",
-        [IN_SMEM, IN_SMEM, IN_VMEM, IN_VMEM, IN_VMEM],
+        [IN_SMEM, IN_VMEM, IN_VMEM, IN_VMEM],
         [
             jax.ShapeDtypeStruct((modes, count // clusters), jnp.float32),
             jax.ShapeDtypeStruct((1, modes, modes), jnp.float32),
         ],
-        me,
         successor,
         gram,
         labels,
@@ -238,67 +249,39 @@
     )
 
 
-def modes_body(near_ref, far_ref, x_ref, *out_refs, late_parts, near_parts):
+def near_body(near_ref, x_ref, own_ref, *sibling_refs, parts):
     modes, count = near_ref.shape[1:]
-    number = far_ref.shape[0]
-    own_ref = out_refs[0]
-    sibling_refs = out_refs[1 : 1 + len(near_parts)]
-    late_refs = out_refs[1 + len(near_parts) :]
-    begin = x_ref.shape[2] - late_refs[0].shape[2]
-
-    def place_of(parts, v):
+    left = near_ref[...].reshape(2 * modes, count)
+    for v in range(x_ref.shape[0]):
+        product = jnp.dot(left, x_ref[v], preferred_element_type=jnp.float32).astype(jnp.bfloat16)
+        own_ref[v] = product[:modes]
         part = max(i for i, first in enumerate(parts) if first <= v)
-        return part, v - parts[part]
-
-    for v in range(x_ref.shape[0]):
-        left = far_ref[...].reshape(number * modes, count)
-        product = jnp.dot(left, x_ref[v, :, begin:], preferred_element_type=jnp.float32)
-        product = product.astype(jnp.bfloat16)
-        part, at = place_of(late_parts, v)
-        for i in range(number):
-            late_refs[i * len(late_parts) + part][at] = product[i * modes : (i + 1) * modes]
-        left = near_ref[...].reshape(2 * modes, count)
-        product = jnp.dot(left, x_ref[v], preferred_element_type=jnp.float32)
-        product = product.astype(jnp.bfloat16)
-        own_ref[v] = product[:modes]
-        part, at = place_of(near_parts, v)
-        sibling_refs[part][at] = product[modes:]
-
-
-def lengths(parts, total):
-    return [b - a for a, b in zip(parts, list(parts[1:]) + [total])]
-
-
-def local_modes(near, left, x, begin, late_parts, near_parts):
+        sibling_refs[part][v - parts[part]] = product[modes:]
+
+
+def near_modes(near, x, parts):
     variables, count, cells = x.shape
-    number, modes, _ = left.shape
-
-    def out(length, width):
-        return pltpu.VMEM((length, modes, width), jnp.bfloat16)
-
-    sibling = [out(length, cells) for length in lengths(near_parts, variables)]
-    late = [out(length, cells - begin) for length in lengths(late_parts, variables)]
-    outs = call(
-        functools.partial(modes_body, late_parts=late_parts, near_parts=near_parts),
-        "modes",
-        [IN_VMEM] * 3,
-        [out(variables, cells)] + sibling + late * number,
+    modes = near.shape[1]
+    lengths = [b - a for a, b in zip(parts, parts[1:] + (variables,))]
+    own, *sibling = call(
+        functools.partial(near_body, parts=parts),
+        "near",
+        [IN_VMEM, IN_VMEM],
+        [pltpu.VMEM((n, modes, cells), jnp.bfloat16) for n in [variables] + lengths],
         near,
-        left,
         x,
     )
-    first = 1 + len(sibling)
-    return outs[0], outs[1:first], outs[first:]
-
-
-def owner_body(me_ref, own_ref, near_ref, *refs, far, near_parts):
+    return own, sibling
+
+
+def owner_body(own_ref, near_ref, *refs, far, near_parts):
     sibling_refs = refs[: len(near_parts)]
     refs = refs[len(near_parts) :]
     rows_refs = refs[: len(far)]
     out_ref = refs[len(far)]
     early_refs = refs[len(far) + 1 : 2 * len(far) + 1]
     sems = refs[2 * len(far) + 1]
-    me = me_ref[0]
+    me = lax.axis_index("clus")
     cells = near_ref.shape[2]
     copies = []
 
@@ -323,16 +306,15 @@
         copy.wait()
 
 
-def owner_modes(me, own, near, sibling, near_parts, rows, far, clusters):
+def owner_modes(own, near, sibling, near_parts, rows, far, clusters):
     variables, modes, cells = near.shape
     early = rows[0].shape[2]
     scratch = [pltpu.VMEM((variables, modes, early), jnp.bfloat16) for _ in far]
     return call(
         functools.partial(owner_body, far=far, near_parts=near_parts),
         "owner",
-        [IN_SMEM] + [IN_VMEM] * (2 + len(sibling) + len(rows)),
+        [IN_VMEM] * (2 + len(sibling) + len(rows)),
         [jax.ShapeDtypeStruct((variables, modes, clusters * cells), jnp.bfloat16)],
-        me,
         own,
         near,
         *sibling,
@@ -342,31 +324,31 @@
     )[0]
 
 
-def place_body(me_ref, out_in_ref, *refs, where, cells):
-    piece_refs = refs[: len(where)]
-    out_ref, sems = refs[len(where) :]
+def place_body(out_in_ref, *refs, offsets, cells):
+    piece_refs = refs[: len(offsets)]
+    out_ref, sems = refs[len(offsets) :]
+    me = lax.axis_index("clus")
     copies = []
-    for (k, v), piece_ref in zip(where, piece_refs):
-        length, _, late = piece_ref.shape
-        at = pl.multiple_of((me_ref[0] ^ k) * cells + (cells - late), 128)
-        target = out_ref.at[pl.ds(v, length), :, pl.ds(at, late)]
+    for k, piece_ref in zip(offsets, piece_refs):
+        late = piece_ref.shape[2]
+        at = pl.multiple_of((me ^ k) * cells + (cells - late), 128)
+        target = out_ref.at[:, :, pl.ds(at, late)]
         copies.append(pltpu.make_async_copy(piece_ref, target, sems.at[len(copies)]))
         copies[-1].start()
     for copy in copies:
         copy.wait()
 
 
-def place(me, out, pieces, where, clusters):
+def place(out, pieces, offsets, clusters):
     return call(
-        functools.partial(place_body, where=where, cells=out.shape[2] // clusters),
+        functools.partial(place_body, offsets=offsets, cells=out.shape[2] // clusters),
         "place",
-        [IN_SMEM, ANYWHERE] + [IN_VMEM] * len(pieces),
+        [ANYWHERE] + [IN_VMEM] * len(pieces),
         [jax.ShapeDtypeStruct(out.shape, out.dtype)],
-        me,
         out,
         *pieces,
         scratch=[pltpu.SemaphoreType.DMA((len(pieces),))],
-        aliases={1: 0},
+        aliases={0: 0},
         out_specs=[ANYWHERE],
     )[0]
 
@@ -380,7 +362,6 @@
     count, variables, cells = snapshots.shape
     clusters = lax.axis_size("clus")
     space = lax.axis_size("space")
-    me = lax.axis_index("clus").astype(jnp.int32).reshape(1)
     total_rows = variables * cells * space * clusters
     slots = CAP * clusters
     far = list(range(2, clusters))
@@ -400,21 +381,19 @@
         if b > 0:
             gram = gram + other
         other = swap(gram, "space", 1 << b)
-    gram, basis, near, left, own = subspace(
-        gram, other, labels, start.T, total_rows, clusters, slots
-    )
-    late_parts, near_parts = (0,), tuple(range(0, variables, 2))
-    own_piece, sibling, late = local_modes(near, left, x, EARLY, late_parts, near_parts)
-    where = [(k, v) for k in far for v in late_parts]
-    late = list(late)
+    gram, basis, near, own, late = subspace(
+        gram, other, labels, start.T, x, total_rows, clusters, slots, EARLY
+    )
     both = lax.optimization_barrier((late[-1], *rows))
     late[-1], rows = both[0], both[1:]
-    late = [swap(piece, "clus", k) for piece, (k, v) in zip(late, where)]
+    late = [swap(piece, "clus", k) for piece, k in zip(late, far)]
+    parts = tuple(range(0, variables, 2))
+    own_piece, sibling = near_modes(near, load(near, x_hbm), parts)
     sibling = [swap(piece, "clus", 1) for piece in sibling]
-    coefficients, correlations = small_outputs(me, successor, gram, labels, basis, clusters)
-    out = owner_modes(me, own, own_piece, sibling, near_parts, rows, far, clusters)
+    coefficients, correlations = small_outputs(successor, gram, labels, basis, clusters)
+    out = owner_modes(own, own_piece, sibling, parts, rows, far, clusters)
     for group in (slice(0, -1), slice(-1, None)):
-        out = place(me, out, late[group], where[group], clusters)
+        out = place(out, late[group], far[group], clusters)
     modes_out = jnp.transpose(out, (1, 0, 2))[None]
     return modes_out, coefficients.T, correlations
 

time: 39.2 us -> 38.3 us (0.977)
  waiting for transfers between devices: 14.3 us -> 10.5 us
  Pallas kernels: 12.3 us -> 14.7 us
  starting transfers between devices: 11.6 us -> 12.1 us
    ppermute x12, waiting for transfers between devices: 14.3 us -> 10.5 us  [swap(): return lax.ppermute(x, axis, [(i, i ^ offset) for i in range(size)])]
    pallas_call x8 -> x9, Pallas kernels: 12.3 us -> 14.7 us  [call(): pl.pallas_call(body, in_specs=in_specs, out_specs=out_specs or [IN_VMEM]...]
    ppermute x12, starting transfers between devices: 11.6 us -> 12.1 us  [swap(): return lax.ppermute(x, axis, [(i, i ^ offset) for i in range(size)])]
  transfers between devices with their start and end apart: 12 -> 12, of which waited for: 4 -> 4; matrix products, arithmetic and copies ran while one was open for 0% -> 0% of each run, Pallas kernels for 21% -> 27%
where the time goes in v5:
time: 38.3 us; the launch traced here: 38.1 us
  Pallas kernels  14.7 us (38%)
  starting transfers between devices  12.1 us (32%)
  waiting for transfers between devices  10.5 us (27%)
  between operations  0.76 us (2%)
    pallas_call x9, Pallas kernels, call(): pl.pallas_call(body, in_specs=in_specs, out_specs=out_specs or [IN_VMEM]...  14.7 us
    ppermute x12, starting transfers between devices, swap(): return lax.ppermute(x, axis, [(i, i ^ offset) for i in range(size)])  12.1 us
    ppermute x12, waiting for transfers between devices, swap(): return lax.ppermute(x, axis, [(i, i ^ offset) for i in range(size)])  10.5 us
  transfers between devices with their start and end apart: 12, of which 4 were waited for; matrix products, arithmetic and copies ran while one was open for 0% of the time, Pallas kernels for 27%

profile of v5, /device:TPU:1, one launch (start us, length us, event | category | flops | bytes accessed | tf_op | source)
XLA Modules:
  0.0 38.1 jit_solution(10485822823896752878)
XLA Ops:
  0.6 3.6 %gram.1 = (f32[72,128]{1,0:T(8,128)S(1)}, bf16[5,32,896]{2,1,0:T(8,128)(2,1)S(1)}, bf16[5,32,896]{2,1,0:T(8,128)(2,1)S(1)}) custom-call(s32[1,128]{1,0:T(1,128)} %bitcast.8, bf16[5,128,3072]{2,1,0:T(8,128)(2,1)} %bitcast.11), custom_call_target="tpu_custom_call" | custom-call | tf_op jit(solution)/shard_map/gram/pallas_call | solution.py:22
  4.2 0.1 collective-permute-start
  4.3 2.6 %collective-permute-start.2 = (f32[72,128]{1,0:T(8,128)S(1)}, f32[72,128]{1,0:T(8,128)S(1)}, u32[]{:S(2)}, u32[]{:S(2)}) collective-permute-start(f32[72,128]{1,0:T(8,128)S(1)} %get-tuple-element.24), channel_id=1, source_target_pairs={{0,3},{1,2},{2,1},{3,0},{4,7},{5,6},{6,5},{7,4},{8,11},{9,10},{10,... | collective-permute-start | bytes 110600 | tf_op jit(solution)/shard_map/ppermute | solution.py:358
  6.9 0.1 collective-permute-start.1
  7.0 0.0 collective-permute-done
  7.0 1.4 %collective-permute-start.8 = (bf16[5,32,896]{2,1,0:T(8,128)(2,1)S(1)}, bf16[5,32,896]{2,1,0:T(8,128)(2,1)S(1)}, u32[]{:S(2)}, u32[]{:S(2)}) collective-permute-start(bf16[5,32,896]{2,1,0:T(8,128)(2,1)S(1)} %get-tuple-element.35), channel_id=1, source_target_pairs={{0,2},{1,3},{2,0},{3,1},{4,6},{5,7},{6,4},{7,5},{8,10},{9,11},{10,... | collective-permute-start | bytes 860168 | tf_op jit(solution)/shard_map/ppermute | solution.py:358
  8.4 0.7 %collective-permute-start.9 = (bf16[5,32,896]{2,1,0:T(8,128)(2,1)S(1)}, bf16[5,32,896]{2,1,0:T(8,128)(2,1)S(1)}, u32[]{:S(2)}, u32[]{:S(2)}) collective-permute-start(bf16[5,32,896]{2,1,0:T(8,128)(2,1)S(1)} %get-tuple-element.36), channel_id=1, source_target_pairs={{0,3},{1,2},{2,1},{3,0},{4,7},{5,6},{6,5},{7,4},{8,11},{9,10},{10,... | collective-permute-start | bytes 860168 | tf_op jit(solution)/shard_map/ppermute | solution.py:358
  9.1 0.0 collective-permute-done.2
  9.1 0.7 %collective-permute-done.1 = f32[72,128]{1,0:T(8,128)S(1)} collective-permute-done((f32[72,128]{1,0:T(8,128)S(1)}, f32[72,128]{1,0:T(8,128)S(1)}, u32[]{:S(2)}, u32[]{:S(2)}) %collective-permute-start.1) | collective-permute-done | bytes 36896 | tf_op jit(solution)/shard_map/ppermute | solution.py:358
  9.8 1.4 %collective-permute-start.3 = (f32[72,128]{1,0:T(8,128)S(1)}, f32[72,128]{1,0:T(8,128)S(1)}, u32[]{:S(2)}, u32[]{:S(2)}) collective-permute-start(f32[72,128]{1,0:T(8,128)S(1)} %add_add_fusion.after_ref), channel_id=1, source_target_pairs={{0,4},{4,0},{8,12},{12,8},{1,5},{5,1},{9,13},{13,9},{2,6},{6,2},{1... | collective-permute-start | bytes 110600 | tf_op jit(solution)/shard_map/ppermute | solution.py:358
  11.1 1.8 %collective-permute-done.3 = f32[72,128]{1,0:T(8,128)S(1)} collective-permute-done((f32[72,128]{1,0:T(8,128)S(1)}, f32[72,128]{1,0:T(8,128)S(1)}, u32[]{:S(2)}, u32[]{:S(2)}) %collective-permute-start.3) | collective-permute-done | bytes 36896 | tf_op jit(solution)/shard_map/ppermute | solution.py:358
  12.9 0.0 copy-start
  13.0 0.0 copy-start.1
  13.0 2.4 %collective-permute-start.4 = (f32[72,128]{1,0:T(8,128)S(1)}, f32[72,128]{1,0:T(8,128)S(1)}, u32[]{:S(2)}, u32[]{:S(2)}) collective-permute-start(f32[72,128]{1,0:T(8,128)S(1)} %add.15.first_ref), channel_id=1, source_target_pairs={{0,8},{4,12},{8,0},{12,4},{1,9},{5,13},{9,1},{13,5},{2,10},{6,14},... | collective-permute-start | bytes 110600 | tf_op jit(solution)/shard_map/ppermute | solution.py:358
  15.3 2.1 %load.2.x_ref = bf16[5,128,3072]{2,1,0:T(8,128)(2,1)S(1)} custom-call(f32[72,128]{1,0:T(8,128)S(1)} %add_add_fusion.after_ref, bf16[5,128,3072]{2,1,0:T(8,128)(2,1)} %bitcast.12), custom_call_target="tpu_custom_call" | custom-call | tf_op jit(solution)/shard_map/load/pallas_call | solution.py:22
  17.5 0.0 collective-permute-done.4.second_ref
  17.5 0.0 copy-done
  17.5 0.0 copy-done.1
  17.5 2.1 %subspace.1 = (f32[128,128]{1,0:T(8,128)S(1)}, f32[16,128]{1,0:T(8,128)S(1)}, bf16[2,16,128]{2,1,0:T(8,128)(2,1)S(1)}, bf16[16,32]{1,0:T(8,128)(2,1)S(1)}, bf16[...) custom-call(f32[72,128]{1,0:T(8,128)S(1)} %add.15.first_ref, ...), custom_call_target="tpu_custom_call" | custom-call | tf_op jit(solution)/shard_map/subspace/pallas_call | solution.py:22
  19.6 1.1 %collective-permute-start.10 = (bf16[5,16,2176]{2,1,0:T(8,128)(2,1)S(1)}, bf16[5,16,2176]{2,1,0:T(8,128)(2,1)S(1)}, u32[]{:S(2)}, u32[]{:S(2)}) collective-permute-start(bf16[5,16,2176]{2,1,0:T(8,128)(2,1)S(1)} %get-tuple-element.39), channel_id=1, source_target_pairs={{0,2},{1,3},{2,0},{3,1},{4,6},{5,7},{6,4},{7,5},{8,10},{9,11},{10,... | collective-permute-start | bytes 1044488 | tf_op jit(solution)/shard_map/ppermute | solution.py:358
  20.7 0.0 collective-permute-done.8.refs_3_
  20.7 2.1 %collective-permute-done.9.refs_4_ = bf16[5,32,896]{2,1,0:T(8,128)(2,1)S(1)} collective-permute-done((bf16[5,32,896]{2,1,0:T(8,128)(2,1)S(1)}, bf16[5,32,896]{2,1,0:T(8,128)(2,1)S(1)}, u32[]{:S(2)}, u32[]{:S(2)}) %collective-permute-start.9) | collective-permute-done | bytes 286752 | tf_op jit(solution)/shard_map/ppermute | solution.py:358
  22.7 1.8 %collective-permute-start.11 = (bf16[5,16,2176]{2,1,0:T(8,128)(2,1)S(1)}, bf16[5,16,2176]{2,1,0:T(8,128)(2,1)S(1)}, u32[]{:S(2)}, u32[]{:S(2)}) collective-permute-start(bf16[5,16,2176]{2,1,0:T(8,128)(2,1)S(1)} %get-tuple-element.40), channel_id=1, source_target_pairs={{0,3},{1,2},{2,1},{3,0},{4,7},{5,6},{6,5},{7,4},{8,11},{9,10},{10,... | collective-permute-start | bytes 1044488 | tf_op jit(solution)/shard_map/ppermute | solution.py:358
  24.5 2.1 %load.3.x_ref = bf16[5,128,3072]{2,1,0:T(8,128)(2,1)S(1)} custom-call(bf16[2,16,128]{2,1,0:T(8,128)(2,1)S(1)} %get-tuple-element.29.after_ref.near_ref, bf16[5,128,3072]{2,1,0:T(8,128)(2,1)} %bitcast.13), custom_call_target="tpu_custom_call" | custom-call | tf_op jit(solution)/shard_map/load/pallas_call | solution.py:22
  26.7 0.0 copy-start.2
  26.7 0.6 %near.1 = (bf16[5,16,3072]{2,1,0:T(8,128)(2,1)S(1)}, bf16[2,16,3072]{2,1,0:T(8,128)(2,1)S(1)}, bf16[2,16,3072]{2,1,0:T(8,128)(2,1)S(1)}, bf16[1,16,3072]{2,1,0:T(8,128)(2,1)S(1)}) custom-call(bf16[2,16,128]{2,1,0:T(8,128)(2,1)S(1)} %get-tuple-element.29.after_ref.near_ref, bf16[5,128,3072]{2,1,0:T(8,128)(2,1)S(1)} %load.3.x_ref), custom_call_target="tpu_custom_call" | custom-call | tf_op jit(solution)/shard_map/near/pallas_call | solution.py:22
  27.3 0.1 collective-permute-start.5
  27.4 0.5 %collective-permute-start.6 = (bf16[2,16,3072]{2,1,0:T(8,128)(2,1)S(1)}, bf16[2,16,3072]{2,1,0:T(8,128)(2,1)S(1)}, u32[]{:S(2)}, u32[]{:S(2)}) collective-permute-start(bf16[2,16,3072]{2,1,0:T(8,128)(2,1)S(1)} %get-tuple-element.32), channel_id=1, source_target_pairs={{0,1},{1,0},{2,3},{3,2},{4,5},{5,4},{6,7},{7,6},{8,9},{9,8},{10,11... | collective-permute-start | bytes 589832 | tf_op jit(solution)/shard_map/ppermute | solution.py:358
  27.9 0.1 collective-permute-start.7
  28.0 0.0 copy-done.2
  28.0 1.5 %small.1 = (f32[16,32]{1,0:T(8,128)}, f32[1,16,16]{2,1,0:T(8,128)}) custom-call(s32[4]{0:T(128)S(1)} %copy-done.2, f32[128,128]{1,0:T(8,128)S(1)} %get-tuple-element.41.gram_ref, s32[1,128]{1,0:T(1,128)S(1)} %bitcast.10, f32[16,128]{1,0:T(8,128)S(1)} %get-tuple-element.42.basis_ref), custom_call_target="tpu_custom_call" | custom-call | tf_op jit(solution)/shard_map/small/pallas_call | solution.py:22
  29.4 0.0 collective-permute-done.7.refs_2_
  29.4 0.0 collective-permute-done.5.refs_0_
  29.5 0.0 collective-permute-done.6.refs_1_
  29.5 1.2 %owner.1.out_in_ref = bf16[5,16,12288]{2,1,0:T(8,128)(2,1)} custom-call(bf16[16,32]{1,0:T(8,128)(2,1)S(1)} %get-tuple-element.28.own_ref, bf16[5,16,3072]{2,1,0:T(8,128)(2,1)S(1)} %get-tuple-element.30.near_ref, bf16[2,16,3072]{2,1,0:T(8,128)(2,1)S(1)} %collective-permute-done.5.refs_0_, bf16[2,16,3072]{2,1,0:T(8,128)(2,1)S(1)} %collective-permute-done.6.refs_1_, ...), custom_call_target="tpu_custom_call" | custom-call | tf_op jit(solution)/shard_map/owner/pallas_call | solution.py:22
  30.7 0.0 collective-permute-done.10.refs_0_
  30.7 0.8 %place.2.out_in_ref = bf16[5,16,12288]{2,1,0:T(8,128)(2,1)} custom-call(bf16[5,16,12288]{2,1,0:T(8,128)(2,1)} %owner.1.out_in_ref, bf16[5,16,2176]{2,1,0:T(8,128)(2,1)S(1)} %collective-permute-done.10.refs_0_), custom_call_target="tpu_custom_call", output_to_operand_aliasing={{}: (0, {})} | custom-call | tf_op jit(solution)/shard_map/place/pallas_call | solution.py:22
  31.4 5.9 %collective-permute-done.11.refs_0_ = bf16[5,16,2176]{2,1,0:T(8,128)(2,1)S(1)} collective-permute-done((bf16[5,16,2176]{2,1,0:T(8,128)(2,1)S(1)}, bf16[5,16,2176]{2,1,0:T(8,128)(2,1)S(1)}, u32[]{:S(2)}, u32[]{:S(2)}) %collective-permute-start.11) | collective-permute-done | bytes 348192 | tf_op jit(solution)/shard_map/ppermute | solution.py:358
  37.4 0.7 %place.3 = bf16[5,16,12288]{2,1,0:T(8,128)(2,1)} custom-call(bf16[5,16,12288]{2,1,0:T(8,128)(2,1)} %place.2.out_in_ref, bf16[5,16,2176]{2,1,0:T(8,128)(2,1)S(1)} %collective-permute-done.11.refs_0_), custom_call_target="tpu_custom_call", output_to_operand_aliasing={{}: (0, {})} | custom-call | tf_op jit(solution)/shard_map/place/pallas_call | solution.py:22
  (2 shorter events, 0.0 us)
Async XLA Ops:
  4.2 2.8 %collective-permute-start = (f32[72,128]{1,0:T(8,128)S(1)}, f32[72,128]{1,0:T(8,128)S(1)}, u32[]{:S(2)}, u32[]{:S(2)}) collective-permute-start(f32[72,128]{1,0:T(8,128)S(1)} %get-tuple-element.24), channel_id=1, source_target_pairs={{0,1},{1,0},{2,3},{3,2},{4,5},{5,4},{6,7},{7,6},{8,9},{9,8},{10,11... | collective-permute-start | bytes 110600 | tf_op jit(solution)/shard_map/ppermute | solution.py:358
  4.3 4.7 %collective-permute-start.2 = (f32[72,128]{1,0:T(8,128)S(1)}, f32[72,128]{1,0:T(8,128)S(1)}, u32[]{:S(2)}, u32[]{:S(2)}) collective-permute-start(f32[72,128]{1,0:T(8,128)S(1)} %get-tuple-element.24), channel_id=1, source_target_pairs={{0,3},{1,2},{2,1},{3,0},{4,7},{5,6},{6,5},{7,4},{8,11},{9,10},{10,... | collective-permute-start | bytes 110600 | tf_op jit(solution)/shard_map/ppermute | solution.py:358
  6.9 2.8 %collective-permute-start.1 = (f32[72,128]{1,0:T(8,128)S(1)}, f32[72,128]{1,0:T(8,128)S(1)}, u32[]{:S(2)}, u32[]{:S(2)}) collective-permute-start(f32[72,128]{1,0:T(8,128)S(1)} %get-tuple-element.24), channel_id=1, source_target_pairs={{0,2},{1,3},{2,0},{3,1},{4,6},{5,7},{6,4},{7,5},{8,10},{9,11},{10,... | collective-permute-start | bytes 110600 | tf_op jit(solution)/shard_map/ppermute | solution.py:358
  7.0 13.7 %collective-permute-start.8 = (bf16[5,32,896]{2,1,0:T(8,128)(2,1)S(1)}, bf16[5,32,896]{2,1,0:T(8,128)(2,1)S(1)}, u32[]{:S(2)}, u32[]{:S(2)}) collective-permute-start(bf16[5,32,896]{2,1,0:T(8,128)(2,1)S(1)} %get-tuple-element.35), channel_id=1, source_target_pairs={{0,2},{1,3},{2,0},{3,1},{4,6},{5,7},{6,4},{7,5},{8,10},{9,11},{10,... | collective-permute-start | bytes 860168 | tf_op jit(solution)/shard_map/ppermute | solution.py:358
  8.4 14.3 %collective-permute-start.9 = (bf16[5,32,896]{2,1,0:T(8,128)(2,1)S(1)}, bf16[5,32,896]{2,1,0:T(8,128)(2,1)S(1)}, u32[]{:S(2)}, u32[]{:S(2)}) collective-permute-start(bf16[5,32,896]{2,1,0:T(8,128)(2,1)S(1)} %get-tuple-element.36), channel_id=1, source_target_pairs={{0,3},{1,2},{2,1},{3,0},{4,7},{5,6},{6,5},{7,4},{8,11},{9,10},{10,... | collective-permute-start | bytes 860168 | tf_op jit(solution)/shard_map/ppermute | solution.py:358
  9.8 3.2 %collective-permute-start.3 = (f32[72,128]{1,0:T(8,128)S(1)}, f32[72,128]{1,0:T(8,128)S(1)}, u32[]{:S(2)}, u32[]{:S(2)}) collective-permute-start(f32[72,128]{1,0:T(8,128)S(1)} %add_add_fusion.after_ref), channel_id=1, source_target_pairs={{0,4},{4,0},{8,12},{12,8},{1,5},{5,1},{9,13},{13,9},{2,6},{6,2},{1... | collective-permute-start | bytes 110600 | tf_op jit(solution)/shard_map/ppermute | solution.py:358
  12.9 4.5 %copy-start = (f32[128,16]{0,1:T(8,128)S(1)}, f32[128,16]{0,1:T(8,128)}, u32[]{:S(2)}) copy-start(f32[128,16]{0,1:T(8,128)} %param.6) | copy-start | bytes 24580
  13.0 4.5 %copy-start.1 = (s32[128]{0:T(128)S(1)}, s32[128]{0:T(128)}, u32[]{:S(2)}) copy-start(s32[128]{0:T(128)} %param.5) | copy-start | bytes 1540
  13.0 4.5 %collective-permute-start.4 = (f32[72,128]{1,0:T(8,128)S(1)}, f32[72,128]{1,0:T(8,128)S(1)}, u32[]{:S(2)}, u32[]{:S(2)}) collective-permute-start(f32[72,128]{1,0:T(8,128)S(1)} %add.15.first_ref), channel_id=1, source_target_pairs={{0,8},{4,12},{8,0},{12,4},{1,9},{5,13},{9,1},{13,5},{2,10},{6,14},... | collective-permute-start | bytes 110600 | tf_op jit(solution)/shard_map/ppermute | solution.py:358
  19.6 11.1 %collective-permute-start.10 = (bf16[5,16,2176]{2,1,0:T(8,128)(2,1)S(1)}, bf16[5,16,2176]{2,1,0:T(8,128)(2,1)S(1)}, u32[]{:S(2)}, u32[]{:S(2)}) collective-permute-start(bf16[5,16,2176]{2,1,0:T(8,128)(2,1)S(1)} %get-tuple-element.39), channel_id=1, source_target_pairs={{0,2},{1,3},{2,0},{3,1},{4,6},{5,7},{6,4},{7,5},{8,10},{9,11},{10,... | collective-permute-start | bytes 1044488 | tf_op jit(solution)/shard_map/ppermute | solution.py:358
  22.7 14.6 %collective-permute-start.11 = (bf16[5,16,2176]{2,1,0:T(8,128)(2,1)S(1)}, bf16[5,16,2176]{2,1,0:T(8,128)(2,1)S(1)}, u32[]{:S(2)}, u32[]{:S(2)}) collective-permute-start(bf16[5,16,2176]{2,1,0:T(8,128)(2,1)S(1)} %get-tuple-element.40), channel_id=1, source_target_pairs={{0,3},{1,2},{2,1},{3,0},{4,7},{5,6},{6,5},{7,4},{8,11},{9,10},{10,... | collective-permute-start | bytes 1044488 | tf_op jit(solution)/shard_map/ppermute | solution.py:358
  26.7 1.3 %copy-start.2 = (s32[4]{0:T(128)S(1)}, s32[4]{0:T(128)}, u32[]{:S(2)}) copy-start(s32[4]{0:T(128)} %successor_ref.1) | copy-start | bytes 52
  27.3 2.1 %collective-permute-start.5 = (bf16[2,16,3072]{2,1,0:T(8,128)(2,1)S(1)}, bf16[2,16,3072]{2,1,0:T(8,128)(2,1)S(1)}, u32[]{:S(2)}, u32[]{:S(2)}) collective-permute-start(bf16[2,16,3072]{2,1,0:T(8,128)(2,1)S(1)} %get-tuple-element.31), channel_id=1, source_target_pairs={{0,1},{1,0},{2,3},{3,2},{4,5},{5,4},{6,7},{7,6},{8,9},{9,8},{10,11... | collective-permute-start | bytes 589832 | tf_op jit(solution)/shard_map/ppermute | solution.py:358
  27.4 2.1 %collective-permute-start.6 = (bf16[2,16,3072]{2,1,0:T(8,128)(2,1)S(1)}, bf16[2,16,3072]{2,1,0:T(8,128)(2,1)S(1)}, u32[]{:S(2)}, u32[]{:S(2)}) collective-permute-start(bf16[2,16,3072]{2,1,0:T(8,128)(2,1)S(1)} %get-tuple-element.32), channel_id=1, source_target_pairs={{0,1},{1,0},{2,3},{3,2},{4,5},{5,4},{6,7},{7,6},{8,9},{9,8},{10,11... | collective-permute-start | bytes 589832 | tf_op jit(solution)/shard_map/ppermute | solution.py:358
  27.9 1.5 %collective-permute-start.7 = (bf16[1,16,3072]{2,1,0:T(8,128)(2,1)S(1)}, bf16[1,16,3072]{2,1,0:T(8,128)(2,1)S(1)}, u32[]{:S(2)}, u32[]{:S(2)}) collective-permute-start(bf16[1,16,3072]{2,1,0:T(8,128)(2,1)S(1)} %get-tuple-element.33), channel_id=1, source_target_pairs={{0,1},{1,0},{2,3},{3,2},{4,5},{5,4},{6,7},{7,6},{8,9},{9,8},{10,11... | collective-permute-start | bytes 294920 | tf_op jit(solution)/shard_map/ppermute | solution.py:358

commit v6 on v5

--- a/solution.py
+++ b/solution.py
@@ -144,16 +144,14 @@
     inner = jnp.dot(products, same, precision=HIGH, preferred_element_type=jnp.float32)
     columns = [inner[c * modes : (c + 1) * modes] for c in range(modes)]
     row = lax.broadcasted_iota(jnp.int32, image.shape, 0)
-    scale = jnp.zeros_like(image)
     for j in range(modes):
-        pivot = columns[j][j : j + 1, :]
-        scale = jnp.where(row == j, lax.rsqrt(pivot), scale)
-        if j + 1 < modes:
-            factor = jnp.where(row > j, columns[j] * (1.0 / pivot), 0.0)
-            for c in range(j + 1, modes):
-                columns[c] = columns[c] - factor * columns[c][j : j + 1, :]
-            image = image - factor * image[j : j + 1, :]
-    return image * scale
+        scale = lax.rsqrt(columns[j][j : j + 1, :])
+        solved = image[j : j + 1, :] * scale
+        lower = jnp.where(row > j, columns[j] * scale, 0.0)
+        image = jnp.where(row == j, solved, image - lower * solved)
+        for c in range(j + 1, modes):
+            columns[c] = columns[c] - lower * lower[c : c + 1, :]
+    return image
 
 
 def subspace_body(

time: 38.3 us -> 38.3 us (level)
  no operation moved by 1% of the time
where the time goes in v6:
time: 38.3 us; the launch traced here: 38.1 us
  Pallas kernels  14.7 us (38%)
  starting transfers between devices  12.2 us (32%)
  waiting for transfers between devices  10.5 us (27%)
  between operations  0.76 us (2%)
    pallas_call x9, Pallas kernels, call(): pl.pallas_call(body, in_specs=in_specs, out_specs=out_specs or [IN_VMEM]...  14.7 us
    ppermute x12, starting transfers between devices, swap(): return lax.ppermute(x, axis, [(i, i ^ offset) for i in range(size)])  12.2 us
    ppermute x12, waiting for transfers between devices, swap(): return lax.ppermute(x, axis, [(i, i ^ offset) for i in range(size)])  10.5 us
  transfers between devices with their start and end apart: 12, of which 4 were waited for; matrix products, arithmetic and copies ran while one was open for 0% of the time, Pallas kernels for 27%

profile of v6, /device:TPU:1, one launch (start us, length us, event | category | flops | bytes accessed | tf_op | source)
XLA Modules:
  0.0 38.1 jit_solution(16311009465974365286)
XLA Ops:
  0.6 3.6 %gram.1 = (f32[72,128]{1,0:T(8,128)S(1)}, bf16[5,32,896]{2,1,0:T(8,128)(2,1)S(1)}, bf16[5,32,896]{2,1,0:T(8,128)(2,1)S(1)}) custom-call(s32[1,128]{1,0:T(1,128)} %bitcast.8, bf16[5,128,3072]{2,1,0:T(8,128)(2,1)} %bitcast.11), custom_call_target="tpu_custom_call" | custom-call | tf_op jit(solution)/shard_map/gram/pallas_call | solution.py:22
  4.2 0.1 collective-permute-start
  4.3 2.6 %collective-permute-start.2 = (f32[72,128]{1,0:T(8,128)S(1)}, f32[72,128]{1,0:T(8,128)S(1)}, u32[]{:S(2)}, u32[]{:S(2)}) collective-permute-start(f32[72,128]{1,0:T(8,128)S(1)} %get-tuple-element.24), channel_id=1, source_target_pairs={{0,3},{1,2},{2,1},{3,0},{4,7},{5,6},{6,5},{7,4},{8,11},{9,10},{10,... | collective-permute-start | bytes 110600 | tf_op jit(solution)/shard_map/ppermute | solution.py:356
  6.9 0.1 collective-permute-start.1
  7.0 0.0 collective-permute-done
  7.0 1.4 %collective-permute-start.8 = (bf16[5,32,896]{2,1,0:T(8,128)(2,1)S(1)}, bf16[5,32,896]{2,1,0:T(8,128)(2,1)S(1)}, u32[]{:S(2)}, u32[]{:S(2)}) collective-permute-start(bf16[5,32,896]{2,1,0:T(8,128)(2,1)S(1)} %get-tuple-element.35), channel_id=1, source_target_pairs={{0,2},{1,3},{2,0},{3,1},{4,6},{5,7},{6,4},{7,5},{8,10},{9,11},{10,... | collective-permute-start | bytes 860168 | tf_op jit(solution)/shard_map/ppermute | solution.py:356
  8.4 0.7 %collective-permute-start.9 = (bf16[5,32,896]{2,1,0:T(8,128)(2,1)S(1)}, bf16[5,32,896]{2,1,0:T(8,128)(2,1)S(1)}, u32[]{:S(2)}, u32[]{:S(2)}) collective-permute-start(bf16[5,32,896]{2,1,0:T(8,128)(2,1)S(1)} %get-tuple-element.36), channel_id=1, source_target_pairs={{0,3},{1,2},{2,1},{3,0},{4,7},{5,6},{6,5},{7,4},{8,11},{9,10},{10,... | collective-permute-start | bytes 860168 | tf_op jit(solution)/shard_map/ppermute | solution.py:356
  9.1 0.0 collective-permute-done.2
  9.1 0.7 %collective-permute-done.1 = f32[72,128]{1,0:T(8,128)S(1)} collective-permute-done((f32[72,128]{1,0:T(8,128)S(1)}, f32[72,128]{1,0:T(8,128)S(1)}, u32[]{:S(2)}, u32[]{:S(2)}) %collective-permute-start.1) | collective-permute-done | bytes 36896 | tf_op jit(solution)/shard_map/ppermute | solution.py:356
  9.8 1.4 %collective-permute-start.3 = (f32[72,128]{1,0:T(8,128)S(1)}, f32[72,128]{1,0:T(8,128)S(1)}, u32[]{:S(2)}, u32[]{:S(2)}) collective-permute-start(f32[72,128]{1,0:T(8,128)S(1)} %add_add_fusion.after_ref), channel_id=1, source_target_pairs={{0,4},{4,0},{8,12},{12,8},{1,5},{5,1},{9,13},{13,9},{2,6},{6,2},{1... | collective-permute-start | bytes 110600 | tf_op jit(solution)/shard_map/ppermute | solution.py:356
  11.1 1.8 %collective-permute-done.3 = f32[72,128]{1,0:T(8,128)S(1)} collective-permute-done((f32[72,128]{1,0:T(8,128)S(1)}, f32[72,128]{1,0:T(8,128)S(1)}, u32[]{:S(2)}, u32[]{:S(2)}) %collective-permute-start.3) | collective-permute-done | bytes 36896 | tf_op jit(solution)/shard_map/ppermute | solution.py:356
  12.9 0.0 copy-start
  13.0 0.0 copy-start.1
  13.0 2.4 %collective-permute-start.4 = (f32[72,128]{1,0:T(8,128)S(1)}, f32[72,128]{1,0:T(8,128)S(1)}, u32[]{:S(2)}, u32[]{:S(2)}) collective-permute-start(f32[72,128]{1,0:T(8,128)S(1)} %add.15.first_ref), channel_id=1, source_target_pairs={{0,8},{4,12},{8,0},{12,4},{1,9},{5,13},{9,1},{13,5},{2,10},{6,14},... | collective-permute-start | bytes 110600 | tf_op jit(solution)/shard_map/ppermute | solution.py:356
  15.3 2.1 %load.2.x_ref = bf16[5,128,3072]{2,1,0:T(8,128)(2,1)S(1)} custom-call(f32[72,128]{1,0:T(8,128)S(1)} %add_add_fusion.after_ref, bf16[5,128,3072]{2,1,0:T(8,128)(2,1)} %bitcast.12), custom_call_target="tpu_custom_call" | custom-call | tf_op jit(solution)/shard_map/load/pallas_call | solution.py:22
  17.5 0.0 collective-permute-done.4.second_ref
  17.5 0.0 copy-done
  17.5 0.0 copy-done.1
  17.5 2.1 %subspace.1 = (f32[128,128]{1,0:T(8,128)S(1)}, f32[16,128]{1,0:T(8,128)S(1)}, bf16[2,16,128]{2,1,0:T(8,128)(2,1)S(1)}, bf16[16,32]{1,0:T(8,128)(2,1)S(1)}, bf16[...) custom-call(f32[72,128]{1,0:T(8,128)S(1)} %add.15.first_ref, ...), custom_call_target="tpu_custom_call" | custom-call | tf_op jit(solution)/shard_map/subspace/pallas_call | solution.py:22
  19.6 1.1 %collective-permute-start.10 = (bf16[5,16,2176]{2,1,0:T(8,128)(2,1)S(1)}, bf16[5,16,2176]{2,1,0:T(8,128)(2,1)S(1)}, u32[]{:S(2)}, u32[]{:S(2)}) collective-permute-start(bf16[5,16,2176]{2,1,0:T(8,128)(2,1)S(1)} %get-tuple-element.39), channel_id=1, source_target_pairs={{0,2},{1,3},{2,0},{3,1},{4,6},{5,7},{6,4},{7,5},{8,10},{9,11},{10,... | collective-permute-start | bytes 1044488 | tf_op jit(solution)/shard_map/ppermute | solution.py:356
  20.7 0.0 collective-permute-done.8.refs_3_
  20.7 2.0 %collective-permute-done.9.refs_4_ = bf16[5,32,896]{2,1,0:T(8,128)(2,1)S(1)} collective-permute-done((bf16[5,32,896]{2,1,0:T(8,128)(2,1)S(1)}, bf16[5,32,896]{2,1,0:T(8,128)(2,1)S(1)}, u32[]{:S(2)}, u32[]{:S(2)}) %collective-permute-start.9) | collective-permute-done | bytes 286752 | tf_op jit(solution)/shard_map/ppermute | solution.py:356
  22.7 1.8 %collective-permute-start.11 = (bf16[5,16,2176]{2,1,0:T(8,128)(2,1)S(1)}, bf16[5,16,2176]{2,1,0:T(8,128)(2,1)S(1)}, u32[]{:S(2)}, u32[]{:S(2)}) collective-permute-start(bf16[5,16,2176]{2,1,0:T(8,128)(2,1)S(1)} %get-tuple-element.40), channel_id=1, source_target_pairs={{0,3},{1,2},{2,1},{3,0},{4,7},{5,6},{6,5},{7,4},{8,11},{9,10},{10,... | collective-permute-start | bytes 1044488 | tf_op jit(solution)/shard_map/ppermute | solution.py:356
  24.5 2.1 %load.3.x_ref = bf16[5,128,3072]{2,1,0:T(8,128)(2,1)S(1)} custom-call(bf16[2,16,128]{2,1,0:T(8,128)(2,1)S(1)} %get-tuple-element.29.after_ref.near_ref, bf16[5,128,3072]{2,1,0:T(8,128)(2,1)} %bitcast.13), custom_call_target="tpu_custom_call" | custom-call | tf_op jit(solution)/shard_map/load/pallas_call | solution.py:22
  26.7 0.0 copy-start.2
  26.7 0.6 %near.1 = (bf16[5,16,3072]{2,1,0:T(8,128)(2,1)S(1)}, bf16[2,16,3072]{2,1,0:T(8,128)(2,1)S(1)}, bf16[2,16,3072]{2,1,0:T(8,128)(2,1)S(1)}, bf16[1,16,3072]{2,1,0:T(8,128)(2,1)S(1)}) custom-call(bf16[2,16,128]{2,1,0:T(8,128)(2,1)S(1)} %get-tuple-element.29.after_ref.near_ref, bf16[5,128,3072]{2,1,0:T(8,128)(2,1)S(1)} %load.3.x_ref), custom_call_target="tpu_custom_call" | custom-call | tf_op jit(solution)/shard_map/near/pallas_call | solution.py:22
  27.3 0.1 collective-permute-start.5
  27.4 0.5 %collective-permute-start.6 = (bf16[2,16,3072]{2,1,0:T(8,128)(2,1)S(1)}, bf16[2,16,3072]{2,1,0:T(8,128)(2,1)S(1)}, u32[]{:S(2)}, u32[]{:S(2)}) collective-permute-start(bf16[2,16,3072]{2,1,0:T(8,128)(2,1)S(1)} %get-tuple-element.32), channel_id=1, source_target_pairs={{0,1},{1,0},{2,3},{3,2},{4,5},{5,4},{6,7},{7,6},{8,9},{9,8},{10,11... | collective-permute-start | bytes 589832 | tf_op jit(solution)/shard_map/ppermute | solution.py:356
  27.9 0.1 collective-permute-start.7
  28.0 0.0 copy-done.2
  28.0 1.5 %small.1 = (f32[16,32]{1,0:T(8,128)}, f32[1,16,16]{2,1,0:T(8,128)}) custom-call(s32[4]{0:T(128)S(1)} %copy-done.2, f32[128,128]{1,0:T(8,128)S(1)} %get-tuple-element.41.gram_ref, s32[1,128]{1,0:T(1,128)S(1)} %bitcast.10, f32[16,128]{1,0:T(8,128)S(1)} %get-tuple-element.42.basis_ref), custom_call_target="tpu_custom_call" | custom-call | tf_op jit(solution)/shard_map/small/pallas_call | solution.py:22
  29.4 0.0 collective-permute-done.7.refs_2_
  29.4 0.0 collective-permute-done.5.refs_0_
  29.5 0.0 collective-permute-done.6.refs_1_
  29.5 1.2 %owner.1.out_in_ref = bf16[5,16,12288]{2,1,0:T(8,128)(2,1)} custom-call(bf16[16,32]{1,0:T(8,128)(2,1)S(1)} %get-tuple-element.28.own_ref, bf16[5,16,3072]{2,1,0:T(8,128)(2,1)S(1)} %get-tuple-element.30.near_ref, bf16[2,16,3072]{2,1,0:T(8,128)(2,1)S(1)} %collective-permute-done.5.refs_0_, bf16[2,16,3072]{2,1,0:T(8,128)(2,1)S(1)} %collective-permute-done.6.refs_1_, ...), custom_call_target="tpu_custom_call" | custom-call | tf_op jit(solution)/shard_map/owner/pallas_call | solution.py:22
  30.7 0.0 collective-permute-done.10.refs_0_
  30.7 0.8 %place.2.out_in_ref = bf16[5,16,12288]{2,1,0:T(8,128)(2,1)} custom-call(bf16[5,16,12288]{2,1,0:T(8,128)(2,1)} %owner.1.out_in_ref, bf16[5,16,2176]{2,1,0:T(8,128)(2,1)S(1)} %collective-permute-done.10.refs_0_), custom_call_target="tpu_custom_call", output_to_operand_aliasing={{}: (0, {})} | custom-call | tf_op jit(solution)/shard_map/place/pallas_call | solution.py:22
  31.4 5.9 %collective-permute-done.11.refs_0_ = bf16[5,16,2176]{2,1,0:T(8,128)(2,1)S(1)} collective-permute-done((bf16[5,16,2176]{2,1,0:T(8,128)(2,1)S(1)}, bf16[5,16,2176]{2,1,0:T(8,128)(2,1)S(1)}, u32[]{:S(2)}, u32[]{:S(2)}) %collective-permute-start.11) | collective-permute-done | bytes 348192 | tf_op jit(solution)/shard_map/ppermute | solution.py:356
  37.4 0.7 %place.3 = bf16[5,16,12288]{2,1,0:T(8,128)(2,1)} custom-call(bf16[5,16,12288]{2,1,0:T(8,128)(2,1)} %place.2.out_in_ref, bf16[5,16,2176]{2,1,0:T(8,128)(2,1)S(1)} %collective-permute-done.11.refs_0_), custom_call_target="tpu_custom_call", output_to_operand_aliasing={{}: (0, {})} | custom-call | tf_op jit(solution)/shard_map/place/pallas_call | solution.py:22
  (2 shorter events, 0.0 us)
Async XLA Ops:
  4.2 2.8 %collective-permute-start = (f32[72,128]{1,0:T(8,128)S(1)}, f32[72,128]{1,0:T(8,128)S(1)}, u32[]{:S(2)}, u32[]{:S(2)}) collective-permute-start(f32[72,128]{1,0:T(8,128)S(1)} %get-tuple-element.24), channel_id=1, source_target_pairs={{0,1},{1,0},{2,3},{3,2},{4,5},{5,4},{6,7},{7,6},{8,9},{9,8},{10,11... | collective-permute-start | bytes 110600 | tf_op jit(solution)/shard_map/ppermute | solution.py:356
  4.3 4.7 %collective-permute-start.2 = (f32[72,128]{1,0:T(8,128)S(1)}, f32[72,128]{1,0:T(8,128)S(1)}, u32[]{:S(2)}, u32[]{:S(2)}) collective-permute-start(f32[72,128]{1,0:T(8,128)S(1)} %get-tuple-element.24), channel_id=1, source_target_pairs={{0,3},{1,2},{2,1},{3,0},{4,7},{5,6},{6,5},{7,4},{8,11},{9,10},{10,... | collective-permute-start | bytes 110600 | tf_op jit(solution)/shard_map/ppermute | solution.py:356
  6.9 2.8 %collective-permute-start.1 = (f32[72,128]{1,0:T(8,128)S(1)}, f32[72,128]{1,0:T(8,128)S(1)}, u32[]{:S(2)}, u32[]{:S(2)}) collective-permute-start(f32[72,128]{1,0:T(8,128)S(1)} %get-tuple-element.24), channel_id=1, source_target_pairs={{0,2},{1,3},{2,0},{3,1},{4,6},{5,7},{6,4},{7,5},{8,10},{9,11},{10,... | collective-permute-start | bytes 110600 | tf_op jit(solution)/shard_map/ppermute | solution.py:356
  7.0 13.7 %collective-permute-start.8 = (bf16[5,32,896]{2,1,0:T(8,128)(2,1)S(1)}, bf16[5,32,896]{2,1,0:T(8,128)(2,1)S(1)}, u32[]{:S(2)}, u32[]{:S(2)}) collective-permute-start(bf16[5,32,896]{2,1,0:T(8,128)(2,1)S(1)} %get-tuple-element.35), channel_id=1, source_target_pairs={{0,2},{1,3},{2,0},{3,1},{4,6},{5,7},{6,4},{7,5},{8,10},{9,11},{10,... | collective-permute-start | bytes 860168 | tf_op jit(solution)/shard_map/ppermute | solution.py:356
  8.4 14.3 %collective-permute-start.9 = (bf16[5,32,896]{2,1,0:T(8,128)(2,1)S(1)}, bf16[5,32,896]{2,1,0:T(8,128)(2,1)S(1)}, u32[]{:S(2)}, u32[]{:S(2)}) collective-permute-start(bf16[5,32,896]{2,1,0:T(8,128)(2,1)S(1)} %get-tuple-element.36), channel_id=1, source_target_pairs={{0,3},{1,2},{2,1},{3,0},{4,7},{5,6},{6,5},{7,4},{8,11},{9,10},{10,... | collective-permute-start | bytes 860168 | tf_op jit(solution)/shard_map/ppermute | solution.py:356
  9.8 3.2 %collective-permute-start.3 = (f32[72,128]{1,0:T(8,128)S(1)}, f32[72,128]{1,0:T(8,128)S(1)}, u32[]{:S(2)}, u32[]{:S(2)}) collective-permute-start(f32[72,128]{1,0:T(8,128)S(1)} %add_add_fusion.after_ref), channel_id=1, source_target_pairs={{0,4},{4,0},{8,12},{12,8},{1,5},{5,1},{9,13},{13,9},{2,6},{6,2},{1... | collective-permute-start | bytes 110600 | tf_op jit(solution)/shard_map/ppermute | solution.py:356
  12.9 4.5 %copy-start = (f32[128,16]{0,1:T(8,128)S(1)}, f32[128,16]{0,1:T(8,128)}, u32[]{:S(2)}) copy-start(f32[128,16]{0,1:T(8,128)} %param.6) | copy-start | bytes 24580
  13.0 4.5 %copy-start.1 = (s32[128]{0:T(128)S(1)}, s32[128]{0:T(128)}, u32[]{:S(2)}) copy-start(s32[128]{0:T(128)} %param.5) | copy-start | bytes 1540
  13.0 4.5 %collective-permute-start.4 = (f32[72,128]{1,0:T(8,128)S(1)}, f32[72,128]{1,0:T(8,128)S(1)}, u32[]{:S(2)}, u32[]{:S(2)}) collective-permute-start(f32[72,128]{1,0:T(8,128)S(1)} %add.15.first_ref), channel_id=1, source_target_pairs={{0,8},{4,12},{8,0},{12,4},{1,9},{5,13},{9,1},{13,5},{2,10},{6,14},... | collective-permute-start | bytes 110600 | tf_op jit(solution)/shard_map/ppermute | solution.py:356
  19.6 11.1 %collective-permute-start.10 = (bf16[5,16,2176]{2,1,0:T(8,128)(2,1)S(1)}, bf16[5,16,2176]{2,1,0:T(8,128)(2,1)S(1)}, u32[]{:S(2)}, u32[]{:S(2)}) collective-permute-start(bf16[5,16,2176]{2,1,0:T(8,128)(2,1)S(1)} %get-tuple-element.39), channel_id=1, source_target_pairs={{0,2},{1,3},{2,0},{3,1},{4,6},{5,7},{6,4},{7,5},{8,10},{9,11},{10,... | collective-permute-start | bytes 1044488 | tf_op jit(solution)/shard_map/ppermute | solution.py:356
  22.7 14.6 %collective-permute-start.11 = (bf16[5,16,2176]{2,1,0:T(8,128)(2,1)S(1)}, bf16[5,16,2176]{2,1,0:T(8,128)(2,1)S(1)}, u32[]{:S(2)}, u32[]{:S(2)}) collective-permute-start(bf16[5,16,2176]{2,1,0:T(8,128)(2,1)S(1)} %get-tuple-element.40), channel_id=1, source_target_pairs={{0,3},{1,2},{2,1},{3,0},{4,7},{5,6},{6,5},{7,4},{8,11},{9,10},{10,... | collective-permute-start | bytes 1044488 | tf_op jit(solution)/shard_map/ppermute | solution.py:356
  26.7 1.3 %copy-start.2 = (s32[4]{0:T(128)S(1)}, s32[4]{0:T(128)}, u32[]{:S(2)}) copy-start(s32[4]{0:T(128)} %successor_ref.1) | copy-start | bytes 52
  27.3 2.1 %collective-permute-start.5 = (bf16[2,16,3072]{2,1,0:T(8,128)(2,1)S(1)}, bf16[2,16,3072]{2,1,0:T(8,128)(2,1)S(1)}, u32[]{:S(2)}, u32[]{:S(2)}) collective-permute-start(bf16[2,16,3072]{2,1,0:T(8,128)(2,1)S(1)} %get-tuple-element.31), channel_id=1, source_target_pairs={{0,1},{1,0},{2,3},{3,2},{4,5},{5,4},{6,7},{7,6},{8,9},{9,8},{10,11... | collective-permute-start | bytes 589832 | tf_op jit(solution)/shard_map/ppermute | solution.py:356
  27.4 2.1 %collective-permute-start.6 = (bf16[2,16,3072]{2,1,0:T(8,128)(2,1)S(1)}, bf16[2,16,3072]{2,1,0:T(8,128)(2,1)S(1)}, u32[]{:S(2)}, u32[]{:S(2)}) collective-permute-start(bf16[2,16,3072]{2,1,0:T(8,128)(2,1)S(1)} %get-tuple-element.32), channel_id=1, source_target_pairs={{0,1},{1,0},{2,3},{3,2},{4,5},{5,4},{6,7},{7,6},{8,9},{9,8},{10,11... | collective-permute-start | bytes 589832 | tf_op jit(solution)/shard_map/ppermute | solution.py:356
  27.9 1.5 %collective-permute-start.7 = (bf16[1,16,3072]{2,1,0:T(8,128)(2,1)S(1)}, bf16[1,16,3072]{2,1,0:T(8,128)(2,1)S(1)}, u32[]{:S(2)}, u32[]{:S(2)}) collective-permute-start(bf16[1,16,3072]{2,1,0:T(8,128)(2,1)S(1)} %get-tuple-element.33), channel_id=1, source_target_pairs={{0,1},{1,0},{2,3},{3,2},{4,5},{5,4},{6,7},{7,6},{8,9},{9,8},{10,11... | collective-permute-start | bytes 294920 | tf_op jit(solution)/shard_map/ppermute | solution.py:356

commit v7 on v6

--- a/solution.py
+++ b/solution.py
@@ -140,9 +140,19 @@
 
 def orthonormal(image, same):
     modes = image.shape[0]
-    products = jnp.concatenate([image * image[c : c + 1, :] for c in range(modes)], axis=0)
+    firsts = [c // 8 * 8 for c in range(modes)]
+    products = jnp.concatenate(
+        [image[first:] * image[c : c + 1, :] for c, first in enumerate(firsts)], axis=0
+    )
     inner = jnp.dot(products, same, precision=HIGH, preferred_element_type=jnp.float32)
-    columns = [inner[c * modes : (c + 1) * modes] for c in range(modes)]
+    columns = []
+    at = 0
+    for first in firsts:
+        column = inner[at : at + modes - first]
+        at += modes - first
+        columns.append(
+            jnp.concatenate([jnp.zeros_like(image[:first]), column], axis=0) if first else column
+        )
     row = lax.broadcasted_iota(jnp.int32, image.shape, 0)
     for j in range(modes):
         scale = lax.rsqrt(columns[j][j : j + 1, :])
@@ -155,7 +165,7 @@
 
 
 def subspace_body(
-    first_ref, second_ref, row_ref, start_ref, x_ref, gram_ref, basis_ref, near_ref, own_ref, *late_refs, total_rows
+    first_ref, second_ref, row_ref, start_ref, x_ref, gram_ref, basis_ref, near_ref, own_ref, *late_refs, total_rows, far
 ):
     row_labels = row_ref[...]
     together = same_cluster(row_labels)
@@ -175,7 +185,7 @@
     for k in range(2):
         near_ref[k] = jnp.where(row_labels == (me ^ k), rounded, 0.0).astype(jnp.bfloat16)
     left = jnp.concatenate(
-        [jnp.where(row_labels == (me ^ (k + 2)), rounded, 0.0) for k in range(len(late_refs))], axis=0
+        [jnp.where(row_labels == (me ^ k), rounded, 0.0) for k in far], axis=0
     ).astype(jnp.bfloat16)
     begin = x_ref.shape[2] - late_refs[0].shape[2]
     modes = rounded.shape[0]
@@ -190,12 +200,12 @@
     ).astype(jnp.bfloat16)
 
 
-def subspace(first, second, labels, start, x, total_rows, clusters, slots, early):
+def subspace(first, second, labels, start, x, total_rows, far, slots, early):
     modes, count = start.shape
     variables, _, cells = x.shape
     late = pltpu.VMEM((variables, modes, cells - early), jnp.bfloat16)
     gram, basis, near, own, *late = call(
-        functools.partial(subspace_body, total_rows=total_rows),
+        functools.partial(subspace_body, total_rows=total_rows, far=far),
         "subspace",
         [IN_VMEM] * 5,
         [
@@ -204,7 +214,7 @@
             pltpu.VMEM((2, modes, count), jnp.bfloat16),
             pltpu.VMEM((modes, slots), jnp.bfloat16),
         ]
-        + [late] * (clusters - 2),
+        + [late] * len(far),
         first,
         second,
         labels,
@@ -370,7 +380,7 @@
     gram, *picked = partial_gram(labels_hbm, x_hbm, far, slots, EARLY)
     terms = [gram] + [swap(gram, "clus", k) for k in range(1, clusters)]
     terms[1], *picked = lax.optimization_barrier((terms[1], *picked))
-    rows = [swap(piece, "clus", k) for piece, k in zip(picked, far)]
+    rows = [swap(piece, "clus", k) for piece, k in zip(picked[::-1], far[::-1])][::-1]
     while len(terms) > 1:
         terms = [a + b for a, b in zip(terms[::2], terms[1::2])]
     gram = terms[0]
@@ -380,10 +390,10 @@
             gram = gram + other
         other = swap(gram, "space", 1 << b)
     gram, basis, near, own, late = subspace(
-        gram, other, labels, start.T, x, total_rows, clusters, slots, EARLY
-    )
-    both = lax.optimization_barrier((late[-1], *rows))
-    late[-1], rows = both[0], both[1:]
+        gram, other, labels, start.T, x, total_rows, far, slots, EARLY
+    )
+    both = lax.optimization_barrier((late[-1], *rows[::-1]))
+    late[-1], rows = both[0], both[:0:-1]
     late = [swap(piece, "clus", k) for piece, k in zip(late, far)]
     parts = tuple(range(0, variables, 2))
     own_piece, sibling = near_modes(near, load(near, x_hbm), parts)

time: 38.3 us -> 38.3 us (level)
  starting transfers between devices: 12.2 us -> 12.6 us
  waiting for transfers between devices: 10.5 us -> 10.1 us
    ppermute x12, starting transfers between devices: 12.2 us -> 12.6 us  [swap(): return lax.ppermute(x, axis, [(i, i ^ offset) for i in range(size)])]
where the time goes in v7:
time: 38.3 us; the launch traced here: 38.1 us
  Pallas kernels  14.6 us (38%)
  starting transfers between devices  12.6 us (33%)
  waiting for transfers between devices  10.1 us (26%)
  between operations  0.76 us (2%)
    pallas_call x9, Pallas kernels, call(): pl.pallas_call(body, in_specs=in_specs, out_specs=out_specs or [IN_VMEM]...  14.6 us
    ppermute x12, starting transfers between devices, swap(): return lax.ppermute(x, axis, [(i, i ^ offset) for i in range(size)])  12.6 us
    ppermute x12, waiting for transfers between devices, swap(): return lax.ppermute(x, axis, [(i, i ^ offset) for i in range(size)])  10.1 us
  transfers between devices with their start and end apart: 12, of which 4 were waited for; matrix products, arithmetic and copies ran while one was open for 0% of the time, Pallas kernels for 27%

profile of v7, /device:TPU:1, one launch (start us, length us, event | category | flops | bytes accessed | tf_op | source)
XLA Modules:
  0.0 38.1 jit_solution(6951882046451758467)
XLA Ops:
  0.6 3.6 %gram.1 = (f32[72,128]{1,0:T(8,128)S(1)}, bf16[5,32,896]{2,1,0:T(8,128)(2,1)S(1)}, bf16[5,32,896]{2,1,0:T(8,128)(2,1)S(1)}) custom-call(s32[1,128]{1,0:T(1,128)} %bitcast.8, bf16[5,128,3072]{2,1,0:T(8,128)(2,1)} %bitcast.11), custom_call_target="tpu_custom_call" | custom-call | tf_op jit(solution)/shard_map/gram/pallas_call | solution.py:22
  4.2 0.1 collective-permute-start
  4.3 2.6 %collective-permute-start.2 = (f32[72,128]{1,0:T(8,128)S(1)}, f32[72,128]{1,0:T(8,128)S(1)}, u32[]{:S(2)}, u32[]{:S(2)}) collective-permute-start(f32[72,128]{1,0:T(8,128)S(1)} %get-tuple-element.24), channel_id=1, source_target_pairs={{0,3},{1,2},{2,1},{3,0},{4,7},{5,6},{6,5},{7,4},{8,11},{9,10},{10,... | collective-permute-start | bytes 110600 | tf_op jit(solution)/shard_map/ppermute | solution.py:366
  6.9 0.1 collective-permute-start.1
  7.0 0.0 collective-permute-done
  7.0 2.0 %collective-permute-start.8 = (bf16[5,32,896]{2,1,0:T(8,128)(2,1)S(1)}, bf16[5,32,896]{2,1,0:T(8,128)(2,1)S(1)}, u32[]{:S(2)}, u32[]{:S(2)}) collective-permute-start(bf16[5,32,896]{2,1,0:T(8,128)(2,1)S(1)} %get-tuple-element.35), channel_id=1, source_target_pairs={{0,3},{1,2},{2,1},{3,0},{4,7},{5,6},{6,5},{7,4},{8,11},{9,10},{10,... | collective-permute-start | bytes 860168 | tf_op jit(solution)/shard_map/ppermute | solution.py:366
  9.0 0.0 collective-permute-start.9
  9.0 0.0 collective-permute-done.2
  9.0 0.7 %collective-permute-done.1 = f32[72,128]{1,0:T(8,128)S(1)} collective-permute-done((f32[72,128]{1,0:T(8,128)S(1)}, f32[72,128]{1,0:T(8,128)S(1)}, u32[]{:S(2)}, u32[]{:S(2)}) %collective-permute-start.1) | collective-permute-done | bytes 36896 | tf_op jit(solution)/shard_map/ppermute | solution.py:366
  9.8 1.4 %collective-permute-start.3 = (f32[72,128]{1,0:T(8,128)S(1)}, f32[72,128]{1,0:T(8,128)S(1)}, u32[]{:S(2)}, u32[]{:S(2)}) collective-permute-start(f32[72,128]{1,0:T(8,128)S(1)} %add_add_fusion.after_ref), channel_id=1, source_target_pairs={{0,4},{4,0},{8,12},{12,8},{1,5},{5,1},{9,13},{13,9},{2,6},{6,2},{1... | collective-permute-start | bytes 110600 | tf_op jit(solution)/shard_map/ppermute | solution.py:366
  11.1 1.8 %collective-permute-done.3 = f32[72,128]{1,0:T(8,128)S(1)} collective-permute-done((f32[72,128]{1,0:T(8,128)S(1)}, f32[72,128]{1,0:T(8,128)S(1)}, u32[]{:S(2)}, u32[]{:S(2)}) %collective-permute-start.3) | collective-permute-done | bytes 36896 | tf_op jit(solution)/shard_map/ppermute | solution.py:366
  12.9 0.0 copy-start
  13.0 0.0 copy-start.1
  13.0 2.4 %collective-permute-start.4 = (f32[72,128]{1,0:T(8,128)S(1)}, f32[72,128]{1,0:T(8,128)S(1)}, u32[]{:S(2)}, u32[]{:S(2)}) collective-permute-start(f32[72,128]{1,0:T(8,128)S(1)} %add.15.first_ref), channel_id=1, source_target_pairs={{0,8},{4,12},{8,0},{12,4},{1,9},{5,13},{9,1},{13,5},{2,10},{6,14},... | collective-permute-start | bytes 110600 | tf_op jit(solution)/shard_map/ppermute | solution.py:366
  15.3 2.1 %load.2.x_ref = bf16[5,128,3072]{2,1,0:T(8,128)(2,1)S(1)} custom-call(f32[72,128]{1,0:T(8,128)S(1)} %add_add_fusion.after_ref, bf16[5,128,3072]{2,1,0:T(8,128)(2,1)} %bitcast.12), custom_call_target="tpu_custom_call" | custom-call | tf_op jit(solution)/shard_map/load/pallas_call | solution.py:22
  17.5 0.0 collective-permute-done.4.second_ref
  17.5 0.0 copy-done
  17.5 0.0 copy-done.1
  17.5 2.0 %subspace.1 = (f32[128,128]{1,0:T(8,128)S(1)}, f32[16,128]{1,0:T(8,128)S(1)}, bf16[2,16,128]{2,1,0:T(8,128)(2,1)S(1)}, bf16[16,32]{1,0:T(8,128)(2,1)S(1)}, bf16[...) custom-call(f32[72,128]{1,0:T(8,128)S(1)} %add.15.first_ref, ...), custom_call_target="tpu_custom_call" | custom-call | tf_op jit(solution)/shard_map/subspace/pallas_call | solution.py:22
  19.5 0.9 %collective-permute-start.10 = (bf16[5,16,2176]{2,1,0:T(8,128)(2,1)S(1)}, bf16[5,16,2176]{2,1,0:T(8,128)(2,1)S(1)}, u32[]{:S(2)}, u32[]{:S(2)}) collective-permute-start(bf16[5,16,2176]{2,1,0:T(8,128)(2,1)S(1)} %get-tuple-element.39), channel_id=1, source_target_pairs={{0,2},{1,3},{2,0},{3,1},{4,6},{5,7},{6,4},{7,5},{8,10},{9,11},{10,... | collective-permute-start | bytes 1044488 | tf_op jit(solution)/shard_map/ppermute | solution.py:366
  20.3 0.0 collective-permute-done.8.refs_4_
  20.4 1.5 %collective-permute-done.9.refs_3_ = bf16[5,32,896]{2,1,0:T(8,128)(2,1)S(1)} collective-permute-done((bf16[5,32,896]{2,1,0:T(8,128)(2,1)S(1)}, bf16[5,32,896]{2,1,0:T(8,128)(2,1)S(1)}, u32[]{:S(2)}, u32[]{:S(2)}) %collective-permute-start.9) | collective-permute-done | bytes 286752 | tf_op jit(solution)/shard_map/ppermute | solution.py:366
  21.8 2.6 %collective-permute-start.11 = (bf16[5,16,2176]{2,1,0:T(8,128)(2,1)S(1)}, bf16[5,16,2176]{2,1,0:T(8,128)(2,1)S(1)}, u32[]{:S(2)}, u32[]{:S(2)}) collective-permute-start(bf16[5,16,2176]{2,1,0:T(8,128)(2,1)S(1)} %get-tuple-element.40), channel_id=1, source_target_pairs={{0,3},{1,2},{2,1},{3,0},{4,7},{5,6},{6,5},{7,4},{8,11},{9,10},{10,... | collective-permute-start | bytes 1044488 | tf_op jit(solution)/shard_map/ppermute | solution.py:366
  24.4 2.1 %load.3.x_ref = bf16[5,128,3072]{2,1,0:T(8,128)(2,1)S(1)} custom-call(bf16[2,16,128]{2,1,0:T(8,128)(2,1)S(1)} %get-tuple-element.29.after_ref.near_ref, bf16[5,128,3072]{2,1,0:T(8,128)(2,1)} %bitcast.13), custom_call_target="tpu_custom_call" | custom-call | tf_op jit(solution)/shard_map/load/pallas_call | solution.py:22
  26.5 0.0 copy-start.2
  26.6 0.6 %near.1 = (bf16[5,16,3072]{2,1,0:T(8,128)(2,1)S(1)}, bf16[2,16,3072]{2,1,0:T(8,128)(2,1)S(1)}, bf16[2,16,3072]{2,1,0:T(8,128)(2,1)S(1)}, bf16[1,16,3072]{2,1,0:T(8,128)(2,1)S(1)}) custom-call(bf16[2,16,128]{2,1,0:T(8,128)(2,1)S(1)} %get-tuple-element.29.after_ref.near_ref, bf16[5,128,3072]{2,1,0:T(8,128)(2,1)S(1)} %load.3.x_ref), custom_call_target="tpu_custom_call" | custom-call | tf_op jit(solution)/shard_map/near/pallas_call | solution.py:22
  27.2 0.1 collective-permute-start.5
  27.3 0.5 %collective-permute-start.6 = (bf16[2,16,3072]{2,1,0:T(8,128)(2,1)S(1)}, bf16[2,16,3072]{2,1,0:T(8,128)(2,1)S(1)}, u32[]{:S(2)}, u32[]{:S(2)}) collective-permute-start(bf16[2,16,3072]{2,1,0:T(8,128)(2,1)S(1)} %get-tuple-element.32), channel_id=1, source_target_pairs={{0,1},{1,0},{2,3},{3,2},{4,5},{5,4},{6,7},{7,6},{8,9},{9,8},{10,11... | collective-permute-start | bytes 589832 | tf_op jit(solution)/shard_map/ppermute | solution.py:366
  27.8 0.1 collective-permute-start.7
  27.9 0.0 copy-done.2
  27.9 1.5 %small.1 = (f32[16,32]{1,0:T(8,128)}, f32[1,16,16]{2,1,0:T(8,128)}) custom-call(s32[4]{0:T(128)S(1)} %copy-done.2, f32[128,128]{1,0:T(8,128)S(1)} %get-tuple-element.41.gram_ref, s32[1,128]{1,0:T(1,128)S(1)} %bitcast.10, f32[16,128]{1,0:T(8,128)S(1)} %get-tuple-element.42.basis_ref), custom_call_target="tpu_custom_call" | custom-call | tf_op jit(solution)/shard_map/small/pallas_call | solution.py:22
  29.3 0.0 collective-permute-done.7.refs_2_
  29.3 0.0 collective-permute-done.5.refs_0_
  29.3 0.0 collective-permute-done.6.refs_1_
  29.3 1.2 %owner.1.out_in_ref = bf16[5,16,12288]{2,1,0:T(8,128)(2,1)} custom-call(bf16[16,32]{1,0:T(8,128)(2,1)S(1)} %get-tuple-element.28.own_ref, bf16[5,16,3072]{2,1,0:T(8,128)(2,1)S(1)} %get-tuple-element.30.near_ref, bf16[2,16,3072]{2,1,0:T(8,128)(2,1)S(1)} %collective-permute-done.5.refs_0_, bf16[2,16,3072]{2,1,0:T(8,128)(2,1)S(1)} %collective-permute-done.6.refs_1_, ...), custom_call_target="tpu_custom_call" | custom-call | tf_op jit(solution)/shard_map/owner/pallas_call | solution.py:22
  30.5 0.0 collective-permute-done.10.refs_0_
  30.5 0.8 %place.2.out_in_ref = bf16[5,16,12288]{2,1,0:T(8,128)(2,1)} custom-call(bf16[5,16,12288]{2,1,0:T(8,128)(2,1)} %owner.1.out_in_ref, bf16[5,16,2176]{2,1,0:T(8,128)(2,1)S(1)} %collective-permute-done.10.refs_0_), custom_call_target="tpu_custom_call", output_to_operand_aliasing={{}: (0, {})} | custom-call | tf_op jit(solution)/shard_map/place/pallas_call | solution.py:22
  31.3 6.1 %collective-permute-done.11.refs_0_ = bf16[5,16,2176]{2,1,0:T(8,128)(2,1)S(1)} collective-permute-done((bf16[5,16,2176]{2,1,0:T(8,128)(2,1)S(1)}, bf16[5,16,2176]{2,1,0:T(8,128)(2,1)S(1)}, u32[]{:S(2)}, u32[]{:S(2)}) %collective-permute-start.11) | collective-permute-done | bytes 348192 | tf_op jit(solution)/shard_map/ppermute | solution.py:366
  37.4 0.7 %place.3 = bf16[5,16,12288]{2,1,0:T(8,128)(2,1)} custom-call(bf16[5,16,12288]{2,1,0:T(8,128)(2,1)} %place.2.out_in_ref, bf16[5,16,2176]{2,1,0:T(8,128)(2,1)S(1)} %collective-permute-done.11.refs_0_), custom_call_target="tpu_custom_call", output_to_operand_aliasing={{}: (0, {})} | custom-call | tf_op jit(solution)/shard_map/place/pallas_call | solution.py:22
  (2 shorter events, 0.0 us)
Async XLA Ops:
  4.2 2.8 %collective-permute-start = (f32[72,128]{1,0:T(8,128)S(1)}, f32[72,128]{1,0:T(8,128)S(1)}, u32[]{:S(2)}, u32[]{:S(2)}) collective-permute-start(f32[72,128]{1,0:T(8,128)S(1)} %get-tuple-element.24), channel_id=1, source_target_pairs={{0,1},{1,0},{2,3},{3,2},{4,5},{5,4},{6,7},{7,6},{8,9},{9,8},{10,11... | collective-permute-start | bytes 110600 | tf_op jit(solution)/shard_map/ppermute | solution.py:366
  4.3 4.7 %collective-permute-start.2 = (f32[72,128]{1,0:T(8,128)S(1)}, f32[72,128]{1,0:T(8,128)S(1)}, u32[]{:S(2)}, u32[]{:S(2)}) collective-permute-start(f32[72,128]{1,0:T(8,128)S(1)} %get-tuple-element.24), channel_id=1, source_target_pairs={{0,3},{1,2},{2,1},{3,0},{4,7},{5,6},{6,5},{7,4},{8,11},{9,10},{10,... | collective-permute-start | bytes 110600 | tf_op jit(solution)/shard_map/ppermute | solution.py:366
  6.9 2.8 %collective-permute-start.1 = (f32[72,128]{1,0:T(8,128)S(1)}, f32[72,128]{1,0:T(8,128)S(1)}, u32[]{:S(2)}, u32[]{:S(2)}) collective-permute-start(f32[72,128]{1,0:T(8,128)S(1)} %get-tuple-element.24), channel_id=1, source_target_pairs={{0,2},{1,3},{2,0},{3,1},{4,6},{5,7},{6,4},{7,5},{8,10},{9,11},{10,... | collective-permute-start | bytes 110600 | tf_op jit(solution)/shard_map/ppermute | solution.py:366
  7.0 13.3 %collective-permute-start.8 = (bf16[5,32,896]{2,1,0:T(8,128)(2,1)S(1)}, bf16[5,32,896]{2,1,0:T(8,128)(2,1)S(1)}, u32[]{:S(2)}, u32[]{:S(2)}) collective-permute-start(bf16[5,32,896]{2,1,0:T(8,128)(2,1)S(1)} %get-tuple-element.35), channel_id=1, source_target_pairs={{0,3},{1,2},{2,1},{3,0},{4,7},{5,6},{6,5},{7,4},{8,11},{9,10},{10,... | collective-permute-start | bytes 860168 | tf_op jit(solution)/shard_map/ppermute | solution.py:366
  9.0 12.8 %collective-permute-start.9 = (bf16[5,32,896]{2,1,0:T(8,128)(2,1)S(1)}, bf16[5,32,896]{2,1,0:T(8,128)(2,1)S(1)}, u32[]{:S(2)}, u32[]{:S(2)}) collective-permute-start(bf16[5,32,896]{2,1,0:T(8,128)(2,1)S(1)} %get-tuple-element.36), channel_id=1, source_target_pairs={{0,2},{1,3},{2,0},{3,1},{4,6},{5,7},{6,4},{7,5},{8,10},{9,11},{10,... | collective-permute-start | bytes 860168 | tf_op jit(solution)/shard_map/ppermute | solution.py:366
  9.8 3.2 %collective-permute-start.3 = (f32[72,128]{1,0:T(8,128)S(1)}, f32[72,128]{1,0:T(8,128)S(1)}, u32[]{:S(2)}, u32[]{:S(2)}) collective-permute-start(f32[72,128]{1,0:T(8,128)S(1)} %add_add_fusion.after_ref), channel_id=1, source_target_pairs={{0,4},{4,0},{8,12},{12,8},{1,5},{5,1},{9,13},{13,9},{2,6},{6,2},{1... | collective-permute-start | bytes 110600 | tf_op jit(solution)/shard_map/ppermute | solution.py:366
  12.9 4.5 %copy-start = (f32[128,16]{0,1:T(8,128)S(1)}, f32[128,16]{0,1:T(8,128)}, u32[]{:S(2)}) copy-start(f32[128,16]{0,1:T(8,128)} %param.6) | copy-start | bytes 24580
  13.0 4.5 %copy-start.1 = (s32[128]{0:T(128)S(1)}, s32[128]{0:T(128)}, u32[]{:S(2)}) copy-start(s32[128]{0:T(128)} %param.5) | copy-start | bytes 1540
  13.0 4.5 %collective-permute-start.4 = (f32[72,128]{1,0:T(8,128)S(1)}, f32[72,128]{1,0:T(8,128)S(1)}, u32[]{:S(2)}, u32[]{:S(2)}) collective-permute-start(f32[72,128]{1,0:T(8,128)S(1)} %add.15.first_ref), channel_id=1, source_target_pairs={{0,8},{4,12},{8,0},{12,4},{1,9},{5,13},{9,1},{13,5},{2,10},{6,14},... | collective-permute-start | bytes 110600 | tf_op jit(solution)/shard_map/ppermute | solution.py:366
  19.5 11.1 %collective-permute-start.10 = (bf16[5,16,2176]{2,1,0:T(8,128)(2,1)S(1)}, bf16[5,16,2176]{2,1,0:T(8,128)(2,1)S(1)}, u32[]{:S(2)}, u32[]{:S(2)}) collective-permute-start(bf16[5,16,2176]{2,1,0:T(8,128)(2,1)S(1)} %get-tuple-element.39), channel_id=1, source_target_pairs={{0,2},{1,3},{2,0},{3,1},{4,6},{5,7},{6,4},{7,5},{8,10},{9,11},{10,... | collective-permute-start | bytes 1044488 | tf_op jit(solution)/shard_map/ppermute | solution.py:366
  21.8 15.5 %collective-permute-start.11 = (bf16[5,16,2176]{2,1,0:T(8,128)(2,1)S(1)}, bf16[5,16,2176]{2,1,0:T(8,128)(2,1)S(1)}, u32[]{:S(2)}, u32[]{:S(2)}) collective-permute-start(bf16[5,16,2176]{2,1,0:T(8,128)(2,1)S(1)} %get-tuple-element.40), channel_id=1, source_target_pairs={{0,3},{1,2},{2,1},{3,0},{4,7},{5,6},{6,5},{7,4},{8,11},{9,10},{10,... | collective-permute-start | bytes 1044488 | tf_op jit(solution)/shard_map/ppermute | solution.py:366
  26.5 1.3 %copy-start.2 = (s32[4]{0:T(128)S(1)}, s32[4]{0:T(128)}, u32[]{:S(2)}) copy-start(s32[4]{0:T(128)} %successor_ref.1) | copy-start | bytes 52
  27.2 2.1 %collective-permute-start.5 = (bf16[2,16,3072]{2,1,0:T(8,128)(2,1)S(1)}, bf16[2,16,3072]{2,1,0:T(8,128)(2,1)S(1)}, u32[]{:S(2)}, u32[]{:S(2)}) collective-permute-start(bf16[2,16,3072]{2,1,0:T(8,128)(2,1)S(1)} %get-tuple-element.31), channel_id=1, source_target_pairs={{0,1},{1,0},{2,3},{3,2},{4,5},{5,4},{6,7},{7,6},{8,9},{9,8},{10,11... | collective-permute-start | bytes 589832 | tf_op jit(solution)/shard_map/ppermute | solution.py:366
  27.3 2.1 %collective-permute-start.6 = (bf16[2,16,3072]{2,1,0:T(8,128)(2,1)S(1)}, bf16[2,16,3072]{2,1,0:T(8,128)(2,1)S(1)}, u32[]{:S(2)}, u32[]{:S(2)}) collective-permute-start(bf16[2,16,3072]{2,1,0:T(8,128)(2,1)S(1)} %get-tuple-element.32), channel_id=1, source_target_pairs={{0,1},{1,0},{2,3},{3,2},{4,5},{5,4},{6,7},{7,6},{8,9},{9,8},{10,11... | collective-permute-start | bytes 589832 | tf_op jit(solution)/shard_map/ppermute | solution.py:366
  27.8 1.5 %collective-permute-start.7 = (bf16[1,16,3072]{2,1,0:T(8,128)(2,1)S(1)}, bf16[1,16,3072]{2,1,0:T(8,128)(2,1)S(1)}, u32[]{:S(2)}, u32[]{:S(2)}) collective-permute-start(bf16[1,16,3072]{2,1,0:T(8,128)(2,1)S(1)} %get-tuple-element.33), channel_id=1, source_target_pairs={{0,1},{1,0},{2,3},{3,2},{4,5},{5,4},{6,7},{7,6},{8,9},{9,8},{10,11... | collective-permute-start | bytes 294920 | tf_op jit(solution)/shard_map/ppermute | solution.py:366

commit v8 on v7

--- a/solution.py
+++ b/solution.py
@@ -385,10 +385,10 @@
         terms = [a + b for a, b in zip(terms[::2], terms[1::2])]
     gram = terms[0]
     x = load(gram, x_hbm)
-    for b in range(space.bit_length() - 1):
-        if b > 0:
-            gram = gram + other
-        other = swap(gram, "space", 1 << b)
+    terms = [gram] + [swap(gram, "space", k) for k in range(1, space)]
+    while len(terms) > 2:
+        terms = [a + b for a, b in zip(terms[::2], terms[1::2])]
+    gram, other = terms
     gram, basis, near, own, late = subspace(
         gram, other, labels, start.T, x, total_rows, far, slots, EARLY
     )

time: 38.3 us -> 38.3 us (level)
  waiting for transfers between devices: 10.1 us -> 9.49 us
  starting transfers between devices: 12.6 us -> 13.2 us
    ppermute x12 -> x13, waiting for transfers between devices: 10.1 us -> 9.49 us  [swap(): return lax.ppermute(x, axis, [(i, i ^ offset) for i in range(size)])]
    ppermute x12 -> x13, starting transfers between devices: 12.6 us -> 13.2 us  [swap(): return lax.ppermute(x, axis, [(i, i ^ offset) for i in range(size)])]
  transfers between devices with their start and end apart: 12 -> 13, of which waited for: 4 -> 5; matrix products, arithmetic and copies ran while one was open for 0% -> 0% of each run, Pallas kernels for 27% -> 27%
where the time goes in v8:
time: 38.3 us; the launch traced here: 38.1 us
  Pallas kernels  14.6 us (38%)
  starting transfers between devices  13.2 us (34%)
  waiting for transfers between devices  9.49 us (25%)
  between operations  0.77 us (2%)
    pallas_call x9, Pallas kernels, call(): pl.pallas_call(body, in_specs=in_specs, out_specs=out_specs or [IN_VMEM]...  14.6 us
    ppermute x13, starting transfers between devices, swap(): return lax.ppermute(x, axis, [(i, i ^ offset) for i in range(size)])  13.2 us
    ppermute x13, waiting for transfers between devices, swap(): return lax.ppermute(x, axis, [(i, i ^ offset) for i in range(size)])  9.49 us
  transfers between devices with their start and end apart: 13, of which 5 were waited for; matrix products, arithmetic and copies ran while one was open for 0% of the time, Pallas kernels for 27%

profile of v8, /device:TPU:1, one launch (start us, length us, event | category | flops | bytes accessed | tf_op | source)
XLA Modules:
  0.0 38.1 jit_solution(970656743869269182)
XLA Ops:
  0.6 3.6 %gram.1 = (f32[72,128]{1,0:T(8,128)S(1)}, bf16[5,32,896]{2,1,0:T(8,128)(2,1)S(1)}, bf16[5,32,896]{2,1,0:T(8,128)(2,1)S(1)}) custom-call(s32[1,128]{1,0:T(1,128)} %bitcast.8, bf16[5,128,3072]{2,1,0:T(8,128)(2,1)} %bitcast.11), custom_call_target="tpu_custom_call" | custom-call | tf_op jit(solution)/shard_map/gram/pallas_call | solution.py:22
  4.2 0.1 collective-permute-start
  4.3 2.6 %collective-permute-start.2 = (f32[72,128]{1,0:T(8,128)S(1)}, f32[72,128]{1,0:T(8,128)S(1)}, u32[]{:S(2)}, u32[]{:S(2)}) collective-permute-start(f32[72,128]{1,0:T(8,128)S(1)} %get-tuple-element.24), channel_id=1, source_target_pairs={{0,3},{1,2},{2,1},{3,0},{4,7},{5,6},{6,5},{7,4},{8,11},{9,10},{10,... | collective-permute-start | bytes 110600 | tf_op jit(solution)/shard_map/ppermute | solution.py:366
  6.9 0.1 collective-permute-start.1
  7.0 0.0 collective-permute-done
  7.0 2.0 %collective-permute-start.9 = (bf16[5,32,896]{2,1,0:T(8,128)(2,1)S(1)}, bf16[5,32,896]{2,1,0:T(8,128)(2,1)S(1)}, u32[]{:S(2)}, u32[]{:S(2)}) collective-permute-start(bf16[5,32,896]{2,1,0:T(8,128)(2,1)S(1)} %get-tuple-element.35), channel_id=1, source_target_pairs={{0,3},{1,2},{2,1},{3,0},{4,7},{5,6},{6,5},{7,4},{8,11},{9,10},{10,... | collective-permute-start | bytes 860168 | tf_op jit(solution)/shard_map/ppermute | solution.py:366
  9.0 0.0 collective-permute-start.10
  9.0 0.0 collective-permute-done.2
  9.0 0.7 %collective-permute-done.1 = f32[72,128]{1,0:T(8,128)S(1)} collective-permute-done((f32[72,128]{1,0:T(8,128)S(1)}, f32[72,128]{1,0:T(8,128)S(1)}, u32[]{:S(2)}, u32[]{:S(2)}) %collective-permute-start.1) | collective-permute-done | bytes 36896 | tf_op jit(solution)/shard_map/ppermute | solution.py:366
  9.8 0.0 copy-start
  9.8 0.0 copy-start.1
  9.8 1.4 %collective-permute-start.3 = (f32[72,128]{1,0:T(8,128)S(1)}, f32[72,128]{1,0:T(8,128)S(1)}, u32[]{:S(2)}, u32[]{:S(2)}) collective-permute-start(f32[72,128]{1,0:T(8,128)S(1)} %add_add_fusion.after_ref), channel_id=1, source_target_pairs={{0,4},{4,0},{8,12},{12,8},{1,5},{5,1},{9,13},{13,9},{2,6},{6,2},{1... | collective-permute-start | bytes 110600 | tf_op jit(solution)/shard_map/ppermute | solution.py:366
  11.2 2.2 %collective-permute-start.5 = (f32[72,128]{1,0:T(8,128)S(1)}, f32[72,128]{1,0:T(8,128)S(1)}, u32[]{:S(2)}, u32[]{:S(2)}) collective-permute-start(f32[72,128]{1,0:T(8,128)S(1)} %add_add_fusion.after_ref), channel_id=1, source_target_pairs={{0,12},{4,8},{8,4},{12,0},{1,13},{5,9},{9,5},{13,1},{2,14},{6,10},... | collective-permute-start | bytes 110600 | tf_op jit(solution)/shard_map/ppermute | solution.py:366
  13.4 0.1 collective-permute-start.4
  13.5 2.1 %load.2.x_ref = bf16[5,128,3072]{2,1,0:T(8,128)(2,1)S(1)} custom-call(f32[72,128]{1,0:T(8,128)S(1)} %add_add_fusion.after_ref, bf16[5,128,3072]{2,1,0:T(8,128)(2,1)} %bitcast.12), custom_call_target="tpu_custom_call" | custom-call | tf_op jit(solution)/shard_map/load/pallas_call | solution.py:22
  15.6 0.0 collective-permute-done.3
  15.6 0.1 collective-permute-done.5
  15.8 1.9 %collective-permute-done.4 = f32[72,128]{1,0:T(8,128)S(1)} collective-permute-done((f32[72,128]{1,0:T(8,128)S(1)}, f32[72,128]{1,0:T(8,128)S(1)}, u32[]{:S(2)}, u32[]{:S(2)}) %collective-permute-start.4) | collective-permute-done | bytes 36896 | tf_op jit(solution)/shard_map/ppermute | solution.py:366
  17.7 0.0 copy-done
  17.7 0.0 copy-done.1
  17.7 2.0 %subspace.1 = (f32[128,128]{1,0:T(8,128)S(1)}, f32[16,128]{1,0:T(8,128)S(1)}, bf16[2,16,128]{2,1,0:T(8,128)(2,1)S(1)}, bf16[16,32]{1,0:T(8,128)(2,1)S(1)}, bf16[...) custom-call(f32[72,128]{1,0:T(8,128)S(1)} %add.18.first_ref, f32[72,128]{1,0:T(8,128)S(1)} %add.19.second_ref, ...), custom_call_target="tpu_custom_call" | custom-call | tf_op jit(solution)/shard_map/subspace/pallas_call | solution.py:22
  19.7 1.0 %collective-permute-start.11 = (bf16[5,16,2176]{2,1,0:T(8,128)(2,1)S(1)}, bf16[5,16,2176]{2,1,0:T(8,128)(2,1)S(1)}, u32[]{:S(2)}, u32[]{:S(2)}) collective-permute-start(bf16[5,16,2176]{2,1,0:T(8,128)(2,1)S(1)} %get-tuple-element.39), channel_id=1, source_target_pairs={{0,2},{1,3},{2,0},{3,1},{4,6},{5,7},{6,4},{7,5},{8,10},{9,11},{10,... | collective-permute-start | bytes 1044488 | tf_op jit(solution)/shard_map/ppermute | solution.py:366
  20.8 0.0 collective-permute-done.9.refs_4_
  20.8 1.1 %collective-permute-done.10.refs_3_ = bf16[5,32,896]{2,1,0:T(8,128)(2,1)S(1)} collective-permute-done((bf16[5,32,896]{2,1,0:T(8,128)(2,1)S(1)}, bf16[5,32,896]{2,1,0:T(8,128)(2,1)S(1)}, u32[]{:S(2)}, u32[]{:S(2)}) %collective-permute-start.10) | collective-permute-done | bytes 286752 | tf_op jit(solution)/shard_map/ppermute | solution.py:366
  21.8 3.0 %collective-permute-start.12 = (bf16[5,16,2176]{2,1,0:T(8,128)(2,1)S(1)}, bf16[5,16,2176]{2,1,0:T(8,128)(2,1)S(1)}, u32[]{:S(2)}, u32[]{:S(2)}) collective-permute-start(bf16[5,16,2176]{2,1,0:T(8,128)(2,1)S(1)} %get-tuple-element.40), channel_id=1, source_target_pairs={{0,3},{1,2},{2,1},{3,0},{4,7},{5,6},{6,5},{7,4},{8,11},{9,10},{10,... | collective-permute-start | bytes 1044488 | tf_op jit(solution)/shard_map/ppermute | solution.py:366
  24.9 2.1 %load.3.x_ref = bf16[5,128,3072]{2,1,0:T(8,128)(2,1)S(1)} custom-call(bf16[2,16,128]{2,1,0:T(8,128)(2,1)S(1)} %get-tuple-element.29.after_ref.near_ref, bf16[5,128,3072]{2,1,0:T(8,128)(2,1)} %bitcast.13), custom_call_target="tpu_custom_call" | custom-call | tf_op jit(solution)/shard_map/load/pallas_call | solution.py:22
  27.0 0.0 copy-start.2
  27.0 0.6 %near.1 = (bf16[5,16,3072]{2,1,0:T(8,128)(2,1)S(1)}, bf16[2,16,3072]{2,1,0:T(8,128)(2,1)S(1)}, bf16[2,16,3072]{2,1,0:T(8,128)(2,1)S(1)}, bf16[1,16,3072]{2,1,0:T(8,128)(2,1)S(1)}) custom-call(bf16[2,16,128]{2,1,0:T(8,128)(2,1)S(1)} %get-tuple-element.29.after_ref.near_ref, bf16[5,128,3072]{2,1,0:T(8,128)(2,1)S(1)} %load.3.x_ref), custom_call_target="tpu_custom_call" | custom-call | tf_op jit(solution)/shard_map/near/pallas_call | solution.py:22
  27.7 0.1 collective-permute-start.6
  27.7 0.5 %collective-permute-start.7 = (bf16[2,16,3072]{2,1,0:T(8,128)(2,1)S(1)}, bf16[2,16,3072]{2,1,0:T(8,128)(2,1)S(1)}, u32[]{:S(2)}, u32[]{:S(2)}) collective-permute-start(bf16[2,16,3072]{2,1,0:T(8,128)(2,1)S(1)} %get-tuple-element.32), channel_id=1, source_target_pairs={{0,1},{1,0},{2,3},{3,2},{4,5},{5,4},{6,7},{7,6},{8,9},{9,8},{10,11... | collective-permute-start | bytes 589832 | tf_op jit(solution)/shard_map/ppermute | solution.py:366
  28.2 0.1 collective-permute-start.8
  28.3 0.0 copy-done.2
  28.3 1.5 %small.1 = (f32[16,32]{1,0:T(8,128)}, f32[1,16,16]{2,1,0:T(8,128)}) custom-call(s32[4]{0:T(128)S(1)} %copy-done.2, f32[128,128]{1,0:T(8,128)S(1)} %get-tuple-element.41.gram_ref, s32[1,128]{1,0:T(1,128)S(1)} %bitcast.10, f32[16,128]{1,0:T(8,128)S(1)} %get-tuple-element.42.basis_ref), custom_call_target="tpu_custom_call" | custom-call | tf_op jit(solution)/shard_map/small/pallas_call | solution.py:22
  29.8 0.0 collective-permute-done.8.refs_2_
  29.8 0.0 collective-permute-done.6.refs_0_
  29.8 0.0 collective-permute-done.7.refs_1_
  29.8 1.2 %owner.1.out_in_ref = bf16[5,16,12288]{2,1,0:T(8,128)(2,1)} custom-call(bf16[16,32]{1,0:T(8,128)(2,1)S(1)} %get-tuple-element.28.own_ref, bf16[5,16,3072]{2,1,0:T(8,128)(2,1)S(1)} %get-tuple-element.30.near_ref, bf16[2,16,3072]{2,1,0:T(8,128)(2,1)S(1)} %collective-permute-done.6.refs_0_, bf16[2,16,3072]{2,1,0:T(8,128)(2,1)S(1)} %collective-permute-done.7.refs_1_, ...), custom_call_target="tpu_custom_call" | custom-call | tf_op jit(solution)/shard_map/owner/pallas_call | solution.py:22
  31.0 0.0 collective-permute-done.11.refs_0_
  31.0 0.8 %place.2.out_in_ref = bf16[5,16,12288]{2,1,0:T(8,128)(2,1)} custom-call(bf16[5,16,12288]{2,1,0:T(8,128)(2,1)} %owner.1.out_in_ref, bf16[5,16,2176]{2,1,0:T(8,128)(2,1)S(1)} %collective-permute-done.11.refs_0_), custom_call_target="tpu_custom_call", output_to_operand_aliasing={{}: (0, {})} | custom-call | tf_op jit(solution)/shard_map/place/pallas_call | solution.py:22
  31.8 5.6 %collective-permute-done.12.refs_0_ = bf16[5,16,2176]{2,1,0:T(8,128)(2,1)S(1)} collective-permute-done((bf16[5,16,2176]{2,1,0:T(8,128)(2,1)S(1)}, bf16[5,16,2176]{2,1,0:T(8,128)(2,1)S(1)}, u32[]{:S(2)}, u32[]{:S(2)}) %collective-permute-start.12) | collective-permute-done | bytes 348192 | tf_op jit(solution)/shard_map/ppermute | solution.py:366
  37.4 0.7 %place.3 = bf16[5,16,12288]{2,1,0:T(8,128)(2,1)} custom-call(bf16[5,16,12288]{2,1,0:T(8,128)(2,1)} %place.2.out_in_ref, bf16[5,16,2176]{2,1,0:T(8,128)(2,1)S(1)} %collective-permute-done.12.refs_0_), custom_call_target="tpu_custom_call", output_to_operand_aliasing={{}: (0, {})} | custom-call | tf_op jit(solution)/shard_map/place/pallas_call | solution.py:22
  (3 shorter events, 0.0 us)
Async XLA Ops:
  4.2 2.8 %collective-permute-start = (f32[72,128]{1,0:T(8,128)S(1)}, f32[72,128]{1,0:T(8,128)S(1)}, u32[]{:S(2)}, u32[]{:S(2)}) collective-permute-start(f32[72,128]{1,0:T(8,128)S(1)} %get-tuple-element.24), channel_id=1, source_target_pairs={{0,1},{1,0},{2,3},{3,2},{4,5},{5,4},{6,7},{7,6},{8,9},{9,8},{10,11... | collective-permute-start | bytes 110600 | tf_op jit(solution)/shard_map/ppermute | solution.py:366
  4.3 4.7 %collective-permute-start.2 = (f32[72,128]{1,0:T(8,128)S(1)}, f32[72,128]{1,0:T(8,128)S(1)}, u32[]{:S(2)}, u32[]{:S(2)}) collective-permute-start(f32[72,128]{1,0:T(8,128)S(1)} %get-tuple-element.24), channel_id=1, source_target_pairs={{0,3},{1,2},{2,1},{3,0},{4,7},{5,6},{6,5},{7,4},{8,11},{9,10},{10,... | collective-permute-start | bytes 110600 | tf_op jit(solution)/shard_map/ppermute | solution.py:366
  6.9 2.8 %collective-permute-start.1 = (f32[72,128]{1,0:T(8,128)S(1)}, f32[72,128]{1,0:T(8,128)S(1)}, u32[]{:S(2)}, u32[]{:S(2)}) collective-permute-start(f32[72,128]{1,0:T(8,128)S(1)} %get-tuple-element.24), channel_id=1, source_target_pairs={{0,2},{1,3},{2,0},{3,1},{4,6},{5,7},{6,4},{7,5},{8,10},{9,11},{10,... | collective-permute-start | bytes 110600 | tf_op jit(solution)/shard_map/ppermute | solution.py:366
  7.0 13.7 %collective-permute-start.9 = (bf16[5,32,896]{2,1,0:T(8,128)(2,1)S(1)}, bf16[5,32,896]{2,1,0:T(8,128)(2,1)S(1)}, u32[]{:S(2)}, u32[]{:S(2)}) collective-permute-start(bf16[5,32,896]{2,1,0:T(8,128)(2,1)S(1)} %get-tuple-element.35), channel_id=1, source_target_pairs={{0,3},{1,2},{2,1},{3,0},{4,7},{5,6},{6,5},{7,4},{8,11},{9,10},{10,... | collective-permute-start | bytes 860168 | tf_op jit(solution)/shard_map/ppermute | solution.py:366
  9.0 12.8 %collective-permute-start.10 = (bf16[5,32,896]{2,1,0:T(8,128)(2,1)S(1)}, bf16[5,32,896]{2,1,0:T(8,128)(2,1)S(1)}, u32[]{:S(2)}, u32[]{:S(2)}) collective-permute-start(bf16[5,32,896]{2,1,0:T(8,128)(2,1)S(1)} %get-tuple-element.36), channel_id=1, source_target_pairs={{0,2},{1,3},{2,0},{3,1},{4,6},{5,7},{6,4},{7,5},{8,10},{9,11},{10,... | collective-permute-start | bytes 860168 | tf_op jit(solution)/shard_map/ppermute | solution.py:366
  9.8 7.9 %copy-start = (f32[128,16]{0,1:T(8,128)S(1)}, f32[128,16]{0,1:T(8,128)}, u32[]{:S(2)}) copy-start(f32[128,16]{0,1:T(8,128)} %param.6) | copy-start | bytes 24580
  9.8 7.9 %copy-start.1 = (s32[128]{0:T(128)S(1)}, s32[128]{0:T(128)}, u32[]{:S(2)}) copy-start(s32[128]{0:T(128)} %param.5) | copy-start | bytes 1540
  9.8 5.8 %collective-permute-start.3 = (f32[72,128]{1,0:T(8,128)S(1)}, f32[72,128]{1,0:T(8,128)S(1)}, u32[]{:S(2)}, u32[]{:S(2)}) collective-permute-start(f32[72,128]{1,0:T(8,128)S(1)} %add_add_fusion.after_ref), channel_id=1, source_target_pairs={{0,4},{4,0},{8,12},{12,8},{1,5},{5,1},{9,13},{13,9},{2,6},{6,2},{1... | collective-permute-start | bytes 110600 | tf_op jit(solution)/shard_map/ppermute | solution.py:366
  11.2 4.6 %collective-permute-start.5 = (f32[72,128]{1,0:T(8,128)S(1)}, f32[72,128]{1,0:T(8,128)S(1)}, u32[]{:S(2)}, u32[]{:S(2)}) collective-permute-start(f32[72,128]{1,0:T(8,128)S(1)} %add_add_fusion.after_ref), channel_id=1, source_target_pairs={{0,12},{4,8},{8,4},{12,0},{1,13},{5,9},{9,5},{13,1},{2,14},{6,10},... | collective-permute-start | bytes 110600 | tf_op jit(solution)/shard_map/ppermute | solution.py:366
  13.4 4.3 %collective-permute-start.4 = (f32[72,128]{1,0:T(8,128)S(1)}, f32[72,128]{1,0:T(8,128)S(1)}, u32[]{:S(2)}, u32[]{:S(2)}) collective-permute-start(f32[72,128]{1,0:T(8,128)S(1)} %add_add_fusion.after_ref), channel_id=1, source_target_pairs={{0,8},{4,12},{8,0},{12,4},{1,9},{5,13},{9,1},{13,5},{2,10},{6,14},... | collective-permute-start | bytes 110600 | tf_op jit(solution)/shard_map/ppermute | solution.py:366
  19.7 11.3 %collective-permute-start.11 = (bf16[5,16,2176]{2,1,0:T(8,128)(2,1)S(1)}, bf16[5,16,2176]{2,1,0:T(8,128)(2,1)S(1)}, u32[]{:S(2)}, u32[]{:S(2)}) collective-permute-start(bf16[5,16,2176]{2,1,0:T(8,128)(2,1)S(1)} %get-tuple-element.39), channel_id=1, source_target_pairs={{0,2},{1,3},{2,0},{3,1},{4,6},{5,7},{6,4},{7,5},{8,10},{9,11},{10,... | collective-permute-start | bytes 1044488 | tf_op jit(solution)/shard_map/ppermute | solution.py:366
  21.8 15.5 %collective-permute-start.12 = (bf16[5,16,2176]{2,1,0:T(8,128)(2,1)S(1)}, bf16[5,16,2176]{2,1,0:T(8,128)(2,1)S(1)}, u32[]{:S(2)}, u32[]{:S(2)}) collective-permute-start(bf16[5,16,2176]{2,1,0:T(8,128)(2,1)S(1)} %get-tuple-element.40), channel_id=1, source_target_pairs={{0,3},{1,2},{2,1},{3,0},{4,7},{5,6},{6,5},{7,4},{8,11},{9,10},{10,... | collective-permute-start | bytes 1044488 | tf_op jit(solution)/shard_map/ppermute | solution.py:366
  27.0 1.3 %copy-start.2 = (s32[4]{0:T(128)S(1)}, s32[4]{0:T(128)}, u32[]{:S(2)}) copy-start(s32[4]{0:T(128)} %successor_ref.1) | copy-start | bytes 52
  27.7 2.1 %collective-permute-start.6 = (bf16[2,16,3072]{2,1,0:T(8,128)(2,1)S(1)}, bf16[2,16,3072]{2,1,0:T(8,128)(2,1)S(1)}, u32[]{:S(2)}, u32[]{:S(2)}) collective-permute-start(bf16[2,16,3072]{2,1,0:T(8,128)(2,1)S(1)} %get-tuple-element.31), channel_id=1, source_target_pairs={{0,1},{1,0},{2,3},{3,2},{4,5},{5,4},{6,7},{7,6},{8,9},{9,8},{10,11... | collective-permute-start | bytes 589832 | tf_op jit(solution)/shard_map/ppermute | solution.py:366
  27.7 2.1 %collective-permute-start.7 = (bf16[2,16,3072]{2,1,0:T(8,128)(2,1)S(1)}, bf16[2,16,3072]{2,1,0:T(8,128)(2,1)S(1)}, u32[]{:S(2)}, u32[]{:S(2)}) collective-permute-start(bf16[2,16,3072]{2,1,0:T(8,128)(2,1)S(1)} %get-tuple-element.32), channel_id=1, source_target_pairs={{0,1},{1,0},{2,3},{3,2},{4,5},{5,4},{6,7},{7,6},{8,9},{9,8},{10,11... | collective-permute-start | bytes 589832 | tf_op jit(solution)/shard_map/ppermute | solution.py:366
  28.2 1.5 %collective-permute-start.8 = (bf16[1,16,3072]{2,1,0:T(8,128)(2,1)S(1)}, bf16[1,16,3072]{2,1,0:T(8,128)(2,1)S(1)}, u32[]{:S(2)}, u32[]{:S(2)}) collective-permute-start(bf16[1,16,3072]{2,1,0:T(8,128)(2,1)S(1)} %get-tuple-element.33), channel_id=1, source_target_pairs={{0,1},{1,0},{2,3},{3,2},{4,5},{5,4},{6,7},{7,6},{8,9},{9,8},{10,11... | collective-permute-start | bytes 294920 | tf_op jit(solution)/shard_map/ppermute | solution.py:366
